TPU v7x, 32 devices: a whole 2x2x4 slice. The times are simulated.
32 devices in a mesh: win: 2 (over x), sta: 16 (over z, y, core).
Axes of the slice: x: 2, y: 2, z: 4, core: 2. Of those that a mesh axis runs over, the one named last changes fastest.
Arguments:
- samples: bfloat16 [256, 1048576], P('sta', 'win'), may hold values from -6 to 6
- coarse_taps: bfloat16 [16, 512], replicated, may hold values from -0.0625 to 0.0625
- fine_taps: bfloat16 [8, 64], replicated, may hold values from -0.25 to 0.25
Outputs:
- visibilities: bfloat16 [128, 64, 2, 256, 256], P('win', 'sta')
All inputs are finite; a program needn't handle non-finite values.
Results may differ from a plain program's by a relative error of at most 0.008.
Values may be sent and summed in bfloat16 or wider, within the bound.
No kernel may reach another device: no remote copies, remote signals or barrier semaphores. Data moves between devices by JAX's collectives and lax.ppermute only.
A program may use at most 320 MiB of HBM per device.

v0:
```python
import functools
import math

import jax
import jax.numpy as jnp
from jax import lax
from jax.experimental import pallas as pl
from jax.experimental.pallas import tpu as pltpu
from jax.sharding import PartitionSpec as P

KEEP = 128
LANES = 128
WIDE = 256
PITCH = 17
ROWS = 16
BLOCK = 128


def from_behind(x, axis, by):
    size = lax.axis_size(axis)
    pairs = [(i, i + by) for i in range(size) if 0 <= i + by < size]
    return lax.ppermute(x, axis, pairs)


def coarse_matrix(frame_len, band_count):
    channels = frame_len // 8 + jnp.arange(band_count, dtype=jnp.int32)
    products = jnp.arange(frame_len, dtype=jnp.int32)[:, None] * channels[None, :]
    angles = (products % frame_len).astype(jnp.float32) * (2.0 * math.pi / frame_len)
    return jnp.concatenate([jnp.cos(angles), -jnp.sin(angles)], axis=1).astype(jnp.bfloat16)


def fine_tables(fine_len):
    products = (
        jnp.arange(fine_len, dtype=jnp.int32)[:, None]
        * jnp.arange(fine_len, dtype=jnp.int32)[None, :]
    )
    angles = (products % fine_len).astype(jnp.float32) * (2.0 * math.pi / fine_len)
    return (jnp.cos(angles), jnp.sin(angles))


def correlate(spectra_in, pieces):
    band_local, fine_local, sig_count, columns = spectra_in.shape
    split_view = spectra_in.reshape(
        band_local, fine_local, sig_count, pieces, 2, columns // (2 * pieces)
    )
    turned = jnp.stack([split_view[:, :, :, :, 1], -split_view[:, :, :, :, 0]], axis=4).reshape(
        band_local, fine_local, sig_count, columns
    )
    real_vis = jnp.einsum(
        "kqsc,kqtc->kqst", spectra_in, spectra_in, preferred_element_type=jnp.float32
    )
    imag_vis = jnp.einsum("kqsc,kqtc->kqst", turned, spectra_in, preferred_element_type=jnp.float32)
    return jnp.stack([real_vis, imag_vis], axis=2)


def per_device_general(samples, coarse_taps, fine_taps):
    sig_local, samp_local = samples.shape
    tap_count, frame_len = coarse_taps.shape
    fine_tap_count, fine_len = fine_taps.shape
    band_count = KEEP
    frame_count = samp_local // frame_len
    frames_local = samples.reshape(sig_local, frame_count, frame_len)
    earlier = from_behind(frames_local[:, frame_count - (tap_count - 1) :], "win", 1)
    padded = jnp.concatenate([earlier, frames_local], axis=1)
    windowed = jnp.zeros((sig_local, frame_count, frame_len), jnp.float32)
    for tap_index in range(tap_count):
        start = tap_count - 1 - tap_index
        windowed = windowed + coarse_taps[tap_index].astype(jnp.float32)[None, None, :] * padded[
            :, start : start + frame_count
        ].astype(jnp.float32)
    spectra = jnp.dot(
        windowed.astype(jnp.bfloat16).reshape(sig_local * frame_count, frame_len),
        coarse_matrix(frame_len, band_count),
        preferred_element_type=jnp.float32,
    )
    spectra = spectra.astype(jnp.bfloat16).reshape(sig_local, frame_count, 2 * band_count)
    history = (fine_tap_count - 1) * fine_len
    carried = from_behind(spectra[:, frame_count - history :], "win", 1)
    extended = jnp.concatenate([carried, spectra], axis=1)
    fine_count = frame_count // fine_len
    groups = extended.reshape(sig_local, fine_count + fine_tap_count - 1, fine_len, 2, band_count)
    filtered = jnp.zeros((sig_local, fine_count, fine_len, 2, band_count), jnp.float32)
    for tap_index in range(fine_tap_count):
        start = fine_tap_count - 1 - tap_index
        filtered = filtered + fine_taps[tap_index].astype(jnp.float32)[
            None, None, :, None, None
        ] * groups[:, start : start + fine_count].astype(jnp.float32)
    cosines, sines = fine_tables(fine_len)
    real_part = filtered[:, :, :, 0]
    imag_part = filtered[:, :, :, 1]
    highest = lax.Precision.HIGHEST
    out_real = jnp.einsum("qj,sgjk->kqsg", cosines, real_part, precision=highest) + jnp.einsum(
        "qj,sgjk->kqsg", sines, imag_part, precision=highest
    )
    out_imag = jnp.einsum("qj,sgjk->kqsg", cosines, imag_part, precision=highest) - jnp.einsum(
        "qj,sgjk->kqsg", sines, real_part, precision=highest
    )
    local_spectra = (
        jnp.stack([out_real, out_imag], axis=3)
        .astype(jnp.bfloat16)
        .reshape(band_count, fine_len, sig_local, 2 * fine_count)
    )
    frame_total = fine_count * lax.axis_size("win")
    moved = lax.all_to_all(local_spectra, "sta", split_axis=1, concat_axis=2, tiled=True)
    moved = lax.all_to_all(moved, "win", split_axis=0, concat_axis=3, tiled=True)
    vis_local = correlate(moved, lax.axis_size("win"))
    return (vis_local / frame_total).astype(jnp.bfloat16)


def swap(x, axis, by):
    return lax.ppermute(x, axis, [(i, i ^ by) for i in range(lax.axis_size(axis))])


def coarse_rows(frame_len, band_half, chunks):
    half = lax.axis_index("win")
    rows = []
    for h in range(2):
        base = 0
        for size in chunks:
            for part in range(2):
                channel = (half ^ h) * band_half + base + jnp.arange(size, dtype=jnp.int32)
                rows.append(channel * 2 + part)
            base += size
    code = jnp.concatenate(rows)
    channel = frame_len // 8 + code // 2
    products = channel[:, None] * jnp.arange(frame_len, dtype=jnp.int32)[None, :]
    angles = (products % frame_len).astype(jnp.float32) * (2.0 * math.pi / frame_len)
    return jnp.where((code % 2 == 0)[:, None], jnp.cos(angles), -jnp.sin(angles)).astype(jnp.bfloat16)


def coarse_kernel(chunks, taps_n, x_ref, before_ref, hist_ref, taps_ref, dft_ref, *refs):
    outs, (xs, even, odd) = refs[:-3], refs[-3:]
    step, last = pl.program_id(0), pl.num_programs(0) - 1
    keep = taps_n - 1
    pieces = xs.shape[1]
    skip = before_ref.shape[1] // (pieces * WIDE) - keep
    group = 8

    def load():
        @pl.when(step == 0)
        def _():
            for f in range(keep):
                for j in range(pieces):
                    at = (f * pieces + j) * WIDE
                    xs[f, j] = hist_ref[:, at : at + WIDE]

        @pl.when(step > 0)
        def _():
            for f in range(keep):
                for j in range(pieces):
                    at = ((f + skip) * pieces + j) * WIDE
                    xs[f, j] = before_ref[:, at : at + WIDE]

        def move(f, _):
            for j in range(pieces):
                at = pl.multiple_of((f * pieces + j) * WIDE, WIDE)
                xs[keep + f, j] = x_ref[:, pl.ds(at, WIDE)]
            return 0

        lax.fori_loop(0, BLOCK, move, 0, unroll=8)

    def fir(wd, first, j):
        taps = [taps_ref[j, m] for m in range(taps_n)]
        xv = [xs[first + t, j] for t in range(group + keep)]
        for g in range(group):
            terms = [taps[m] * xv[g + keep - m] for m in range(taps_n)]
            for _ in range(2):
                terms = [a + b for a, b in zip(terms[::2], terms[1::2])]
            wide = [t.astype(jnp.float32) for t in terms]
            while len(wide) > 1:
                wide = [a + b for a, b in zip(wide[::2], wide[1::2])]
            rows = pl.ds((first + g) * PITCH, ROWS)
            for n in range(WIDE // LANES):
                wd[j * (WIDE // LANES) + n, rows, :] = wide[0][:, n * LANES : (n + 1) * LANES]

    def project(wd, p):
        rows = []
        for t in range(2):
            parts = [wd[j, pl.ds(2 * p + t, BLOCK, stride=PITCH), :] for j in range(wd.shape[0])]
            rows.append(jnp.concatenate(parts, axis=1).astype(jnp.bfloat16))
        both = jnp.concatenate(rows, axis=0)
        res = lax.dot_general(
            dft_ref[...], both, (((1,), (1,)), ((), ())), preferred_element_type=jnp.float32
        ).astype(jnp.bfloat16)
        for t in range(2):
            base = 0
            for n, out in enumerate(outs):
                size = 2 * chunks[n % len(chunks)]
                out[2 * p + t] = res[base : base + size, t * BLOCK : (t + 1) * BLOCK]
                base += size

    pairs = ROWS // 2
    share = BLOCK // pairs // group

    def run(fill, drain):
        def body(p, _):
            if drain is not None:
                project(drain, p)
            if fill is not None:
                for n in range(share):
                    for j in range(pieces):
                        fir(fill, (p * share + n) * group, j)
            return 0

        if fill is not None:
            load()
        lax.fori_loop(0, pairs, body, 0)

    @pl.when(step == 0)
    def _():
        run(even, None)

    @pl.when((step > 0) & (step < last) & (step % 2 == 1))
    def _():
        run(odd, even)

    @pl.when((step > 0) & (step < last) & (step % 2 == 0))
    def _():
        run(even, odd)

    @pl.when((step == last) & (step % 2 == 1))
    def _():
        run(None, even)

    @pl.when((step == last) & (step % 2 == 0))
    def _():
        run(None, odd)


def coarse(samples, hist, coarse_taps, dft, chunks):
    sig, samp = samples.shape
    taps_n, frame_len = coarse_taps.shape
    pieces = frame_len // WIDE
    frames = samp // frame_len
    before = taps_n
    taps = jnp.broadcast_to(
        coarse_taps.reshape(taps_n, pieces, WIDE).transpose(1, 0, 2)[:, :, None],
        (pieces, taps_n, ROWS, WIDE),
    )
    ratio = BLOCK // before
    blocks = frames // BLOCK
    shapes = [jax.ShapeDtypeStruct((sig, 2 * c, frames), jnp.bfloat16) for c in chunks * 2]

    def at(i):
        return jnp.minimum(i, blocks - 1)

    return pl.pallas_call(
        functools.partial(coarse_kernel, chunks, taps_n),
        grid=(blocks + 1,),
        in_specs=[
            pl.BlockSpec((sig, BLOCK * frame_len), lambda i: (0, at(i))),
            pl.BlockSpec((sig, before * frame_len), lambda i: (0, jnp.maximum(at(i) * ratio - 1, 0))),
            pl.BlockSpec(hist.shape, lambda i: (0, 0)),
            pl.BlockSpec(taps.shape, lambda i: (0, 0, 0, 0)),
            pl.BlockSpec(dft.shape, lambda i: (0, 0)),
        ],
        out_specs=[
            pl.BlockSpec((sig, 2 * c, BLOCK), lambda i: (0, 0, jnp.maximum(i - 1, 0)))
            for c in chunks * 2
        ],
        out_shape=shapes,
        scratch_shapes=[pltpu.VMEM((BLOCK + taps_n - 1, pieces, sig, WIDE), jnp.bfloat16)]
        + [pltpu.VMEM((frame_len // LANES, BLOCK * PITCH, LANES), jnp.float32)] * 2,
        compiler_params=pltpu.CompilerParams(vmem_limit_bytes=50 << 20),
        cost_estimate=pl.CostEstimate(
            flops=2 * sig * frames * frame_len * (dft.shape[0] + 128 * taps_n),
            bytes_accessed=2 * sig * samp * 2,
            transcendentals=0,
        ),
    )(samples, samples, hist, taps, dft)


def fine_kernel(low, own_ref, oth_ref, town_ref, toth_ref, cos_ref, sin_ref, *refs):
    outs, zs = refs[:-1], refs[-1]
    sig, two_c, frames = own_ref.shape
    size = two_c // 2
    r = pl.program_id(0)
    cos, sin = cos_ref[...], sin_ref[...]

    def table(t_ref):
        t = t_ref[...]
        return jnp.concatenate(
            [(t * w).astype(jnp.bfloat16).reshape(frames, LANES) for w in (cos, sin)], axis=1
        )

    acc = jnp.dot(
        own_ref[...].reshape(sig * two_c, frames), table(town_ref), preferred_element_type=jnp.float32
    ) + jnp.dot(
        oth_ref[...].reshape(sig * two_c, frames), table(toth_ref), preferred_element_type=jnp.float32
    )
    acc = acc.reshape(sig, 2, size, 2 * LANES)
    p, q = acc[..., :LANES], acc[..., LANES:]
    pitch = two_c + 1
    real, imag = p[:, 0] + q[:, 1], p[:, 1] - q[:, 0]
    for s in range(sig):
        zs[pl.ds(s * pitch, size), :] = real[s]
        zs[pl.ds(s * pitch + size, size), :] = imag[s]
    for n, out in enumerate(outs):

        @pl.when(r // low == n)
        def _(out=out):
            for c in range(size):
                for part in range(2):
                    out[0, c, part] = zs[pl.ds(part * size + c, sig, stride=pitch), :].astype(
                        jnp.bfloat16
                    )


def fine(own, oth, town, toth, cos, sin, low):
    sig, two_c, frames = own.shape
    dests = cos.shape[0]
    unit = (two_c // 2, 2, sig, LANES)
    highs = dests // low

    def place(n):
        return lambda r: (jnp.clip(r - n * low, 0, low - 1), 0, 0, 0, 0)

    return pl.pallas_call(
        functools.partial(fine_kernel, low),
        grid=(dests,),
        in_specs=[
            pl.BlockSpec(own.shape, lambda r: (0, 0, 0)),
            pl.BlockSpec(oth.shape, lambda r: (0, 0, 0)),
            pl.BlockSpec(town.shape, lambda r: (0, 0, 0)),
            pl.BlockSpec(toth.shape, lambda r: (0, 0, 0)),
            pl.BlockSpec((1,) + cos.shape[1:], lambda r: (r, 0, 0)),
            pl.BlockSpec((1,) + sin.shape[1:], lambda r: (r, 0, 0)),
        ],
        out_specs=[pl.BlockSpec((1,) + unit, place(n)) for n in range(highs)],
        out_shape=[jax.ShapeDtypeStruct((low,) + unit, jnp.bfloat16) for _ in range(highs)],
        scratch_shapes=[pltpu.VMEM((sig * (two_c + 8), LANES), jnp.float32)],
        compiler_params=pltpu.CompilerParams(vmem_limit_bytes=50 << 20),
        cost_estimate=pl.CostEstimate(
            flops=2 * sig * two_c * 2 * frames * dests * 2 * LANES,
            bytes_accessed=6 * sig * two_c * frames,
            transcendentals=0,
        ),
    )(own, oth, town, toth, cos, sin)


def correlate_kernel(sources, scale, per_q, me_ref, *refs):
    ins, out, xr, xi = refs[: len(sources)], refs[-3], refs[-2], refs[-1]
    me = me_ref[0]
    for ref, units in zip(ins, sources):
        for at, rel in units:
            row = pl.multiple_of((me ^ rel) * ROWS, ROWS)
            xr[pl.ds(row, ROWS), :] = ref[at + (0, 0)]
            xi[pl.ds(row, ROWS), :] = ref[at + (0, 1)]
    re, im = xr[...], xi[...]
    lane = lax.broadcasted_iota(jnp.int32, (1, LANES), 1)
    zero = jnp.zeros((), jnp.bfloat16)
    picks = [lane // per_q == q for q in range(LANES // per_q)]
    left = jnp.concatenate(
        [jnp.concatenate([jnp.where(p, re, zero), jnp.where(p, im, zero)], axis=1) for p in picks],
        axis=0,
    )
    dims = (((1,), (1,)), ((), ()))
    for part, right in enumerate((jnp.concatenate([re, im], axis=1), jnp.concatenate([-im, re], axis=1))):
        vis = lax.dot_general(left, right, dims, preferred_element_type=jnp.float32)
        vis = (vis * scale).astype(jnp.bfloat16)
        for q in range(len(picks)):
            out[0, q, part] = vis[q * re.shape[0] : (q + 1) * re.shape[0]]


def correlate_chunk(me, arrays, leads, sources, whole, offset, shape, per_q, scale):
    size = arrays[0].shape[-4]
    signals = shape[-1]
    specs = [pl.BlockSpec(memory_space=pltpu.SMEM)]
    for a, lead in zip(arrays, leads):
        specs.append(
            pl.BlockSpec(
                tuple(lead) + (1,) + a.shape[-3:],
                lambda c, n=len(lead): (0,) * n + (c, 0, 0, 0),
            )
        )
    operands = [me] + list(arrays)
    alias = {}
    if whole is not None:
        alias = {len(operands): 0}
        specs.append(pl.BlockSpec(memory_space=pl.ANY))
        operands.append(whole)
    return pl.pallas_call(
        functools.partial(correlate_kernel, sources, scale, per_q),
        grid=(size,),
        in_specs=specs,
        out_specs=pl.BlockSpec((1,) + shape[1:], lambda c: (c + offset, 0, 0, 0, 0)),
        out_shape=jax.ShapeDtypeStruct(shape, jnp.bfloat16),
        scratch_shapes=[pltpu.VMEM((signals, LANES), jnp.bfloat16)] * 2,
        input_output_aliases=alias,
        compiler_params=pltpu.CompilerParams(vmem_limit_bytes=40 << 20),
        cost_estimate=pl.CostEstimate(
            flops=size * 8 * signals * signals * 4 * LANES,
            bytes_accessed=size * 2 * math.prod(shape[1:]),
            transcendentals=0,
        ),
    )(*operands)


def chunk_sizes(channels):
    eighth = channels // 8
    return [eighth, eighth, 2 * eighth, 2 * eighth, 2 * eighth]


DIRECT = 3


def per_device(samples, coarse_taps, fine_taps):
    sig, samp = samples.shape
    taps_n, frame_len = coarse_taps.shape
    ftaps_n, fine_len = fine_taps.shape
    dests = lax.axis_size("sta")
    me = lax.axis_index("sta")
    win = lax.axis_index("win")
    frames = samp // frame_len
    fine_local = frames // fine_len
    total = fine_local * 2
    per_dest = fine_len // dests
    channels = KEEP // 2
    chunks = chunk_sizes(channels)
    low = 4
    high = dests // low

    hist = from_behind(samples[:, samp - (taps_n - 1) * frame_len :], "win", 1)
    dft = coarse_rows(frame_len, channels, chunks)
    parts = coarse(samples, hist, coarse_taps, dft, chunks)
    own, away = parts[: len(chunks)], parts[len(chunks) :]

    lane = jnp.arange(LANES, dtype=jnp.int32)
    frame_of = lane % total
    weights = fine_taps.astype(jnp.float32)

    def taps_table(side):
        block = side * fine_local + jnp.arange(fine_local, dtype=jnp.int32)
        late = frame_of[None, :] - block[:, None]
        table = jnp.zeros((fine_local, fine_len, LANES), jnp.float32)
        for m in range(ftaps_n):
            table = table + jnp.where((late == m)[:, None, :], weights[m][None, :, None], 0.0)
        return table

    def turn_tables(order):
        fine_of = (me ^ jnp.array(order, jnp.int32))[:, None] * per_dest + (lane // total)[None, :]
        turns = fine_of[:, None, :] * jnp.arange(fine_len, dtype=jnp.int32)[None, :, None]
        angles = (turns % fine_len).astype(jnp.float32) * (2.0 * math.pi / fine_len)
        return jnp.cos(angles), jnp.sin(angles)

    town, toth = taps_table(win), taps_table(1 - win)
    straight = turn_tables(list(range(dests)))
    turned = turn_tables([low * z + 2 * y + c for c in range(2) for y in range(2) for z in range(high)])

    shape = (channels, per_dest, 2, sig * dests, sig * dests)
    result, offset = None, 0
    oths = [swap(away[k], "win", 1) for k in range(len(chunks))]
    for k, size in enumerate(chunks):
        sent = fine(
            own[k], oths[k], town, toth, *(straight if k < DIRECT else turned), low if k < DIRECT else dests // 2
        )
        highs = range(high)
        if k < DIRECT:
            held = [sent[0]] + [swap(sent[n], "sta", low * n) for n in highs if n]
            over = swap(jnp.stack([h[2:] for h in held]), "sta", 2)
            last = swap(jnp.stack([jnp.stack([h[1] for h in held]), over[:, 1]]), "sta", 1)
            arrays = held + [over, last]
            leads = [(1,)] * high + [(high, 1), (2, high)]
            sources = [[((0,), low * n)] for n in highs]
            sources.append([((n, 0), low * n + 2) for n in highs])
            sources.append([((y, n), low * n + 2 * y + 1) for y in range(2) for n in highs])
        else:
            near, pair = sent[0], swap(sent[1], "sta", 1)
            over = swap(jnp.stack([near[high:], pair[high:]]), "sta", 2)
            arrays, leads = [near, pair, over], [(1,), (1,), (2, 1)]
            sources = [[((0,), 0)], [((0,), 1)], [((c, 0), 2 + c) for c in range(2)]]
            for n in highs:
                if n:
                    block = jnp.stack([near[n], pair[n], over[0, n], over[1, n]])
                    arrays.append(swap(block, "sta", low * n))
                    leads.append((low,))
                    sources.append([((b,), low * n + b) for b in range(low)])
        result = correlate_chunk(
            me[None].astype(jnp.int32), arrays, leads, sources, result, offset, shape, total, 1.0 / total
        )
        offset += size
    return result


def serves(mesh, samples, coarse_taps, fine_taps):
    wins, stas = mesh.shape["win"], mesh.shape["sta"]
    sig, samp = samples.shape[0] // stas, samples.shape[1] // wins
    taps_n, frame_len = coarse_taps.shape
    fine_len = fine_taps.shape[1]
    frames = samp // frame_len
    return (
        wins == 2
        and stas % 4 == 0
        and stas & (stas - 1) == 0
        and sig == ROWS
        and taps_n == ROWS
        and frame_len % WIDE == 0
        and frames % BLOCK == 0
        and frames % fine_len == 0
        and fine_len % stas == 0
        and fine_len // stas * (2 * frames // fine_len) == LANES
    )


def solution(mesh):
    placed = (P("sta", "win"), P(), P())

    def step(samples, coarse_taps, fine_taps):
        own_path = serves(mesh, samples, coarse_taps, fine_taps)

        def body(*args):
            if not own_path:
                return per_device_general(*args)
            return per_device(*args)

        f = jax.shard_map(
            body,
            mesh=mesh,
            in_specs=placed,
            out_specs=P("win", "sta", None, None, None),
            check_vma=False,
        )
        return f(samples, coarse_taps, fine_taps)

    return step
```

profile of v0, /device:TPU:0, one launch (start us, length us, event | category | flops | bytes accessed | tf_op | source)
XLA Modules:
  0.0 383.2 jit_solution(556940021694191433)
XLA Ops:
  0.0 1.0 slice.200
  1.0 4.9 %collective-permute-start = (bf16[16,7680]{1,0:T(8,128)(2,1)S(1)}, bf16[16,7680]{1,0:T(8,128)(2,1)S(1)}, u32[]{:S(2)}, u32[]{:S(2)}) collective-permute-start(bf16[16,7680]{1,0:T(8,128)(2,1)S(1)} %slice.200), channel_id=1, source_target_pairs={{0,16},{1,17},{2,18},{3,19},{4,20},{5,21},{6,22},{7,23},{8,24},{9,... | collective-permute-start | bytes 737288 | tf_op jit(solution)/shard_map/ppermute | solution.py:22
  6.0 0.1 concatenate.26
  6.2 0.7 copy.22
  6.9 0.7 convert_element_type.17
  7.6 2.5 select_convert_fusion.dft_ref
  10.1 0.7 xor_multiply_fusion
  10.8 0.1 subtract_compare_fusion.7
  10.9 2.9 fusion.18
  13.8 50.1 %shard_map.55 = (bf16[16,16,1024]{2,1,0:T(8,128)(2,1)S(1)}, bf16[16,16,1024]{2,1,0:T(8,128)(2,1)S(1)}, bf16[16,32,1024]{2,1,0:T(8,128)(2,1)S(1)}, bf16[16,32,102...) custom-call(bf16[16,524288]{1,0:T(8,128)(2,1)} %before_ref.1, ...), custom_call_target="tpu_custom_call" | custom-call | flops 38654705664 | bytes 33554432 | tf_op jit(solution)/shard_map/pallas_call | solution.py:247
  64.0 0.6 select_add_fusion.toth_ref
  64.5 2.0 fusion.20
  66.6 2.1 collective-permute-start.19
  68.7 0.6 select_add_fusion.1.town_ref
  69.2 0.1 collective-permute-start.13
  69.3 2.0 collective-permute-start.7
  71.4 7.4 %collective-permute-done.25.oth_ref = bf16[16,16,1024]{2,1,0:T(8,128)(2,1)S(1)} collective-permute-done((bf16[16,16,1024]{2,1,0:T(8,128)(2,1)S(1)}, bf16[16,16,1024]{2,1,0:T(8,128)(2,1)S(1)}, u32[]{:S(2)}, u32[]{:S(2)}) %collective-permute-start.25) | collective-permute-done | bytes 524320 | tf_op jit(solution)/shard_map/ppermute | solution.py:111
  78.7 10.4 %shard_map.60 = (bf16[4,8,2,16,128]{4,3,2,1,0:T(8,128)(2,1)S(1)}, bf16[4,8,2,16,128]{4,3,2,1,0:T(8,128)(2,1)S(1)}, bf16[4,8,2,16,128]{4,3,2,1,0:T(8,128)(2,1)S(1)}, bf16[4,8,2,16,128]{4,3,2,1,0:T(8,128)(2,1)S(1)}) custom-call(bf16[16,16,1024]{2,1,0:T(8,128)(2,1)S(1)} %get-tuple-element.51.own_ref, bf16[16,16,1024]{2,1,0:T(8,128)(2,1)S(1)} %collective-permute-done.25.oth_ref, ...), custom_call_target="tpu_custom_call" | custom-call | flops 4294967296 | bytes 1572864 | tf_op jit(solution)/shard_map/pallas_call | solution.py:318
  89.2 2.7 collective-permute-start.27
  91.8 1.8 collective-permute-start.28
  93.6 10.4 %shard_map.59 = (bf16[4,8,2,16,128]{4,3,2,1,0:T(8,128)(2,1)S(1)}, bf16[4,8,2,16,128]{4,3,2,1,0:T(8,128)(2,1)S(1)}, bf16[4,8,2,16,128]{4,3,2,1,0:T(8,128)(2,1)S(1)}, bf16[4,8,2,16,128]{4,3,2,1,0:T(8,128)(2,1)S(1)}) custom-call(bf16[16,16,1024]{2,1,0:T(8,128)(2,1)S(1)} %get-tuple-element.45.own_ref, bf16[16,16,1024]{2,1,0:T(8,128)(2,1)S(1)} %collective-permute-done.19.oth_ref, ...), custom_call_target="tpu_custom_call" | custom-call | flops 4294967296 | bytes 1572864 | tf_op jit(solution)/shard_map/pallas_call | solution.py:318
  104.1 9.1 %collective-permute-start.26 = (bf16[4,8,2,16,128]{4,3,2,1,0:T(8,128)(2,1)S(1)}, bf16[4,8,2,16,128]{4,3,2,1,0:T(8,128)(2,1)S(1)}, u32[]{:S(2)}, u32[]{:S(2)}) collective-permute-start(bf16[4,8,2,16,128]{4,3,2,1,0:T(8,128)(2,1)S(1)} %get-tuple-element.54), channel_id=1, source_target_pairs={{0,4},{1,5},{2,6},{3,7},{4,0},{5,1},{6,2},{7,3},{8,12},{9,13},{10,... | collective-permute-start | bytes 786440 | tf_op jit(solution)/shard_map/ppermute | solution.py:111
  113.2 3.4 collective-permute-start.22
  116.6 3.2 collective-permute-done.26.refs_1_
  119.8 2.5 collective-permute-start.20
  122.3 7.0 %collective-permute-done.22.refs_3_ = bf16[4,8,2,16,128]{4,3,2,1,0:T(8,128)(2,1)S(1)} collective-permute-done((bf16[4,8,2,16,128]{4,3,2,1,0:T(8,128)(2,1)S(1)}, bf16[4,8,2,16,128]{4,3,2,1,0:T(8,128)(2,1)S(1)}, u32[]{:S(2)}, u32[]{:S(2)}) %collective-permute-start.22) | collective-permute-done | bytes 262176 | tf_op jit(solution)/shard_map/ppermute | solution.py:111
  129.4 13.1 %collective-permute-done.21.refs_2_ = bf16[4,8,2,16,128]{4,3,2,1,0:T(8,128)(2,1)S(1)} collective-permute-done((bf16[4,8,2,16,128]{4,3,2,1,0:T(8,128)(2,1)S(1)}, bf16[4,8,2,16,128]{4,3,2,1,0:T(8,128)(2,1)S(1)}, u32[]{:S(2)}, u32[]{:S(2)}) %collective-permute-start.21) | collective-permute-done | bytes 262176 | tf_op jit(solution)/shard_map/ppermute | solution.py:111
  142.5 1.5 collective-permute-start.29
  144.1 0.6 collective-permute-start.23
  144.9 1.0 copy-done.3
  145.8 14.4 %shard_map.57 = (bf16[8,16,2,16,128]{4,3,2,1,0:T(8,128)(2,1)S(1)}, bf16[8,16,2,16,128]{4,3,2,1,0:T(8,128)(2,1)}) custom-call(bf16[16,32,1024]{2,1,0:T(8,128)(2,1)} %get-tuple-element.35.own_ref, bf16[16,32,1024]{2,1,0:T(8,128)(2,1)} %copy-done.3, f32[16,64,128]{2,1,0:T(8,128)S(1)} %select_add_fusion.1.town_ref, f32[16,64,128]{2,1,0:T(8,128)S(1)} %select_add_fusion.toth_ref, ...), custom_call_target="tpu_custom_call" | custom-call | flops 8589934592 | bytes 3145728 | tf_op jit(solution)/shard_map/pallas_call | solution.py:318
  160.3 14.1 %shard_map.58 = (bf16[4,16,2,16,128]{4,3,2,1,0:T(8,128)(2,1)S(1)}, bf16[4,16,2,16,128]{4,3,2,1,0:T(8,128)(2,1)S(1)}, bf16[4,16,2,16,128]{4,3,2,1,0:T(8,128)(2,1)S(1)}, bf16[4,16,2,16,128]{4,3,2,1,0:T(8,128)(2,1)S(1)}) custom-call(bf16[16,32,1024]{2,1,0:T(8,128)(2,1)} %copy-done, bf16[16,32,1024]{2,1,0:T(8,128)(2,1)} %collective-permute-done.13.oth_ref, ...), custom_call_target="tpu_custom_call" | custom-call | flops 8589934592 | bytes 3145728 | tf_op jit(solution)/shard_map/pallas_call | solution.py:318
  174.4 1.0 copy-done.1
  175.4 14.4 %shard_map.56 = (bf16[8,16,2,16,128]{4,3,2,1,0:T(8,128)(2,1)S(1)}, bf16[8,16,2,16,128]{4,3,2,1,0:T(8,128)(2,1)}) custom-call(bf16[16,32,1024]{2,1,0:T(8,128)(2,1)} %get-tuple-element.31.own_ref, bf16[16,32,1024]{2,1,0:T(8,128)(2,1)} %copy-done.1, f32[16,64,128]{2,1,0:T(8,128)S(1)} %select_add_fusion.1.town_ref, f32[16,64,128]{2,1,0:T(8,128)S(1)} %select_add_fusion.toth_ref, ...), custom_call_target="tpu_custom_call" | custom-call | flops 8589934592 | bytes 3145728 | tf_op jit(solution)/shard_map/pallas_call | solution.py:318
  189.9 0.8 collective-permute-start.15
  190.7 3.5 collective-permute-start.16
  194.5 0.6 collective-permute-start.2
  195.2 27.2 %collective-permute-done.16.refs_3_ = bf16[4,16,2,16,128]{4,3,2,1,0:T(8,128)(2,1)S(1)} collective-permute-done((bf16[4,16,2,16,128]{4,3,2,1,0:T(8,128)(2,1)S(1)}, bf16[4,16,2,16,128]{4,3,2,1,0:T(8,128)(2,1)S(1)}, u32[]{:S(2)}, u32[]{:S(2)}) %collective-permute-start.16) | collective-permute-done | bytes 524320 | tf_op jit(solution)/shard_map/ppermute | solution.py:111
  222.5 5.7 %collective-permute-done.15.refs_2_ = bf16[4,16,2,16,128]{4,3,2,1,0:T(8,128)(2,1)S(1)} collective-permute-done((bf16[4,16,2,16,128]{4,3,2,1,0:T(8,128)(2,1)S(1)}, bf16[4,16,2,16,128]{4,3,2,1,0:T(8,128)(2,1)S(1)}, u32[]{:S(2)}, u32[]{:S(2)}) %collective-permute-start.15) | collective-permute-done | bytes 524320 | tf_op jit(solution)/shard_map/ppermute | solution.py:111
  228.2 0.1 pad_maximum_fusion.2
  228.3 1.6 collective-permute-start.17
  230.1 6.5 %shard_map.61.refs_6_ = bf16[64,4,2,256,256]{4,3,2,1,0:T(8,128)(2,1)} custom-call(s32[1]{0:T(128)} %bitcast.me_ref, bf16[4,8,2,16,128]{4,3,2,1,0:T(8,128)(2,1)S(1)} %get-tuple-element.53.refs_0_, bf16[4,8,2,16,128]{4,3,2,1,0:T(8,128)(2,1)S(1)} %collective-permute-done.26.refs_1_, bf16[4,8,2,16,128]{4,3,2,1,0:T(8,128)(2,1)S(1)} %collective-permute-done.27.refs_2_, ...), custom_call_target="tpu_custom_call" | custom-call | flops 2147483648 | bytes 8388608 | tf_op jit(solution)/shard_map/pallas_call | solution.py:382
  236.6 6.5 %shard_map.62.refs_6_ = bf16[64,4,2,256,256]{4,3,2,1,0:T(8,128)(2,1)} custom-call(s32[1]{0:T(128)} %bitcast.me_ref, bf16[4,8,2,16,128]{4,3,2,1,0:T(8,128)(2,1)S(1)} %get-tuple-element.47.refs_0_, bf16[4,8,2,16,128]{4,3,2,1,0:T(8,128)(2,1)S(1)} %collective-permute-done.20.refs_1_, ...), custom_call_target="tpu_custom_call", output_to_operand_aliasing={{}: (7, {})} | custom-call | flops 2147483648 | bytes 8388608 | tf_op jit(solution)/shard_map/pallas_call | solution.py:382
  243.2 0.1 pad_maximum_fusion.1
  243.3 0.6 collective-permute-start.9
  243.9 0.1 pad_maximum_fusion
  244.0 1.6 collective-permute-start.3
  245.6 8.8 %collective-permute-done.17 = bf16[4,2,16,2,16,128]{5,4,3,2,0,1:T(8,128)(2,1)S(1)} collective-permute-done((bf16[4,2,16,2,16,128]{5,4,3,2,0,1:T(8,128)(2,1)S(1)}, bf16[4,2,16,2,16,128]{5,4,3,2,0,1:T(8,128)(2,1)S(1)}, u32[]{:S(2)}, u32[]{:S(2)}) %collective-permute-start.17) | collective-permute-done | bytes 1048608 | tf_op jit(solution)/shard_map/ppermute | solution.py:111
  254.5 0.1 pad_maximum_fusion.3
  254.7 0.1 copy.19.refs_4_
  254.8 22.1 %collective-permute-done.9.refs_2_ = bf16[2,4,16,2,16,128]{5,4,3,2,1,0:T(8,128)(2,1)S(1)} collective-permute-done((bf16[2,4,16,2,16,128]{5,4,3,2,1,0:T(8,128)(2,1)S(1)}, bf16[2,4,16,2,16,128]{5,4,3,2,1,0:T(8,128)(2,1)S(1)}, u32[]{:S(2)}, u32[]{:S(2)}) %collective-permute-start.9) | collective-permute-done | bytes 1048608 | tf_op jit(solution)/shard_map/ppermute | solution.py:111
  276.9 0.1 slice_bitcast_fusion.18
  277.1 1.4 collective-permute-start.12
  278.6 8.9 %collective-permute-start.11 = (bf16[4,16,2,16,128]{4,3,2,1,0:T(8,128)(2,1)S(1)}, bf16[4,16,2,16,128]{4,3,2,1,0:T(8,128)(2,1)S(1)}, u32[]{:S(2)}, u32[]{:S(2)}) collective-permute-start(bf16[4,16,2,16,128]{4,3,2,1,0:T(8,128)(2,1)S(1)} %pad_maximum_fusion.8), channel_id=1, source_target_pairs={{0,8},{1,9},{2,10},{3,11},{4,12},{5,13},{6,14},{7,15},{8,0},{9,1},... | collective-permute-start | bytes 1572872 | tf_op jit(solution)/shard_map/ppermute | solution.py:111
  287.7 11.2 %collective-permute-done.3.refs_2_ = bf16[2,4,16,2,16,128]{5,4,3,2,1,0:T(8,128)(2,1)S(1)} collective-permute-done((bf16[2,4,16,2,16,128]{5,4,3,2,1,0:T(8,128)(2,1)S(1)}, bf16[2,4,16,2,16,128]{5,4,3,2,1,0:T(8,128)(2,1)S(1)}, u32[]{:S(2)}, u32[]{:S(2)}) %collective-permute-start.3) | collective-permute-done | bytes 1048608 | tf_op jit(solution)/shard_map/ppermute | solution.py:111
  298.9 0.1 slice_bitcast_fusion.24
  299.1 1.4 collective-permute-start.6
  300.7 8.5 %collective-permute-start.5 = (bf16[4,16,2,16,128]{4,3,2,1,0:T(8,128)(2,1)S(1)}, bf16[4,16,2,16,128]{4,3,2,1,0:T(8,128)(2,1)S(1)}, u32[]{:S(2)}, u32[]{:S(2)}) collective-permute-start(bf16[4,16,2,16,128]{4,3,2,1,0:T(8,128)(2,1)S(1)} %pad_maximum_fusion.5), channel_id=1, source_target_pairs={{0,8},{1,9},{2,10},{3,11},{4,12},{5,13},{6,14},{7,15},{8,0},{9,1},... | collective-permute-start | bytes 1572872 | tf_op jit(solution)/shard_map/ppermute | solution.py:111
  309.2 7.7 %collective-permute-start.4 = (bf16[4,16,2,16,128]{4,3,2,1,0:T(8,128)(2,1)S(1)}, bf16[4,16,2,16,128]{4,3,2,1,0:T(8,128)(2,1)S(1)}, u32[]{:S(2)}, u32[]{:S(2)}) collective-permute-start(bf16[4,16,2,16,128]{4,3,2,1,0:T(8,128)(2,1)S(1)} %pad_maximum_fusion.4), channel_id=1, source_target_pairs={{0,4},{1,5},{2,6},{3,7},{4,0},{5,1},{6,2},{7,3},{8,12},{9,13},{10,... | collective-permute-start | bytes 1572872 | tf_op jit(solution)/shard_map/ppermute | solution.py:111
  316.9 12.5 %shard_map.63.refs_6_ = bf16[64,4,2,256,256]{4,3,2,1,0:T(8,128)(2,1)} custom-call(s32[1]{0:T(128)} %bitcast.me_ref, bf16[4,16,2,16,128]{4,3,2,1,0:T(8,128)(2,1)S(1)} %get-tuple-element.41.refs_0_, bf16[4,16,2,16,128]{4,3,2,1,0:T(8,128)(2,1)S(1)} %collective-permute-done.14.refs_1_, ...), custom_call_target="tpu_custom_call", output_to_operand_aliasing={{}: (7, {})} | custom-call | flops 4294967296 | bytes 16777216 | tf_op jit(solution)/shard_map/pallas_call | solution.py:382
  329.4 18.9 %collective-permute-done.11.refs_4_ = bf16[4,16,2,16,128]{4,3,2,1,0:T(8,128)(2,1)S(1)} collective-permute-done((bf16[4,16,2,16,128]{4,3,2,1,0:T(8,128)(2,1)S(1)}, bf16[4,16,2,16,128]{4,3,2,1,0:T(8,128)(2,1)S(1)}, u32[]{:S(2)}, u32[]{:S(2)}) %collective-permute-start.11) | collective-permute-done | bytes 524320 | tf_op jit(solution)/shard_map/ppermute | solution.py:111
  348.3 12.5 %shard_map.64.refs_6_ = bf16[64,4,2,256,256]{4,3,2,1,0:T(8,128)(2,1)} custom-call(s32[1]{0:T(128)} %bitcast.me_ref, bf16[8,16,2,16,128]{4,3,2,1,0:T(8,128)(2,1)S(1)} %get-tuple-element.37.refs_0_, bf16[8,16,2,16,128]{4,3,2,1,0:T(8,128)(2,1)S(1)} %collective-permute-done.8.refs_1_, ...), custom_call_target="tpu_custom_call", output_to_operand_aliasing={{}: (7, {})} | custom-call | flops 4294967296 | bytes 16777216 | tf_op jit(solution)/shard_map/pallas_call | solution.py:382
  360.8 9.9 %collective-permute-done.5.refs_4_ = bf16[4,16,2,16,128]{4,3,2,1,0:T(8,128)(2,1)S(1)} collective-permute-done((bf16[4,16,2,16,128]{4,3,2,1,0:T(8,128)(2,1)S(1)}, bf16[4,16,2,16,128]{4,3,2,1,0:T(8,128)(2,1)S(1)}, u32[]{:S(2)}, u32[]{:S(2)}) %collective-permute-start.5) | collective-permute-done | bytes 524320 | tf_op jit(solution)/shard_map/ppermute | solution.py:111
  370.7 12.5 %shard_map.65 = bf16[64,4,2,256,256]{4,3,2,1,0:T(8,128)(2,1)} custom-call(s32[1]{0:T(128)} %bitcast.me_ref, bf16[8,16,2,16,128]{4,3,2,1,0:T(8,128)(2,1)S(1)} %get-tuple-element.33.refs_0_, bf16[8,16,2,16,128]{4,3,2,1,0:T(8,128)(2,1)S(1)} %collective-permute-done.2.refs_1_, ...), custom_call_target="tpu_custom_call", output_to_operand_aliasing={{}: (7, {})} | custom-call | flops 4294967296 | bytes 16777216 | tf_op jit(solution)/shard_map/pallas_call | solution.py:382
  (103 shorter events, 2.1 us)
Async XLA Ops:
  1.0 12.8 %collective-permute-start = (bf16[16,7680]{1,0:T(8,128)(2,1)S(1)}, bf16[16,7680]{1,0:T(8,128)(2,1)S(1)}, u32[]{:S(2)}, u32[]{:S(2)}) collective-permute-start(bf16[16,7680]{1,0:T(8,128)(2,1)S(1)} %slice.200), channel_id=1, source_target_pairs={{0,16},{1,17},{2,18},{3,19},{4,20},{5,21},{6,22},{7,23},{8,24},{9,... | collective-permute-start | bytes 737288 | tf_op jit(solution)/shard_map/ppermute | solution.py:22
  63.9 2.7 copy-start
  63.9 14.8 %collective-permute-start.25 = (bf16[16,16,1024]{2,1,0:T(8,128)(2,1)S(1)}, bf16[16,16,1024]{2,1,0:T(8,128)(2,1)S(1)}, u32[]{:S(2)}, u32[]{:S(2)}) collective-permute-start(bf16[16,16,1024]{2,1,0:T(8,128)(2,1)S(1)} %get-tuple-element.52), channel_id=1, source_target_pairs={{0,16},{16,0},{1,17},{17,1},{2,18},{18,2},{3,19},{19,3},{4,20},{20... | collective-permute-start | bytes 1572872 | tf_op jit(solution)/shard_map/ppermute | solution.py:111
  66.6 25.2 %collective-permute-start.19 = (bf16[16,16,1024]{2,1,0:T(8,128)(2,1)S(1)}, bf16[16,16,1024]{2,1,0:T(8,128)(2,1)S(1)}, u32[]{:S(2)}, u32[]{:S(2)}) collective-permute-start(bf16[16,16,1024]{2,1,0:T(8,128)(2,1)S(1)} %get-tuple-element.46), channel_id=1, source_target_pairs={{0,16},{16,0},{1,17},{17,1},{2,18},{18,2},{3,19},{19,3},{4,20},{20... | collective-permute-start | bytes 1572872 | tf_op jit(solution)/shard_map/ppermute | solution.py:111
  69.2 91.1 %collective-permute-start.13 = (bf16[16,32,1024]{2,1,0:T(8,128)(2,1)}, bf16[16,32,1024]{2,1,0:T(8,128)(2,1)}, u32[]{:S(2)}, u32[]{:S(2)}) collective-permute-start(bf16[16,32,1024]{2,1,0:T(8,128)(2,1)} %get-tuple-element.40), channel_id=1, source_target_pairs={{0,16},{16,0},{1,17},{17,1},{2,18},{18,2},{3,19},{19,3},{4,20},{20... | collective-permute-start | bytes 3145736 | tf_op jit(solution)/shard_map/ppermute | solution.py:111
  69.3 75.5 %collective-permute-start.7 = (bf16[16,32,1024]{2,1,0:T(8,128)(2,1)}, bf16[16,32,1024]{2,1,0:T(8,128)(2,1)S(1)}, u32[]{:S(2)}, u32[]{:S(2)}) collective-permute-start(bf16[16,32,1024]{2,1,0:T(8,128)(2,1)} %get-tuple-element.36), channel_id=1, source_target_pairs={{0,16},{16,0},{1,17},{17,1},{2,18},{18,2},{3,19},{19,3},{4,20},{20... | collective-permute-start | bytes 3145736 | tf_op jit(solution)/shard_map/ppermute | solution.py:111
  71.3 103.1 %collective-permute-start.1 = (bf16[16,32,1024]{2,1,0:T(8,128)(2,1)}, bf16[16,32,1024]{2,1,0:T(8,128)(2,1)S(1)}, u32[]{:S(2)}, u32[]{:S(2)}) collective-permute-start(bf16[16,32,1024]{2,1,0:T(8,128)(2,1)} %get-tuple-element.32), channel_id=1, source_target_pairs={{0,16},{16,0},{1,17},{17,1},{2,18},{18,2},{3,19},{19,3},{4,20},{20... | collective-permute-start | bytes 3145736 | tf_op jit(solution)/shard_map/ppermute | solution.py:111
  89.2 24.0 %collective-permute-start.27 = (bf16[4,8,2,16,128]{4,3,2,1,0:T(8,128)(2,1)S(1)}, bf16[4,8,2,16,128]{4,3,2,1,0:T(8,128)(2,1)S(1)}, u32[]{:S(2)}, u32[]{:S(2)}) collective-permute-start(bf16[4,8,2,16,128]{4,3,2,1,0:T(8,128)(2,1)S(1)} %get-tuple-element.55), channel_id=1, source_target_pairs={{0,8},{1,9},{2,10},{3,11},{4,12},{5,13},{6,14},{7,15},{8,0},{9,1},... | collective-permute-start | bytes 786440 | tf_op jit(solution)/shard_map/ppermute | solution.py:111
  91.8 12.2 %collective-permute-start.28 = (bf16[4,8,2,16,128]{4,3,2,1,0:T(8,128)(2,1)S(1)}, bf16[4,8,2,16,128]{4,3,2,1,0:T(8,128)(2,1)S(1)}, u32[]{:S(2)}, u32[]{:S(2)}) collective-permute-start(bf16[4,8,2,16,128]{4,3,2,1,0:T(8,128)(2,1)S(1)} %get-tuple-element.56), channel_id=1, source_target_pairs={{0,12},{1,13},{2,14},{3,15},{4,8},{5,9},{6,10},{7,11},{8,4},{9,5},... | collective-permute-start | bytes 786440 | tf_op jit(solution)/shard_map/ppermute | solution.py:111
  104.1 15.8 %collective-permute-start.26 = (bf16[4,8,2,16,128]{4,3,2,1,0:T(8,128)(2,1)S(1)}, bf16[4,8,2,16,128]{4,3,2,1,0:T(8,128)(2,1)S(1)}, u32[]{:S(2)}, u32[]{:S(2)}) collective-permute-start(bf16[4,8,2,16,128]{4,3,2,1,0:T(8,128)(2,1)S(1)} %get-tuple-element.54), channel_id=1, source_target_pairs={{0,4},{1,5},{2,6},{3,7},{4,0},{5,1},{6,2},{7,3},{8,12},{9,13},{10,... | collective-permute-start | bytes 786440 | tf_op jit(solution)/shard_map/ppermute | solution.py:111
  113.2 16.1 %collective-permute-start.22 = (bf16[4,8,2,16,128]{4,3,2,1,0:T(8,128)(2,1)S(1)}, bf16[4,8,2,16,128]{4,3,2,1,0:T(8,128)(2,1)S(1)}, u32[]{:S(2)}, u32[]{:S(2)}) collective-permute-start(bf16[4,8,2,16,128]{4,3,2,1,0:T(8,128)(2,1)S(1)} %get-tuple-element.50), channel_id=1, source_target_pairs={{0,12},{1,13},{2,14},{3,15},{4,8},{5,9},{6,10},{7,11},{8,4},{9,5},... | collective-permute-start | bytes 786440 | tf_op jit(solution)/shard_map/ppermute | solution.py:111
  119.8 24.2 %collective-permute-start.20 = (bf16[4,8,2,16,128]{4,3,2,1,0:T(8,128)(2,1)S(1)}, bf16[4,8,2,16,128]{4,3,2,1,0:T(8,128)(2,1)S(1)}, u32[]{:S(2)}, u32[]{:S(2)}) collective-permute-start(bf16[4,8,2,16,128]{4,3,2,1,0:T(8,128)(2,1)S(1)} %get-tuple-element.48), channel_id=1, source_target_pairs={{0,4},{1,5},{2,6},{3,7},{4,0},{5,1},{6,2},{7,3},{8,12},{9,13},{10,... | collective-permute-start | bytes 786440 | tf_op jit(solution)/shard_map/ppermute | solution.py:111
  129.3 13.2 %collective-permute-start.21 = (bf16[4,8,2,16,128]{4,3,2,1,0:T(8,128)(2,1)S(1)}, bf16[4,8,2,16,128]{4,3,2,1,0:T(8,128)(2,1)S(1)}, u32[]{:S(2)}, u32[]{:S(2)}) collective-permute-start(bf16[4,8,2,16,128]{4,3,2,1,0:T(8,128)(2,1)S(1)} %get-tuple-element.49), channel_id=1, source_target_pairs={{0,8},{1,9},{2,10},{3,11},{4,12},{5,13},{6,14},{7,15},{8,0},{9,1},... | collective-permute-start | bytes 786440 | tf_op jit(solution)/shard_map/ppermute | solution.py:111
  142.5 51.8 %collective-permute-start.29 = (bf16[4,2,8,2,16,128]{5,4,3,2,0,1:T(8,128)(2,1)S(1)}, bf16[4,2,8,2,16,128]{5,4,3,2,0,1:T(8,128)(2,1)S(1)}, u32[]{:S(2)}, u32[]{:S(2)}) collective-permute-start(bf16[4,2,8,2,16,128]{5,4,3,2,0,1:T(8,128)(2,1)S(1)} %pad_maximum_fusion.12), channel_id=1, source_target_pairs={{0,2},{1,3},{2,0},{3,1},{4,6},{5,7},{6,4},{7,5},{8,10},{9,11},{10,... | collective-permute-start | bytes 1572872 | tf_op jit(solution)/shard_map/ppermute | solution.py:111
  144.1 50.3 %collective-permute-start.23 = (bf16[4,2,8,2,16,128]{5,4,3,2,0,1:T(8,128)(2,1)S(1)}, bf16[4,2,8,2,16,128]{5,4,3,2,0,1:T(8,128)(2,1)S(1)}, u32[]{:S(2)}, u32[]{:S(2)}) collective-permute-start(bf16[4,2,8,2,16,128]{5,4,3,2,0,1:T(8,128)(2,1)S(1)} %pad_maximum_fusion.10), channel_id=1, source_target_pairs={{0,2},{1,3},{2,0},{3,1},{4,6},{5,7},{6,4},{7,5},{8,10},{9,11},{10,... | collective-permute-start | bytes 1572872 | tf_op jit(solution)/shard_map/ppermute | solution.py:111
  144.9 1.0 copy-start.3
  160.2 34.1 %copy-start.2 = (bf16[8,16,2,16,128]{4,3,2,1,0:T(8,128)(2,1)S(1)}, bf16[8,16,2,16,128]{4,3,2,1,0:T(8,128)(2,1)}, u32[]{:S(2)}) copy-start(bf16[8,16,2,16,128]{4,3,2,1,0:T(8,128)(2,1)} %get-tuple-element.38) | copy-start | bytes 3145732
  174.4 1.0 copy-start.1
  189.8 38.3 %collective-permute-start.14 = (bf16[4,16,2,16,128]{4,3,2,1,0:T(8,128)(2,1)S(1)}, bf16[4,16,2,16,128]{4,3,2,1,0:T(8,128)(2,1)S(1)}, u32[]{:S(2)}, u32[]{:S(2)}) collective-permute-start(bf16[4,16,2,16,128]{4,3,2,1,0:T(8,128)(2,1)S(1)} %get-tuple-element.42), channel_id=1, source_target_pairs={{0,4},{1,5},{2,6},{3,7},{4,0},{5,1},{6,2},{7,3},{8,12},{9,13},{10,... | collective-permute-start | bytes 1572872 | tf_op jit(solution)/shard_map/ppermute | solution.py:111
  189.9 38.2 %collective-permute-start.15 = (bf16[4,16,2,16,128]{4,3,2,1,0:T(8,128)(2,1)S(1)}, bf16[4,16,2,16,128]{4,3,2,1,0:T(8,128)(2,1)S(1)}, u32[]{:S(2)}, u32[]{:S(2)}) collective-permute-start(bf16[4,16,2,16,128]{4,3,2,1,0:T(8,128)(2,1)S(1)} %get-tuple-element.43), channel_id=1, source_target_pairs={{0,8},{1,9},{2,10},{3,11},{4,12},{5,13},{6,14},{7,15},{8,0},{9,1},... | collective-permute-start | bytes 1572872 | tf_op jit(solution)/shard_map/ppermute | solution.py:111
  190.7 31.7 %collective-permute-start.16 = (bf16[4,16,2,16,128]{4,3,2,1,0:T(8,128)(2,1)S(1)}, bf16[4,16,2,16,128]{4,3,2,1,0:T(8,128)(2,1)S(1)}, u32[]{:S(2)}, u32[]{:S(2)}) collective-permute-start(bf16[4,16,2,16,128]{4,3,2,1,0:T(8,128)(2,1)S(1)} %get-tuple-element.44), channel_id=1, source_target_pairs={{0,12},{1,13},{2,14},{3,15},{4,8},{5,9},{6,10},{7,11},{8,4},{9,5},... | collective-permute-start | bytes 1572872 | tf_op jit(solution)/shard_map/ppermute | solution.py:111
  194.3 48.8 %collective-permute-start.8 = (bf16[8,16,2,16,128]{4,3,2,1,0:T(8,128)(2,1)S(1)}, bf16[8,16,2,16,128]{4,3,2,1,0:T(8,128)(2,1)S(1)}, u32[]{:S(2)}, u32[]{:S(2)}) collective-permute-start(bf16[8,16,2,16,128]{4,3,2,1,0:T(8,128)(2,1)S(1)} %copy-done.2), channel_id=1, source_target_pairs={{0,1},{1,0},{2,3},{3,2},{4,5},{5,4},{6,7},{7,6},{8,9},{9,8},{10,11... | collective-permute-start | bytes 3145736 | tf_op jit(solution)/shard_map/ppermute | solution.py:111
  194.5 49.4 %collective-permute-start.2 = (bf16[8,16,2,16,128]{4,3,2,1,0:T(8,128)(2,1)}, bf16[8,16,2,16,128]{4,3,2,1,0:T(8,128)(2,1)S(1)}, u32[]{:S(2)}, u32[]{:S(2)}) collective-permute-start(bf16[8,16,2,16,128]{4,3,2,1,0:T(8,128)(2,1)} %get-tuple-element.34), channel_id=1, source_target_pairs={{0,1},{1,0},{2,3},{3,2},{4,5},{5,4},{6,7},{7,6},{8,9},{9,8},{10,11... | collective-permute-start | bytes 3145736 | tf_op jit(solution)/shard_map/ppermute | solution.py:111
  222.5 7.6 %collective-permute-start.30 = (bf16[2,4,8,2,16,128]{5,4,3,2,1,0:T(8,128)(2,1)S(1)}, bf16[2,4,8,2,16,128]{5,4,3,2,1,0:T(8,128)(2,1)S(1)}, u32[]{:S(2)}, u32[]{:S(2)}) collective-permute-start(bf16[2,4,8,2,16,128]{5,4,3,2,1,0:T(8,128)(2,1)S(1)} %pad_maximum_fusion.13), channel_id=1, source_target_pairs={{0,1},{1,0},{2,3},{3,2},{4,5},{5,4},{6,7},{7,6},{8,9},{9,8},{10,11... | collective-permute-start | bytes 1572872 | tf_op jit(solution)/shard_map/ppermute | solution.py:111
  228.1 8.5 %collective-permute-start.24 = (bf16[2,4,8,2,16,128]{5,4,3,2,1,0:T(8,128)(2,1)S(1)}, bf16[2,4,8,2,16,128]{5,4,3,2,1,0:T(8,128)(2,1)S(1)}, u32[]{:S(2)}, u32[]{:S(2)}) collective-permute-start(bf16[2,4,8,2,16,128]{5,4,3,2,1,0:T(8,128)(2,1)S(1)} %pad_maximum_fusion.11), channel_id=1, source_target_pairs={{0,1},{1,0},{2,3},{3,2},{4,5},{5,4},{6,7},{7,6},{8,9},{9,8},{10,11... | collective-permute-start | bytes 1572872 | tf_op jit(solution)/shard_map/ppermute | solution.py:111
  228.3 26.1 %collective-permute-start.17 = (bf16[4,2,16,2,16,128]{5,4,3,2,0,1:T(8,128)(2,1)S(1)}, bf16[4,2,16,2,16,128]{5,4,3,2,0,1:T(8,128)(2,1)S(1)}, u32[]{:S(2)}, u32[]{:S(2)}) collective-permute-start(bf16[4,2,16,2,16,128]{5,4,3,2,0,1:T(8,128)(2,1)S(1)} %pad_maximum_fusion.2), channel_id=1, source_target_pairs={{0,2},{1,3},{2,0},{3,1},{4,6},{5,7},{6,4},{7,5},{8,10},{9,11},{10,... | collective-permute-start | bytes 3145736 | tf_op jit(solution)/shard_map/ppermute | solution.py:111
  243.3 33.6 %collective-permute-start.9 = (bf16[2,4,16,2,16,128]{5,4,3,2,1,0:T(8,128)(2,1)S(1)}, bf16[2,4,16,2,16,128]{5,4,3,2,1,0:T(8,128)(2,1)S(1)}, u32[]{:S(2)}, u32[]{:S(2)}) collective-permute-start(bf16[2,4,16,2,16,128]{5,4,3,2,1,0:T(8,128)(2,1)S(1)} %pad_maximum_fusion.1), channel_id=1, source_target_pairs={{0,2},{1,3},{2,0},{3,1},{4,6},{5,7},{6,4},{7,5},{8,10},{9,11},{10,... | collective-permute-start | bytes 3145736 | tf_op jit(solution)/shard_map/ppermute | solution.py:111
  244.0 54.9 %collective-permute-start.3 = (bf16[2,4,16,2,16,128]{5,4,3,2,1,0:T(8,128)(2,1)S(1)}, bf16[2,4,16,2,16,128]{5,4,3,2,1,0:T(8,128)(2,1)S(1)}, u32[]{:S(2)}, u32[]{:S(2)}) collective-permute-start(bf16[2,4,16,2,16,128]{5,4,3,2,1,0:T(8,128)(2,1)S(1)} %pad_maximum_fusion), channel_id=1, source_target_pairs={{0,2},{1,3},{2,0},{3,1},{4,6},{5,7},{6,4},{7,5},{8,10},{9,11},{10,... | collective-permute-start | bytes 3145736 | tf_op jit(solution)/shard_map/ppermute | solution.py:111
  254.6 46.1 %collective-permute-start.18 = (bf16[2,4,16,2,16,128]{5,4,3,2,1,0:T(8,128)(2,1)S(1)}, bf16[2,4,16,2,16,128]{5,4,3,2,1,0:T(8,128)(2,1)S(1)}, u32[]{:S(2)}, u32[]{:S(2)}) collective-permute-start(bf16[2,4,16,2,16,128]{5,4,3,2,1,0:T(8,128)(2,1)S(1)} %pad_maximum_fusion.3), channel_id=1, source_target_pairs={{0,1},{1,0},{2,3},{3,2},{4,5},{5,4},{6,7},{7,6},{8,9},{9,8},{10,11... | collective-permute-start | bytes 3145736 | tf_op jit(solution)/shard_map/ppermute | solution.py:111
  277.1 32.1 %collective-permute-start.12 = (bf16[4,16,2,16,128]{4,3,2,1,0:T(8,128)(2,1)S(1)}, bf16[4,16,2,16,128]{4,3,2,1,0:T(8,128)(2,1)S(1)}, u32[]{:S(2)}, u32[]{:S(2)}) collective-permute-start(bf16[4,16,2,16,128]{4,3,2,1,0:T(8,128)(2,1)S(1)} %pad_maximum_fusion.9), channel_id=1, source_target_pairs={{0,12},{1,13},{2,14},{3,15},{4,8},{5,9},{6,10},{7,11},{8,4},{9,5},... | collective-permute-start | bytes 1572872 | tf_op jit(solution)/shard_map/ppermute | solution.py:111
  278.6 69.7 %collective-permute-start.11 = (bf16[4,16,2,16,128]{4,3,2,1,0:T(8,128)(2,1)S(1)}, bf16[4,16,2,16,128]{4,3,2,1,0:T(8,128)(2,1)S(1)}, u32[]{:S(2)}, u32[]{:S(2)}) collective-permute-start(bf16[4,16,2,16,128]{4,3,2,1,0:T(8,128)(2,1)S(1)} %pad_maximum_fusion.8), channel_id=1, source_target_pairs={{0,8},{1,9},{2,10},{3,11},{4,12},{5,13},{6,14},{7,15},{8,0},{9,1},... | collective-permute-start | bytes 1572872 | tf_op jit(solution)/shard_map/ppermute | solution.py:111
  287.6 60.7 %collective-permute-start.10 = (bf16[4,16,2,16,128]{4,3,2,1,0:T(8,128)(2,1)S(1)}, bf16[4,16,2,16,128]{4,3,2,1,0:T(8,128)(2,1)S(1)}, u32[]{:S(2)}, u32[]{:S(2)}) collective-permute-start(bf16[4,16,2,16,128]{4,3,2,1,0:T(8,128)(2,1)S(1)} %pad_maximum_fusion.7), channel_id=1, source_target_pairs={{0,4},{1,5},{2,6},{3,7},{4,0},{5,1},{6,2},{7,3},{8,12},{9,13},{10,... | collective-permute-start | bytes 1572872 | tf_op jit(solution)/shard_map/ppermute | solution.py:111
  299.1 61.7 %collective-permute-start.6 = (bf16[4,16,2,16,128]{4,3,2,1,0:T(8,128)(2,1)S(1)}, bf16[4,16,2,16,128]{4,3,2,1,0:T(8,128)(2,1)S(1)}, u32[]{:S(2)}, u32[]{:S(2)}) collective-permute-start(bf16[4,16,2,16,128]{4,3,2,1,0:T(8,128)(2,1)S(1)} %pad_maximum_fusion.6), channel_id=1, source_target_pairs={{0,12},{1,13},{2,14},{3,15},{4,8},{5,9},{6,10},{7,11},{8,4},{9,5},... | collective-permute-start | bytes 1572872 | tf_op jit(solution)/shard_map/ppermute | solution.py:111
  300.7 70.0 %collective-permute-start.5 = (bf16[4,16,2,16,128]{4,3,2,1,0:T(8,128)(2,1)S(1)}, bf16[4,16,2,16,128]{4,3,2,1,0:T(8,128)(2,1)S(1)}, u32[]{:S(2)}, u32[]{:S(2)}) collective-permute-start(bf16[4,16,2,16,128]{4,3,2,1,0:T(8,128)(2,1)S(1)} %pad_maximum_fusion.5), channel_id=1, source_target_pairs={{0,8},{1,9},{2,10},{3,11},{4,12},{5,13},{6,14},{7,15},{8,0},{9,1},... | collective-permute-start | bytes 1572872 | tf_op jit(solution)/shard_map/ppermute | solution.py:111
  309.2 61.5 %collective-permute-start.4 = (bf16[4,16,2,16,128]{4,3,2,1,0:T(8,128)(2,1)S(1)}, bf16[4,16,2,16,128]{4,3,2,1,0:T(8,128)(2,1)S(1)}, u32[]{:S(2)}, u32[]{:S(2)}) collective-permute-start(bf16[4,16,2,16,128]{4,3,2,1,0:T(8,128)(2,1)S(1)} %pad_maximum_fusion.4), channel_id=1, source_target_pairs={{0,4},{1,5},{2,6},{3,7},{4,0},{5,1},{6,2},{7,3},{8,12},{9,13},{10,... | collective-permute-start | bytes 1572872 | tf_op jit(solution)/shard_map/ppermute | solution.py:111
where the time goes:
time: 386 us; the launch traced here: 383 us
  Pallas kernels  164 us (42%)
  waiting for transfers between devices  134 us (35%)
  starting transfers between devices  67.6 us (18%)
  other arithmetic  11.4 us (3%)
  local copies, waits for them, and re-layouts  4.73 us (1%)
    ppermute x30, waiting for transfers between devices, swap(): lax.ppermute(x, axis, [(i, i ^ by) for i in range(lax.axis_size(axis))])  134 us
    pallas_call x5, Pallas kernels, fine(): pl.pallas_call(functools.partial(fine_kernel, low), grid=(dests,), in_spe...  63.6 us
    ppermute x30, starting transfers between devices, swap(): lax.ppermute(x, axis, [(i, i ^ by) for i in range(lax.axis_size(axis))])  62.8 us
    pallas_call x5, Pallas kernels, correlate_chunk(): pl.pallas_call(functools.partial(correlate_kernel, sources, scale, per_q)...  50.5 us
    pallas_call x1, Pallas kernels, coarse(): pl.pallas_call(functools.partial(coarse_kernel, chunks, taps_n), grid=(bl...  50.1 us
  transfers between devices with their start and end apart: 31, of which 11 were waited for; matrix products, arithmetic and copies ran while one was open for 3% of the time, Pallas kernels for 27%

commit v1 on v0

--- a/solution.py
+++ b/solution.py
@@ -12,6 +12,8 @@
 LANES = 128
 WIDE = 256
 PITCH = 17
+GROUP = 4
+VMEM = 63 << 20
 ROWS = 16
 BLOCK = 128
 
@@ -164,7 +166,7 @@
         xv = [xs[first + t, j] for t in range(group + keep)]
         for g in range(group):
             terms = [taps[m] * xv[g + keep - m] for m in range(taps_n)]
-            for _ in range(2):
+            for _ in range(1):
                 terms = [a + b for a, b in zip(terms[::2], terms[1::2])]
             wide = [t.astype(jnp.float32) for t in terms]
             while len(wide) > 1:
@@ -261,7 +263,7 @@
         out_shape=shapes,
         scratch_shapes=[pltpu.VMEM((BLOCK + taps_n - 1, pieces, sig, WIDE), jnp.bfloat16)]
         + [pltpu.VMEM((frame_len // LANES, BLOCK * PITCH, LANES), jnp.float32)] * 2,
-        compiler_params=pltpu.CompilerParams(vmem_limit_bytes=50 << 20),
+        compiler_params=pltpu.CompilerParams(vmem_limit_bytes=VMEM),
         cost_estimate=pl.CostEstimate(
             flops=2 * sig * frames * frame_len * (dft.shape[0] + 128 * taps_n),
             bytes_accessed=2 * sig * samp * 2,
@@ -270,72 +272,125 @@
     )(samples, samples, hist, taps, dft)
 
 
-def fine_kernel(low, own_ref, oth_ref, town_ref, toth_ref, cos_ref, sin_ref, *refs):
-    outs, zs = refs[:-1], refs[-1]
+def fill_tables(tables, town_ref, toth_ref, cos_ref, sin_ref, u):
+    fine_local, fine_len, _ = town_ref.shape
+    frames = fine_local * fine_len
+    for side, t_ref in enumerate((town_ref, toth_ref)):
+        for part, turn in enumerate((cos_ref[u], sin_ref[u])):
+            rows = (t_ref[...] * turn).astype(jnp.bfloat16).reshape(frames, LANES)
+            tables[u, side * frames : (side + 1) * frames, part * LANES : (part + 1) * LANES] = rows
+
+
+def fine_kernel(steps, first, own_ref, oth_ref, *refs):
+    if first:
+        makers, outs, table_ref, zs = refs[:4], refs[4:-2], refs[-2], refs[-1]
+    else:
+        table_ref, outs, zs = refs[0], refs[1:-1], refs[-1]
     sig, two_c, frames = own_ref.shape
     size = two_c // 2
-    r = pl.program_id(0)
-    cos, sin = cos_ref[...], sin_ref[...]
-
-    def table(t_ref):
-        t = t_ref[...]
-        return jnp.concatenate(
-            [(t * w).astype(jnp.bfloat16).reshape(frames, LANES) for w in (cos, sin)], axis=1
+    pitch = two_c + 1
+    step = pl.program_id(0)
+    units = table_ref.shape[0] * table_ref.shape[1]
+    span = sig * (two_c + 8)
+    tables = table_ref.reshape(units, 2 * frames, 2 * LANES)
+    for u in range(units):
+        if first:
+            fill_tables(tables, *makers, u)
+        acc = jnp.dot(
+            own_ref[...].reshape(sig * two_c, frames),
+            tables[u, :frames],
+            preferred_element_type=jnp.float32,
+        ) + jnp.dot(
+            oth_ref[...].reshape(sig * two_c, frames),
+            tables[u, frames:],
+            preferred_element_type=jnp.float32,
         )
-
-    acc = jnp.dot(
-        own_ref[...].reshape(sig * two_c, frames), table(town_ref), preferred_element_type=jnp.float32
-    ) + jnp.dot(
-        oth_ref[...].reshape(sig * two_c, frames), table(toth_ref), preferred_element_type=jnp.float32
-    )
-    acc = acc.reshape(sig, 2, size, 2 * LANES)
-    p, q = acc[..., :LANES], acc[..., LANES:]
-    pitch = two_c + 1
-    real, imag = p[:, 0] + q[:, 1], p[:, 1] - q[:, 0]
-    for s in range(sig):
-        zs[pl.ds(s * pitch, size), :] = real[s]
-        zs[pl.ds(s * pitch + size, size), :] = imag[s]
+        acc = acc.reshape(sig, 2, size, 2 * LANES)
+        p, q = acc[..., :LANES], acc[..., LANES:]
+        real, imag = p[:, 0] + q[:, 1], p[:, 1] - q[:, 0]
+        for s in range(sig):
+            zs[pl.ds(u * span + s * pitch, size), :] = real[s]
+            zs[pl.ds(u * span + s * pitch + size, size), :] = imag[s]
     for n, out in enumerate(outs):
 
-        @pl.when(r // low == n)
+        @pl.when(step // steps == n)
         def _(out=out):
-            for c in range(size):
-                for part in range(2):
-                    out[0, c, part] = zs[pl.ds(part * size + c, sig, stride=pitch), :].astype(
-                        jnp.bfloat16
-                    )
-
-
-def fine(own, oth, town, toth, cos, sin, low):
+            for u in range(units):
+                for c in range(size):
+                    for part in range(2):
+                        at = pl.ds(u * span + part * size + c, sig, stride=pitch)
+                        out[u, c, part] = zs[at, :].astype(jnp.bfloat16)
+
+
+def fine(own, oth, tables, turned, makers=None):
     sig, two_c, frames = own.shape
-    dests = cos.shape[0]
+    first = makers is not None
+    if first:
+        dests = makers[2].shape[0]
+        tables = jax.ShapeDtypeStruct((dests // 4, 4, 2 * frames, 2 * LANES), jnp.bfloat16)
+    high, low = tables.shape[:2]
     unit = (two_c // 2, 2, sig, LANES)
-    highs = dests // low
+    if turned:
+        grid, units, count = low, high, 2
+        spec = pl.BlockSpec((high, 1) + tables.shape[2:], lambda t: (0, t % 2 * 2 + t // 2, 0, 0))
+    else:
+        grid, units, count = high, low, high
+        spec = pl.BlockSpec((1, low) + tables.shape[2:], lambda t: (t, 0, 0, 0))
+    steps = grid // count
 
     def place(n):
-        return lambda r: (jnp.clip(r - n * low, 0, low - 1), 0, 0, 0, 0)
-
+        return lambda t: (jnp.clip(t - n * steps, 0, steps - 1), 0, 0, 0, 0)
+
+    whole = pl.BlockSpec(own.shape, lambda t: (0, 0, 0))
+    out_specs = [pl.BlockSpec((units,) + unit, place(n)) for n in range(count)]
+    out_shape = [jax.ShapeDtypeStruct((steps * units,) + unit, jnp.bfloat16) for _ in range(count)]
+    if first:
+        kept = pl.BlockSpec(makers[0].shape, lambda t: (0, 0, 0))
+        turn = pl.BlockSpec((low,) + makers[2].shape[1:], lambda t: (t, 0, 0))
+        in_specs, operands = [whole, whole, kept, kept, turn, turn], (own, oth, *makers)
+        out_specs, out_shape = out_specs + [spec], out_shape + [tables]
+    else:
+        in_specs, operands = [whole, whole, spec], (own, oth, tables)
     return pl.pallas_call(
-        functools.partial(fine_kernel, low),
-        grid=(dests,),
-        in_specs=[
-            pl.BlockSpec(own.shape, lambda r: (0, 0, 0)),
-            pl.BlockSpec(oth.shape, lambda r: (0, 0, 0)),
-            pl.BlockSpec(town.shape, lambda r: (0, 0, 0)),
-            pl.BlockSpec(toth.shape, lambda r: (0, 0, 0)),
-            pl.BlockSpec((1,) + cos.shape[1:], lambda r: (r, 0, 0)),
-            pl.BlockSpec((1,) + sin.shape[1:], lambda r: (r, 0, 0)),
-        ],
-        out_specs=[pl.BlockSpec((1,) + unit, place(n)) for n in range(highs)],
-        out_shape=[jax.ShapeDtypeStruct((low,) + unit, jnp.bfloat16) for _ in range(highs)],
-        scratch_shapes=[pltpu.VMEM((sig * (two_c + 8), LANES), jnp.float32)],
-        compiler_params=pltpu.CompilerParams(vmem_limit_bytes=50 << 20),
+        functools.partial(fine_kernel, steps, first),
+        grid=(grid,),
+        in_specs=in_specs,
+        out_specs=out_specs,
+        out_shape=out_shape,
+        scratch_shapes=[pltpu.VMEM((units * sig * (two_c + 8), LANES), jnp.float32)],
+        compiler_params=pltpu.CompilerParams(vmem_limit_bytes=VMEM),
         cost_estimate=pl.CostEstimate(
-            flops=2 * sig * two_c * 2 * frames * dests * 2 * LANES,
-            bytes_accessed=6 * sig * two_c * frames,
+            flops=2 * sig * two_c * 2 * frames * high * low * 2 * LANES,
+            bytes_accessed=6 * sig * two_c * frames + 8 * high * low * frames * LANES,
             transcendentals=0,
         ),
-    )(own, oth, town, toth, cos, sin)
+    )(*operands)
+
+
+def pack_kernel(*refs):
+    ins, out = refs[:-1], refs[-1]
+    for n, ref in enumerate(ins):
+        out[n] = ref[(0,) * (len(ref.shape) - 4)]
+
+
+def pack(slots):
+    size = slots[0][0].shape[-4]
+    tail = slots[0][0].shape[-3:]
+    half = size // 2
+    return pl.pallas_call(
+        pack_kernel,
+        grid=(2,),
+        in_specs=[
+            pl.BlockSpec((1,) * len(at) + (half,) + tail, lambda c, at=at: at + (c, 0, 0, 0))
+            for _, at in slots
+        ],
+        out_specs=pl.BlockSpec((len(slots), half) + tail, lambda c: (0, c, 0, 0, 0)),
+        out_shape=jax.ShapeDtypeStruct((len(slots), size) + tail, jnp.bfloat16),
+        compiler_params=pltpu.CompilerParams(vmem_limit_bytes=VMEM),
+        cost_estimate=pl.CostEstimate(
+            flops=0, bytes_accessed=4 * len(slots) * size * math.prod(tail), transcendentals=0
+        ),
+    )(*[array for array, _ in slots])
 
 
 def correlate_kernel(sources, scale, per_q, me_ref, *refs):
@@ -343,23 +398,26 @@
     me = me_ref[0]
     for ref, units in zip(ins, sources):
         for at, rel in units:
-            row = pl.multiple_of((me ^ rel) * ROWS, ROWS)
-            xr[pl.ds(row, ROWS), :] = ref[at + (0, 0)]
-            xi[pl.ds(row, ROWS), :] = ref[at + (0, 1)]
-    re, im = xr[...], xi[...]
+            row = pl.ds(pl.multiple_of((me ^ rel) * ROWS, ROWS), ROWS)
+            for c in range(out.shape[0]):
+                xr[c, row, :] = ref[at + (c, 0)]
+                xi[c, row, :] = ref[at + (c, 1)]
     lane = lax.broadcasted_iota(jnp.int32, (1, LANES), 1)
     zero = jnp.zeros((), jnp.bfloat16)
     picks = [lane // per_q == q for q in range(LANES // per_q)]
-    left = jnp.concatenate(
-        [jnp.concatenate([jnp.where(p, re, zero), jnp.where(p, im, zero)], axis=1) for p in picks],
-        axis=0,
-    )
     dims = (((1,), (1,)), ((), ()))
-    for part, right in enumerate((jnp.concatenate([re, im], axis=1), jnp.concatenate([-im, re], axis=1))):
-        vis = lax.dot_general(left, right, dims, preferred_element_type=jnp.float32)
-        vis = (vis * scale).astype(jnp.bfloat16)
-        for q in range(len(picks)):
-            out[0, q, part] = vis[q * re.shape[0] : (q + 1) * re.shape[0]]
+
+    def body(c, _):
+        re, im = xr[c], xi[c]
+        for part in range(2):
+            right = jnp.concatenate([-im, re] if part else [re, im], axis=1)
+            for q, pick in enumerate(picks):
+                left = jnp.concatenate([jnp.where(pick, re, zero), jnp.where(pick, im, zero)], axis=1)
+                vis = lax.dot_general(left, right, dims, preferred_element_type=jnp.float32)
+                out[c, q, part] = (vis * scale).astype(jnp.bfloat16)
+        return 0
+
+    lax.fori_loop(0, out.shape[0], body, 0)
 
 
 def correlate_chunk(me, arrays, leads, sources, whole, offset, shape, per_q, scale):
@@ -369,7 +427,7 @@
     for a, lead in zip(arrays, leads):
         specs.append(
             pl.BlockSpec(
-                tuple(lead) + (1,) + a.shape[-3:],
+                tuple(lead) + (GROUP,) + a.shape[-3:],
                 lambda c, n=len(lead): (0,) * n + (c, 0, 0, 0),
             )
         )
@@ -381,13 +439,13 @@
         operands.append(whole)
     return pl.pallas_call(
         functools.partial(correlate_kernel, sources, scale, per_q),
-        grid=(size,),
+        grid=(size // GROUP,),
         in_specs=specs,
-        out_specs=pl.BlockSpec((1,) + shape[1:], lambda c: (c + offset, 0, 0, 0, 0)),
+        out_specs=pl.BlockSpec((GROUP,) + shape[1:], lambda c: (c + offset // GROUP, 0, 0, 0, 0)),
         out_shape=jax.ShapeDtypeStruct(shape, jnp.bfloat16),
-        scratch_shapes=[pltpu.VMEM((signals, LANES), jnp.bfloat16)] * 2,
+        scratch_shapes=[pltpu.VMEM((GROUP, signals, LANES), jnp.bfloat16)] * 2,
         input_output_aliases=alias,
-        compiler_params=pltpu.CompilerParams(vmem_limit_bytes=40 << 20),
+        compiler_params=pltpu.CompilerParams(vmem_limit_bytes=VMEM),
         cost_estimate=pl.CostEstimate(
             flops=size * 8 * signals * signals * 4 * LANES,
             bytes_accessed=size * 2 * math.prod(shape[1:]),
@@ -398,10 +456,10 @@
 
 def chunk_sizes(channels):
     eighth = channels // 8
-    return [eighth, eighth, 2 * eighth, 2 * eighth, 2 * eighth]
-
-
-DIRECT = 3
+    return [eighth, 2 * eighth, 2 * eighth, 2 * eighth, eighth]
+
+
+DIRECT = 2
 
 
 def per_device(samples, coarse_taps, fine_taps):
@@ -437,48 +495,52 @@
             table = table + jnp.where((late == m)[:, None, :], weights[m][None, :, None], 0.0)
         return table
 
-    def turn_tables(order):
-        fine_of = (me ^ jnp.array(order, jnp.int32))[:, None] * per_dest + (lane // total)[None, :]
-        turns = fine_of[:, None, :] * jnp.arange(fine_len, dtype=jnp.int32)[None, :, None]
-        angles = (turns % fine_len).astype(jnp.float32) * (2.0 * math.pi / fine_len)
-        return jnp.cos(angles), jnp.sin(angles)
-
-    town, toth = taps_table(win), taps_table(1 - win)
-    straight = turn_tables(list(range(dests)))
-    turned = turn_tables([low * z + 2 * y + c for c in range(2) for y in range(2) for z in range(high)])
+    fine_of = (me ^ jnp.arange(dests, dtype=jnp.int32))[:, None] * per_dest + (lane // total)[None, :]
+    turns = fine_of[:, None, :] * jnp.arange(fine_len, dtype=jnp.int32)[None, :, None]
+    angles = (turns % fine_len).astype(jnp.float32) * (2.0 * math.pi / fine_len)
+    makers = (taps_table(win), taps_table(1 - win), jnp.cos(angles), jnp.sin(angles))
 
     shape = (channels, per_dest, 2, sig * dests, sig * dests)
-    result, offset = None, 0
+    highs = range(high)
     oths = [swap(away[k], "win", 1) for k in range(len(chunks))]
-    for k, size in enumerate(chunks):
-        sent = fine(
-            own[k], oths[k], town, toth, *(straight if k < DIRECT else turned), low if k < DIRECT else dests // 2
-        )
-        highs = range(high)
+
+    pieces = []
+    for k in range(len(chunks)):
+        if k == 0:
+            *sent, tables = fine(own[k], oths[k], None, False, makers)
+        else:
+            sent = fine(own[k], oths[k], tables, k >= DIRECT)
         if k < DIRECT:
             held = [sent[0]] + [swap(sent[n], "sta", low * n) for n in highs if n]
-            over = swap(jnp.stack([h[2:] for h in held]), "sta", 2)
-            last = swap(jnp.stack([jnp.stack([h[1] for h in held]), over[:, 1]]), "sta", 1)
+            block = pack([(h, (2 + c,)) for c in range(2) for h in held])
+            over = swap(block, "sta", 2)
+            block = pack([(h, (1,)) for h in held] + [(over, (high + n,)) for n in highs])
+            last = swap(block, "sta", 1)
             arrays = held + [over, last]
-            leads = [(1,)] * high + [(high, 1), (2, high)]
+            leads = [(1,)] * high + [(high,), (2 * high,)]
             sources = [[((0,), low * n)] for n in highs]
-            sources.append([((n, 0), low * n + 2) for n in highs])
-            sources.append([((y, n), low * n + 2 * y + 1) for y in range(2) for n in highs])
+            sources.append([((n,), low * n + 2) for n in highs])
+            sources.append([((y * high + n,), low * n + 2 * y + 1) for y in range(2) for n in highs])
         else:
             near, pair = sent[0], swap(sent[1], "sta", 1)
-            over = swap(jnp.stack([near[high:], pair[high:]]), "sta", 2)
-            arrays, leads = [near, pair, over], [(1,), (1,), (2, 1)]
-            sources = [[((0,), 0)], [((0,), 1)], [((c, 0), 2 + c) for c in range(2)]]
+            block = pack([(a, (high + n,)) for n in highs for a in (near, pair)])
+            over = swap(block, "sta", 2)
+            arrays, leads = [near, pair, over], [(1,), (1,), (2,)]
+            sources = [[((0,), 0)], [((0,), 1)], [((c,), 2 + c) for c in range(2)]]
             for n in highs:
                 if n:
-                    block = jnp.stack([near[n], pair[n], over[0, n], over[1, n]])
+                    slots = [(near, (n,)), (pair, (n,)), (over, (2 * n,)), (over, (2 * n + 1,))]
+                    block = pack(slots)
                     arrays.append(swap(block, "sta", low * n))
                     leads.append((low,))
                     sources.append([((b,), low * n + b) for b in range(low)])
+        pieces.append((arrays, leads, sources))
+    result = None
+    who = me[None].astype(jnp.int32)
+    for k in range(len(chunks)):
         result = correlate_chunk(
-            me[None].astype(jnp.int32), arrays, leads, sources, result, offset, shape, total, 1.0 / total
+            who, *pieces[k], result, sum(chunks[:k]), shape, total, 1.0 / total
         )
-        offset += size
     return result
 
 

time: 386 us -> 419 us (1.085)
  Pallas kernels: 164 us -> 195 us
    pallas_call x5 -> x21, Pallas kernels: 63.6 us -> 90 us  [the longest x5 60.9 us: fine(): pl.pallas_call(functools.partial(fine_kernel, steps, first), grid=(grid,)...]
    pallas_call x1, Pallas kernels: 50.1 us -> 56.8 us  [coarse(): pl.pallas_call(functools.partial(coarse_kernel, chunks, taps_n), grid=(bl...]
  transfers between devices with their start and end apart: 31 -> 31, of which waited for: 11 -> 9; matrix products, arithmetic and copies ran while one was open for 3% -> 3% of each run, Pallas kernels for 27% -> 32%
where the time goes in v1:
time: 419 us; the launch traced here: 413 us
  Pallas kernels  195 us (47%)
  waiting for transfers between devices  132 us (32%)
  starting transfers between devices  70 us (17%)
  other arithmetic  9.69 us (2%)
  local copies, waits for them, and re-layouts  6.9 us (2%)
    ppermute x30, waiting for transfers between devices, swap(): lax.ppermute(x, axis, [(i, i ^ by) for i in range(lax.axis_size(axis))])  132 us
    ppermute x30, starting transfers between devices, swap(): lax.ppermute(x, axis, [(i, i ^ by) for i in range(lax.axis_size(axis))])  65.1 us
    pallas_call x5, Pallas kernels, fine(): pl.pallas_call(functools.partial(fine_kernel, steps, first), grid=(grid,)...  60.9 us
    pallas_call x1, Pallas kernels, coarse(): pl.pallas_call(functools.partial(coarse_kernel, chunks, taps_n), grid=(bl...  56.8 us
    pallas_call x5, Pallas kernels, correlate_chunk(): pl.pallas_call(functools.partial(correlate_kernel, sources, scale, per_q)...  48 us
    pallas_call x16, Pallas kernels, pack(): pl.pallas_call(pack_kernel, grid=(2,), in_specs=[pl.BlockSpec((1,) * len(...  29.1 us
  transfers between devices with their start and end apart: 31, of which 9 were waited for; matrix products, arithmetic and copies ran while one was open for 3% of the time, Pallas kernels for 32%

profile of v1, /device:TPU:0, one launch (start us, length us, event | category | flops | bytes accessed | tf_op | source)
XLA Modules:
  0.0 413.2 jit_solution(6521501252001422274)
XLA Ops:
  0.0 1.0 slice.35
  1.0 4.9 %collective-permute-start = (bf16[16,7680]{1,0:T(8,128)(2,1)S(1)}, bf16[16,7680]{1,0:T(8,128)(2,1)S(1)}, u32[]{:S(2)}, u32[]{:S(2)}) collective-permute-start(bf16[16,7680]{1,0:T(8,128)(2,1)S(1)} %slice.35), channel_id=1, source_target_pairs={{0,16},{1,17},{2,18},{3,19},{4,20},{5,21},{6,22},{7,23},{8,24},{9,... | collective-permute-start | bytes 737288 | tf_op jit(solution)/shard_map/ppermute | solution.py:24
  6.9 3.1 select_convert_fusion.dft_ref
  10.1 0.7 copy.11
  10.8 1.3 select_add_fusion.refs_1_
  12.2 0.8 broadcast_in_dim.230.taps_ref
  13.0 56.8 %shard_map.37 = (bf16[16,16,1024]{2,1,0:T(8,128)(2,1)}, bf16[16,32,1024]{2,1,0:T(8,128)(2,1)}, bf16[16,32,1024]{2,1,0:T(8,128)(2,1)}, bf16[16,32,1024]{2,1,0:T(8...) custom-call(bf16[16,524288]{1,0:T(8,128)(2,1)} %before_ref.1, ...), custom_call_target="tpu_custom_call" | custom-call | flops 38654705664 | bytes 33554432 | tf_op jit(solution)/shard_map/pallas_call | solution.py:249
  69.7 1.4 collective-permute-start.2
  71.9 1.4 select_add_fusion.1.refs_0_
  73.3 2.9 fusion.12
  76.1 1.3 collective-permute-start.1
  78.2 1.3 collective-permute-start.14
  79.5 5.3 %collective-permute-done.2.oth_ref = bf16[16,16,1024]{2,1,0:T(8,128)(2,1)S(1)} collective-permute-done((bf16[16,16,1024]{2,1,0:T(8,128)(2,1)}, bf16[16,16,1024]{2,1,0:T(8,128)(2,1)S(1)}, u32[]{:S(2)}, u32[]{:S(2)}) %collective-permute-start.2) | collective-permute-done | bytes 524320 | tf_op jit(solution)/shard_map/ppermute | solution.py:113
  84.8 0.8 copy-done.8
  85.6 10.1 %shard_map.38 = (bf16[4,8,2,16,128]{4,3,2,1,0:T(8,128)(2,1)}, bf16[4,8,2,16,128]{4,3,2,1,0:T(8,128)(2,1)}, bf16[4,8,2,16,128]{4,3,2,1,0:T(8,128)(2,1)}, bf16[4,8...) custom-call(bf16[16,16,1024]{2,1,0:T(8,128)(2,1)} %get-tuple-element.32.own_ref, bf16[16,16,1024]{2,1,0:T(8,128)(2,1)} %copy-done.8, ...), custom_call_target="tpu_custom_call" | custom-call | flops 4294967296 | bytes 18350080 | tf_op jit(solution)/shard_map/pallas_call | solution.py:354
  95.7 11.7 %collective-permute-done.20.oth_ref = bf16[16,32,1024]{2,1,0:T(8,128)(2,1)} collective-permute-done((bf16[16,32,1024]{2,1,0:T(8,128)(2,1)}, bf16[16,32,1024]{2,1,0:T(8,128)(2,1)}, u32[]{:S(2)}, u32[]{:S(2)}) %collective-permute-start.20) | collective-permute-done | bytes 1048608 | tf_op jit(solution)/shard_map/ppermute | solution.py:113
  107.4 13.9 %shard_map.54 = (bf16[4,16,2,16,128]{4,3,2,1,0:T(8,128)(2,1)}, bf16[4,16,2,16,128]{4,3,2,1,0:T(8,128)(2,1)}, bf16[4,16,2,16,128]{4,3,2,1,0:T(8,128)(2,1)}, bf16[4,16,2,16,128]{4,3,2,1,0:T(8,128)(2,1)}) custom-call(bf16[16,32,1024]{2,1,0:T(8,128)(2,1)} %get-tuple-element.45.own_ref, bf16[16,32,1024]{2,1,0:T(8,128)(2,1)} %collective-permute-done.20.oth_ref, ...), custom_call_target="tpu_custom_call" | custom-call | flops 8589934592 | bytes 19922944 | tf_op jit(solution)/shard_map/pallas_call | solution.py:354
  121.2 1.6 collective-permute-start.21
  122.8 2.6 collective-permute-start.22
  125.4 36.7 %collective-permute-done.14.oth_ref = bf16[16,32,1024]{2,1,0:T(8,128)(2,1)} collective-permute-done((bf16[16,32,1024]{2,1,0:T(8,128)(2,1)}, bf16[16,32,1024]{2,1,0:T(8,128)(2,1)}, u32[]{:S(2)}, u32[]{:S(2)}) %collective-permute-start.14) | collective-permute-done | bytes 1048608 | tf_op jit(solution)/shard_map/ppermute | solution.py:113
  162.1 3.6 collective-permute-start.23
  165.7 13.6 %shard_map.49 = (bf16[8,16,2,16,128]{4,3,2,1,0:T(8,128)(2,1)}, bf16[8,16,2,16,128]{4,3,2,1,0:T(8,128)(2,1)}) custom-call(bf16[16,32,1024]{2,1,0:T(8,128)(2,1)} %get-tuple-element.41.own_ref, bf16[16,32,1024]{2,1,0:T(8,128)(2,1)} %collective-permute-done.14.oth_ref, bf16[4,4,2048,256]{3,2,1,0:T(8,128)(2,1)} %get-tuple-element.34.refs_0_), custom_call_target="tpu_custom_call" | custom-call | flops 8589934592 | bytes 19922944 | tf_op jit(solution)/shard_map/pallas_call | solution.py:354
  179.3 13.8 %shard_map.44 = (bf16[8,16,2,16,128]{4,3,2,1,0:T(8,128)(2,1)}, bf16[8,16,2,16,128]{4,3,2,1,0:T(8,128)(2,1)}) custom-call(bf16[16,32,1024]{2,1,0:T(8,128)(2,1)} %get-tuple-element.37.own_ref, bf16[16,32,1024]{2,1,0:T(8,128)(2,1)} %collective-permute-done.8.oth_ref, bf16[4,4,2048,256]{3,2,1,0:T(8,128)(2,1)} %get-tuple-element.34.refs_0_), custom_call_target="tpu_custom_call" | custom-call | flops 8589934592 | bytes 19922944 | tf_op jit(solution)/shard_map/pallas_call | solution.py:354
  193.9 2.2 shard_map.55
  196.1 1.5 collective-permute-start.24
  197.6 0.8 collective-permute-start.27
  198.4 2.1 shard_map.50
  200.5 3.7 collective-permute-start.28
  204.2 5.8 %collective-permute-done.26.refs_1_.refs_5_ = bf16[4,8,2,16,128]{4,3,2,1,0:T(8,128)(2,1)S(1)} collective-permute-done((bf16[4,8,2,16,128]{4,3,2,1,0:T(8,128)(2,1)}, bf16[4,8,2,16,128]{4,3,2,1,0:T(8,128)(2,1)S(1)}, u32[]{:S(2)}, u32[]{:S(2)}) %collective-permute-start.26) | collective-permute-done | bytes 262176 | tf_op jit(solution)/shard_map/ppermute | solution.py:113
  210.5 9.6 %shard_map.39 = (bf16[8,8,2,16,128]{4,3,2,1,0:T(8,128)(2,1)}, bf16[8,8,2,16,128]{4,3,2,1,0:T(8,128)(2,1)}) custom-call(bf16[16,16,1024]{2,1,0:T(8,128)(2,1)} %get-tuple-element.30.own_ref, bf16[16,16,1024]{2,1,0:T(8,128)(2,1)} %collective-permute-done.1.oth_ref, bf16[4,4,2048,256]{3,2,1,0:T(8,128)(2,1)} %get-tuple-element.34.refs_0_), custom_call_target="tpu_custom_call" | custom-call | flops 4294967296 | bytes 18350080 | tf_op jit(solution)/shard_map/pallas_call | solution.py:354
  220.8 1.7 shard_map.57
  222.5 1.5 collective-permute-start.29
  224.1 2.1 shard_map.45
  226.7 2.1 shard_map.56
  228.8 0.8 copy-done
  229.6 1.7 shard_map.40
  231.3 1.5 collective-permute-start.4
  232.8 23.3 %collective-permute-done.29.refs_4_.refs_5_.refs_6_.refs_7_ = bf16[8,8,2,16,128]{4,3,2,1,0:T(8,128)(2,1)} collective-permute-done((bf16[8,8,2,16,128]{4,3,2,1,0:T(8,128)(2,1)}, bf16[8,8,2,16,128]{4,3,2,1,0:T(8,128)(2,1)}, u32[]{:S(2)}, u32[]{:S(2)}) %collective-permute-start.29) | collective-permute-done | bytes 524320 | tf_op jit(solution)/shard_map/ppermute | solution.py:113
  256.1 1.7 shard_map.58
  257.9 1.8 shard_map.51
  259.7 29.4 %collective-permute-done.4.refs_2_.refs_3_ = bf16[8,8,2,16,128]{4,3,2,1,0:T(8,128)(2,1)S(1)} collective-permute-done((bf16[8,8,2,16,128]{4,3,2,1,0:T(8,128)(2,1)}, bf16[8,8,2,16,128]{4,3,2,1,0:T(8,128)(2,1)S(1)}, u32[]{:S(2)}, u32[]{:S(2)}) %collective-permute-start.4) | collective-permute-done | bytes 524320 | tf_op jit(solution)/shard_map/ppermute | solution.py:113
  289.0 0.8 copy-done.1
  289.8 1.5 shard_map.43
  291.3 1.5 shard_map.42
  292.9 1.5 shard_map.41
  294.4 1.8 shard_map.52
  296.3 1.8 shard_map.53
  298.1 1.9 collective-permute-start.19
  300.0 7.2 %shard_map.59.refs_6_ = bf16[64,4,2,256,256]{4,3,2,1,0:T(8,128)(2,1)} custom-call(s32[1]{0:T(128)} %bitcast.me_ref, bf16[4,8,2,16,128]{4,3,2,1,0:T(8,128)(2,1)} %get-tuple-element.51.refs_0_.refs_4_, bf16[4,8,2,16,128]{4,3,2,1,0:T(8,128)(2,1)} %copy-done.3, bf16[4,8,2,16,128]{4,3,2,1,0:T(8,128)(2,1)} %copy-done.4, ...), custom_call_target="tpu_custom_call" | custom-call | flops 2147483648 | bytes 8388608 | tf_op jit(solution)/shard_map/pallas_call | solution.py:440
  307.1 1.8 shard_map.46
  308.9 1.6 collective-permute-start.11
  310.5 1.8 shard_map.48
  312.3 1.8 shard_map.47
  314.1 0.9 collective-permute-start.12
  315.0 1.9 collective-permute-start.13
  316.9 11.3 %shard_map.60.refs_6_ = bf16[64,4,2,256,256]{4,3,2,1,0:T(8,128)(2,1)} custom-call(s32[1]{0:T(128)} %bitcast.me_ref, bf16[4,16,2,16,128]{4,3,2,1,0:T(8,128)(2,1)} %get-tuple-element.47.refs_0_.refs_4_, bf16[4,16,2,16,128]{4,3,2,1,0:T(8,128)(2,1)} %copy-done.2, ...), custom_call_target="tpu_custom_call", output_to_operand_aliasing={{}: (7, {})} | custom-call | flops 4294967296 | bytes 16777216 | tf_op jit(solution)/shard_map/pallas_call | solution.py:440
  328.2 5.6 %collective-permute-done.18.refs_4_ = bf16[4,16,2,16,128]{4,3,2,1,0:T(8,128)(2,1)S(1)} collective-permute-done((bf16[4,16,2,16,128]{4,3,2,1,0:T(8,128)(2,1)}, bf16[4,16,2,16,128]{4,3,2,1,0:T(8,128)(2,1)S(1)}, u32[]{:S(2)}, u32[]{:S(2)}) %collective-permute-start.18) | collective-permute-done | bytes 524320 | tf_op jit(solution)/shard_map/ppermute | solution.py:113
  333.8 33.5 %collective-permute-start.6 = (bf16[4,8,2,16,128]{4,3,2,1,0:T(8,128)(2,1)}, bf16[4,8,2,16,128]{4,3,2,1,0:T(8,128)(2,1)}, u32[]{:S(2)}, u32[]{:S(2)}) collective-permute-start(bf16[4,8,2,16,128]{4,3,2,1,0:T(8,128)(2,1)} %shard_map.42), channel_id=1, source_target_pairs={{0,8},{1,9},{2,10},{3,11},{4,12},{5,13},{6,14},{7,15},{8,0},{9,1},... | collective-permute-start | bytes 786440 | tf_op jit(solution)/shard_map/ppermute | solution.py:113
  367.3 11.2 %shard_map.61.refs_6_ = bf16[64,4,2,256,256]{4,3,2,1,0:T(8,128)(2,1)} custom-call(s32[1]{0:T(128)} %bitcast.me_ref, bf16[8,16,2,16,128]{4,3,2,1,0:T(8,128)(2,1)} %get-tuple-element.43.refs_0_.refs_2_.refs_4_.refs_6_, bf16[8,16,2,16,128]{4,3,2,1,0:T(8,128)(2,1)} %collective-permute-done.15.refs_1_.refs_3_.refs_5_.refs_7_, ...), custom_call_target="tpu_custom_call", output_to_operand_aliasing={{}: (7, {})} | custom-call | flops 4294967296 | bytes 16777216 | tf_op jit(solution)/shard_map/pallas_call | solution.py:440
  378.5 1.7 collective-permute-start.7
  380.2 8.3 %collective-permute-done.12.refs_4_ = bf16[4,16,2,16,128]{4,3,2,1,0:T(8,128)(2,1)} collective-permute-done((bf16[4,16,2,16,128]{4,3,2,1,0:T(8,128)(2,1)}, bf16[4,16,2,16,128]{4,3,2,1,0:T(8,128)(2,1)}, u32[]{:S(2)}, u32[]{:S(2)}) %collective-permute-start.12) | collective-permute-done | bytes 524320 | tf_op jit(solution)/shard_map/ppermute | solution.py:113
  388.5 11.2 %shard_map.62.refs_6_ = bf16[64,4,2,256,256]{4,3,2,1,0:T(8,128)(2,1)} custom-call(s32[1]{0:T(128)} %bitcast.me_ref, bf16[8,16,2,16,128]{4,3,2,1,0:T(8,128)(2,1)} %get-tuple-element.39.refs_0_.refs_2_.refs_4_.refs_6_, bf16[8,16,2,16,128]{4,3,2,1,0:T(8,128)(2,1)} %collective-permute-done.9.refs_1_.refs_3_.refs_5_.refs_7_, ...), custom_call_target="tpu_custom_call", output_to_operand_aliasing={{}: (7, {})} | custom-call | flops 4294967296 | bytes 16777216 | tf_op jit(solution)/shard_map/pallas_call | solution.py:440
  399.7 5.6 %collective-permute-done.6.refs_4_ = bf16[4,8,2,16,128]{4,3,2,1,0:T(8,128)(2,1)} collective-permute-done((bf16[4,8,2,16,128]{4,3,2,1,0:T(8,128)(2,1)}, bf16[4,8,2,16,128]{4,3,2,1,0:T(8,128)(2,1)}, u32[]{:S(2)}, u32[]{:S(2)}) %collective-permute-start.6) | collective-permute-done | bytes 262176 | tf_op jit(solution)/shard_map/ppermute | solution.py:113
  406.0 7.1 %shard_map.63 = bf16[64,4,2,256,256]{4,3,2,1,0:T(8,128)(2,1)} custom-call(s32[1]{0:T(128)} %bitcast.me_ref, bf16[8,8,2,16,128]{4,3,2,1,0:T(8,128)(2,1)} %get-tuple-element.35.refs_0_.refs_2_.refs_4_.refs_6_, bf16[8,8,2,16,128]{4,3,2,1,0:T(8,128)(2,1)} %copy-done, bf16[8,8,2,16,128]{4,3,2,1,0:T(8,128)(2,1)} %copy-done.1, ...), custom_call_target="tpu_custom_call", output_to_operand_aliasing={{}: (7, {})} | custom-call | flops 2147483648 | bytes 8388608 | tf_op jit(solution)/shard_map/pallas_call | solution.py:440
  (75 shorter events, 5.8 us)
Async XLA Ops:
  1.0 11.2 %collective-permute-start = (bf16[16,7680]{1,0:T(8,128)(2,1)S(1)}, bf16[16,7680]{1,0:T(8,128)(2,1)S(1)}, u32[]{:S(2)}, u32[]{:S(2)}) collective-permute-start(bf16[16,7680]{1,0:T(8,128)(2,1)S(1)} %slice.35), channel_id=1, source_target_pairs={{0,16},{1,17},{2,18},{3,19},{4,20},{5,21},{6,22},{7,23},{8,24},{9,... | collective-permute-start | bytes 737288 | tf_op jit(solution)/shard_map/ppermute | solution.py:24
  12.2 0.8 copy-start.10
  69.7 15.1 %collective-permute-start.2 = (bf16[16,16,1024]{2,1,0:T(8,128)(2,1)}, bf16[16,16,1024]{2,1,0:T(8,128)(2,1)S(1)}, u32[]{:S(2)}, u32[]{:S(2)}) collective-permute-start(bf16[16,16,1024]{2,1,0:T(8,128)(2,1)} %get-tuple-element.33), channel_id=1, source_target_pairs={{0,16},{16,0},{1,17},{17,1},{2,18},{18,2},{3,19},{19,3},{4,20},{20... | collective-permute-start | bytes 1572872 | tf_op jit(solution)/shard_map/ppermute | solution.py:113
  71.1 36.2 %collective-permute-start.20 = (bf16[16,32,1024]{2,1,0:T(8,128)(2,1)}, bf16[16,32,1024]{2,1,0:T(8,128)(2,1)}, u32[]{:S(2)}, u32[]{:S(2)}) collective-permute-start(bf16[16,32,1024]{2,1,0:T(8,128)(2,1)} %get-tuple-element.46), channel_id=1, source_target_pairs={{0,16},{16,0},{1,17},{17,1},{2,18},{18,2},{3,19},{19,3},{4,20},{20... | collective-permute-start | bytes 3145736 | tf_op jit(solution)/shard_map/ppermute | solution.py:113
  76.1 124.3 %collective-permute-start.1 = (bf16[16,16,1024]{2,1,0:T(8,128)(2,1)}, bf16[16,16,1024]{2,1,0:T(8,128)(2,1)}, u32[]{:S(2)}, u32[]{:S(2)}) collective-permute-start(bf16[16,16,1024]{2,1,0:T(8,128)(2,1)} %get-tuple-element.31), channel_id=1, source_target_pairs={{0,16},{16,0},{1,17},{17,1},{2,18},{18,2},{3,19},{19,3},{4,20},{20... | collective-permute-start | bytes 1572872 | tf_op jit(solution)/shard_map/ppermute | solution.py:113
  77.5 101.8 %collective-permute-start.8 = (bf16[16,32,1024]{2,1,0:T(8,128)(2,1)}, bf16[16,32,1024]{2,1,0:T(8,128)(2,1)}, u32[]{:S(2)}, u32[]{:S(2)}) collective-permute-start(bf16[16,32,1024]{2,1,0:T(8,128)(2,1)} %get-tuple-element.38), channel_id=1, source_target_pairs={{0,16},{16,0},{1,17},{17,1},{2,18},{18,2},{3,19},{19,3},{4,20},{20... | collective-permute-start | bytes 3145736 | tf_op jit(solution)/shard_map/ppermute | solution.py:113
  78.2 84.0 %collective-permute-start.14 = (bf16[16,32,1024]{2,1,0:T(8,128)(2,1)}, bf16[16,32,1024]{2,1,0:T(8,128)(2,1)}, u32[]{:S(2)}, u32[]{:S(2)}) collective-permute-start(bf16[16,32,1024]{2,1,0:T(8,128)(2,1)} %get-tuple-element.42), channel_id=1, source_target_pairs={{0,16},{16,0},{1,17},{17,1},{2,18},{18,2},{3,19},{19,3},{4,20},{20... | collective-permute-start | bytes 3145736 | tf_op jit(solution)/shard_map/ppermute | solution.py:113
  84.8 0.8 copy-start.8
  95.7 101.9 %copy-start.9 = (bf16[4,8,2,16,128]{4,3,2,1,0:T(8,128)(2,1)S(1)}, bf16[4,8,2,16,128]{4,3,2,1,0:T(8,128)(2,1)}, u32[]{:S(2)}) copy-start(bf16[4,8,2,16,128]{4,3,2,1,0:T(8,128)(2,1)} %get-tuple-element.53) | copy-start | bytes 786436
  121.2 71.9 %collective-permute-start.21 = (bf16[4,16,2,16,128]{4,3,2,1,0:T(8,128)(2,1)}, bf16[4,16,2,16,128]{4,3,2,1,0:T(8,128)(2,1)S(1)}, u32[]{:S(2)}, u32[]{:S(2)}) collective-permute-start(bf16[4,16,2,16,128]{4,3,2,1,0:T(8,128)(2,1)} %get-tuple-element.48), channel_id=1, source_target_pairs={{0,4},{1,5},{2,6},{3,7},{4,0},{5,1},{6,2},{7,3},{8,12},{9,13},{10,... | collective-permute-start | bytes 1572872 | tf_op jit(solution)/shard_map/ppermute | solution.py:113
  122.8 70.6 %collective-permute-start.22 = (bf16[4,16,2,16,128]{4,3,2,1,0:T(8,128)(2,1)}, bf16[4,16,2,16,128]{4,3,2,1,0:T(8,128)(2,1)}, u32[]{:S(2)}, u32[]{:S(2)}) collective-permute-start(bf16[4,16,2,16,128]{4,3,2,1,0:T(8,128)(2,1)} %get-tuple-element.49), channel_id=1, source_target_pairs={{0,8},{1,9},{2,10},{3,11},{4,12},{5,13},{6,14},{7,15},{8,0},{9,1},... | collective-permute-start | bytes 1572872 | tf_op jit(solution)/shard_map/ppermute | solution.py:113
  162.1 31.3 %collective-permute-start.23 = (bf16[4,16,2,16,128]{4,3,2,1,0:T(8,128)(2,1)}, bf16[4,16,2,16,128]{4,3,2,1,0:T(8,128)(2,1)}, u32[]{:S(2)}, u32[]{:S(2)}) collective-permute-start(bf16[4,16,2,16,128]{4,3,2,1,0:T(8,128)(2,1)} %get-tuple-element.50), channel_id=1, source_target_pairs={{0,12},{1,13},{2,14},{3,15},{4,8},{5,9},{6,10},{7,11},{8,4},{9,5},... | collective-permute-start | bytes 1572872 | tf_op jit(solution)/shard_map/ppermute | solution.py:113
  179.3 18.3 %collective-permute-start.15 = (bf16[8,16,2,16,128]{4,3,2,1,0:T(8,128)(2,1)}, bf16[8,16,2,16,128]{4,3,2,1,0:T(8,128)(2,1)}, u32[]{:S(2)}, u32[]{:S(2)}) collective-permute-start(bf16[8,16,2,16,128]{4,3,2,1,0:T(8,128)(2,1)} %get-tuple-element.44), channel_id=1, source_target_pairs={{0,1},{1,0},{2,3},{3,2},{4,5},{5,4},{6,7},{7,6},{8,9},{9,8},{10,11... | collective-permute-start | bytes 3145736 | tf_op jit(solution)/shard_map/ppermute | solution.py:113
  193.1 0.8 copy-start.2
  193.1 31.0 %collective-permute-start.9 = (bf16[8,16,2,16,128]{4,3,2,1,0:T(8,128)(2,1)}, bf16[8,16,2,16,128]{4,3,2,1,0:T(8,128)(2,1)}, u32[]{:S(2)}, u32[]{:S(2)}) collective-permute-start(bf16[8,16,2,16,128]{4,3,2,1,0:T(8,128)(2,1)} %get-tuple-element.40), channel_id=1, source_target_pairs={{0,1},{1,0},{2,3},{3,2},{4,5},{5,4},{6,7},{7,6},{8,9},{9,8},{10,11... | collective-permute-start | bytes 3145736 | tf_op jit(solution)/shard_map/ppermute | solution.py:113
  196.1 30.6 %collective-permute-start.24 = (bf16[8,16,2,16,128]{4,3,2,1,0:T(8,128)(2,1)}, bf16[8,16,2,16,128]{4,3,2,1,0:T(8,128)(2,1)}, u32[]{:S(2)}, u32[]{:S(2)}) collective-permute-start(bf16[8,16,2,16,128]{4,3,2,1,0:T(8,128)(2,1)} %shard_map.55), channel_id=1, source_target_pairs={{0,2},{1,3},{2,0},{3,1},{4,6},{5,7},{6,4},{7,5},{8,10},{9,11},{10,... | collective-permute-start | bytes 3145736 | tf_op jit(solution)/shard_map/ppermute | solution.py:113
  197.6 12.3 %collective-permute-start.26 = (bf16[4,8,2,16,128]{4,3,2,1,0:T(8,128)(2,1)}, bf16[4,8,2,16,128]{4,3,2,1,0:T(8,128)(2,1)S(1)}, u32[]{:S(2)}, u32[]{:S(2)}) collective-permute-start(bf16[4,8,2,16,128]{4,3,2,1,0:T(8,128)(2,1)} %get-tuple-element.52), channel_id=1, source_target_pairs={{0,4},{1,5},{2,6},{3,7},{4,0},{5,1},{6,2},{7,3},{8,12},{9,13},{10,... | collective-permute-start | bytes 786440 | tf_op jit(solution)/shard_map/ppermute | solution.py:113
  197.6 22.5 %collective-permute-start.27 = (bf16[4,8,2,16,128]{4,3,2,1,0:T(8,128)(2,1)S(1)}, bf16[4,8,2,16,128]{4,3,2,1,0:T(8,128)(2,1)S(1)}, u32[]{:S(2)}, u32[]{:S(2)}) collective-permute-start(bf16[4,8,2,16,128]{4,3,2,1,0:T(8,128)(2,1)S(1)} %copy-done.9), channel_id=1, source_target_pairs={{0,8},{1,9},{2,10},{3,11},{4,12},{5,13},{6,14},{7,15},{8,0},{9,1},... | collective-permute-start | bytes 786440 | tf_op jit(solution)/shard_map/ppermute | solution.py:113
  200.5 20.3 %collective-permute-start.28 = (bf16[4,8,2,16,128]{4,3,2,1,0:T(8,128)(2,1)}, bf16[4,8,2,16,128]{4,3,2,1,0:T(8,128)(2,1)}, u32[]{:S(2)}, u32[]{:S(2)}) collective-permute-start(bf16[4,8,2,16,128]{4,3,2,1,0:T(8,128)(2,1)} %get-tuple-element.54), channel_id=1, source_target_pairs={{0,12},{1,13},{2,14},{3,15},{4,8},{5,9},{6,10},{7,11},{8,4},{9,5},... | collective-permute-start | bytes 786440 | tf_op jit(solution)/shard_map/ppermute | solution.py:113
  209.9 10.8 %copy-start.3 = (bf16[4,8,2,16,128]{4,3,2,1,0:T(8,128)(2,1)}, bf16[4,8,2,16,128]{4,3,2,1,0:T(8,128)(2,1)S(1)}, u32[]{:S(2)}) copy-start(bf16[4,8,2,16,128]{4,3,2,1,0:T(8,128)(2,1)S(1)} %collective-permute-done.26.refs_1_.refs_5_) | copy-start | bytes 786436
  209.9 47.9 %collective-permute-start.16 = (bf16[8,16,2,16,128]{4,3,2,1,0:T(8,128)(2,1)}, bf16[8,16,2,16,128]{4,3,2,1,0:T(8,128)(2,1)}, u32[]{:S(2)}, u32[]{:S(2)}) collective-permute-start(bf16[8,16,2,16,128]{4,3,2,1,0:T(8,128)(2,1)} %shard_map.50), channel_id=1, source_target_pairs={{0,2},{1,3},{2,0},{3,1},{4,6},{5,7},{6,4},{7,5},{8,10},{9,11},{10,... | collective-permute-start | bytes 3145736 | tf_op jit(solution)/shard_map/ppermute | solution.py:113
  220.1 0.7 copy-start.4
  220.8 8.0 %collective-permute-start.3 = (bf16[8,8,2,16,128]{4,3,2,1,0:T(8,128)(2,1)}, bf16[8,8,2,16,128]{4,3,2,1,0:T(8,128)(2,1)S(1)}, u32[]{:S(2)}, u32[]{:S(2)}) collective-permute-start(bf16[8,8,2,16,128]{4,3,2,1,0:T(8,128)(2,1)} %get-tuple-element.36), channel_id=1, source_target_pairs={{0,1},{1,0},{2,3},{3,2},{4,5},{5,4},{6,7},{7,6},{8,9},{9,8},{10,11... | collective-permute-start | bytes 1572872 | tf_op jit(solution)/shard_map/ppermute | solution.py:113
  222.5 33.6 %collective-permute-start.29 = (bf16[8,8,2,16,128]{4,3,2,1,0:T(8,128)(2,1)}, bf16[8,8,2,16,128]{4,3,2,1,0:T(8,128)(2,1)}, u32[]{:S(2)}, u32[]{:S(2)}) collective-permute-start(bf16[8,8,2,16,128]{4,3,2,1,0:T(8,128)(2,1)} %shard_map.57), channel_id=1, source_target_pairs={{0,2},{1,3},{2,0},{3,1},{4,6},{5,7},{6,4},{7,5},{8,10},{9,11},{10,... | collective-permute-start | bytes 1572872 | tf_op jit(solution)/shard_map/ppermute | solution.py:113
  226.2 81.0 %collective-permute-start.10 = (bf16[8,16,2,16,128]{4,3,2,1,0:T(8,128)(2,1)}, bf16[8,16,2,16,128]{4,3,2,1,0:T(8,128)(2,1)}, u32[]{:S(2)}, u32[]{:S(2)}) collective-permute-start(bf16[8,16,2,16,128]{4,3,2,1,0:T(8,128)(2,1)} %shard_map.45), channel_id=1, source_target_pairs={{0,2},{1,3},{2,0},{3,1},{4,6},{5,7},{6,4},{7,5},{8,10},{9,11},{10,... | collective-permute-start | bytes 3145736 | tf_op jit(solution)/shard_map/ppermute | solution.py:113
  228.8 85.3 %collective-permute-start.25 = (bf16[8,16,2,16,128]{4,3,2,1,0:T(8,128)(2,1)}, bf16[8,16,2,16,128]{4,3,2,1,0:T(8,128)(2,1)}, u32[]{:S(2)}, u32[]{:S(2)}) collective-permute-start(bf16[8,16,2,16,128]{4,3,2,1,0:T(8,128)(2,1)} %shard_map.56), channel_id=1, source_target_pairs={{0,1},{1,0},{2,3},{3,2},{4,5},{5,4},{6,7},{7,6},{8,9},{9,8},{10,11... | collective-permute-start | bytes 3145736 | tf_op jit(solution)/shard_map/ppermute | solution.py:113
  228.8 0.8 copy-start
  231.3 57.7 %collective-permute-start.4 = (bf16[8,8,2,16,128]{4,3,2,1,0:T(8,128)(2,1)}, bf16[8,8,2,16,128]{4,3,2,1,0:T(8,128)(2,1)S(1)}, u32[]{:S(2)}, u32[]{:S(2)}) collective-permute-start(bf16[8,8,2,16,128]{4,3,2,1,0:T(8,128)(2,1)} %shard_map.40), channel_id=1, source_target_pairs={{0,2},{1,3},{2,0},{3,1},{4,6},{5,7},{6,4},{7,5},{8,10},{9,11},{10,... | collective-permute-start | bytes 1572872 | tf_op jit(solution)/shard_map/ppermute | solution.py:113
  257.8 40.2 %collective-permute-start.30 = (bf16[8,8,2,16,128]{4,3,2,1,0:T(8,128)(2,1)}, bf16[8,8,2,16,128]{4,3,2,1,0:T(8,128)(2,1)}, u32[]{:S(2)}, u32[]{:S(2)}) collective-permute-start(bf16[8,8,2,16,128]{4,3,2,1,0:T(8,128)(2,1)} %shard_map.58), channel_id=1, source_target_pairs={{0,1},{1,0},{2,3},{3,2},{4,5},{5,4},{6,7},{7,6},{8,9},{9,8},{10,11... | collective-permute-start | bytes 1572872 | tf_op jit(solution)/shard_map/ppermute | solution.py:113
  259.7 55.3 %collective-permute-start.17 = (bf16[4,16,2,16,128]{4,3,2,1,0:T(8,128)(2,1)}, bf16[4,16,2,16,128]{4,3,2,1,0:T(8,128)(2,1)}, u32[]{:S(2)}, u32[]{:S(2)}) collective-permute-start(bf16[4,16,2,16,128]{4,3,2,1,0:T(8,128)(2,1)} %shard_map.51), channel_id=1, source_target_pairs={{0,4},{1,5},{2,6},{3,7},{4,0},{5,1},{6,2},{7,3},{8,12},{9,13},{10,... | collective-permute-start | bytes 1572872 | tf_op jit(solution)/shard_map/ppermute | solution.py:113
  289.0 0.8 copy-start.1
  296.3 37.5 %collective-permute-start.18 = (bf16[4,16,2,16,128]{4,3,2,1,0:T(8,128)(2,1)}, bf16[4,16,2,16,128]{4,3,2,1,0:T(8,128)(2,1)S(1)}, u32[]{:S(2)}, u32[]{:S(2)}) collective-permute-start(bf16[4,16,2,16,128]{4,3,2,1,0:T(8,128)(2,1)} %shard_map.52), channel_id=1, source_target_pairs={{0,8},{1,9},{2,10},{3,11},{4,12},{5,13},{6,14},{7,15},{8,0},{9,1},... | collective-permute-start | bytes 1572872 | tf_op jit(solution)/shard_map/ppermute | solution.py:113
  298.1 35.7 %collective-permute-start.19 = (bf16[4,16,2,16,128]{4,3,2,1,0:T(8,128)(2,1)}, bf16[4,16,2,16,128]{4,3,2,1,0:T(8,128)(2,1)}, u32[]{:S(2)}, u32[]{:S(2)}) collective-permute-start(bf16[4,16,2,16,128]{4,3,2,1,0:T(8,128)(2,1)} %shard_map.53), channel_id=1, source_target_pairs={{0,12},{1,13},{2,14},{3,15},{4,8},{5,9},{6,10},{7,11},{8,4},{9,5},... | collective-permute-start | bytes 1572872 | tf_op jit(solution)/shard_map/ppermute | solution.py:113
  308.9 69.6 %collective-permute-start.11 = (bf16[4,16,2,16,128]{4,3,2,1,0:T(8,128)(2,1)}, bf16[4,16,2,16,128]{4,3,2,1,0:T(8,128)(2,1)}, u32[]{:S(2)}, u32[]{:S(2)}) collective-permute-start(bf16[4,16,2,16,128]{4,3,2,1,0:T(8,128)(2,1)} %shard_map.46), channel_id=1, source_target_pairs={{0,4},{1,5},{2,6},{3,7},{4,0},{5,1},{6,2},{7,3},{8,12},{9,13},{10,... | collective-permute-start | bytes 1572872 | tf_op jit(solution)/shard_map/ppermute | solution.py:113
  314.1 74.4 %collective-permute-start.12 = (bf16[4,16,2,16,128]{4,3,2,1,0:T(8,128)(2,1)}, bf16[4,16,2,16,128]{4,3,2,1,0:T(8,128)(2,1)}, u32[]{:S(2)}, u32[]{:S(2)}) collective-permute-start(bf16[4,16,2,16,128]{4,3,2,1,0:T(8,128)(2,1)} %shard_map.47), channel_id=1, source_target_pairs={{0,8},{1,9},{2,10},{3,11},{4,12},{5,13},{6,14},{7,15},{8,0},{9,1},... | collective-permute-start | bytes 1572872 | tf_op jit(solution)/shard_map/ppermute | solution.py:113
  315.0 73.5 %collective-permute-start.13 = (bf16[4,16,2,16,128]{4,3,2,1,0:T(8,128)(2,1)}, bf16[4,16,2,16,128]{4,3,2,1,0:T(8,128)(2,1)}, u32[]{:S(2)}, u32[]{:S(2)}) collective-permute-start(bf16[4,16,2,16,128]{4,3,2,1,0:T(8,128)(2,1)} %shard_map.48), channel_id=1, source_target_pairs={{0,12},{1,13},{2,14},{3,15},{4,8},{5,9},{6,10},{7,11},{8,4},{9,5},... | collective-permute-start | bytes 1572872 | tf_op jit(solution)/shard_map/ppermute | solution.py:113
  333.8 33.5 %copy-start.5 = (bf16[4,16,2,16,128]{4,3,2,1,0:T(8,128)(2,1)}, bf16[4,16,2,16,128]{4,3,2,1,0:T(8,128)(2,1)S(1)}, u32[]{:S(2)}) copy-start(bf16[4,16,2,16,128]{4,3,2,1,0:T(8,128)(2,1)S(1)} %collective-permute-done.18.refs_4_) | copy-start | bytes 1572868
  333.8 65.9 %collective-permute-start.5 = (bf16[4,8,2,16,128]{4,3,2,1,0:T(8,128)(2,1)}, bf16[4,8,2,16,128]{4,3,2,1,0:T(8,128)(2,1)S(1)}, u32[]{:S(2)}, u32[]{:S(2)}) collective-permute-start(bf16[4,8,2,16,128]{4,3,2,1,0:T(8,128)(2,1)} %shard_map.41), channel_id=1, source_target_pairs={{0,4},{1,5},{2,6},{3,7},{4,0},{5,1},{6,2},{7,3},{8,12},{9,13},{10,... | collective-permute-start | bytes 786440 | tf_op jit(solution)/shard_map/ppermute | solution.py:113
  333.8 71.6 %collective-permute-start.6 = (bf16[4,8,2,16,128]{4,3,2,1,0:T(8,128)(2,1)}, bf16[4,8,2,16,128]{4,3,2,1,0:T(8,128)(2,1)}, u32[]{:S(2)}, u32[]{:S(2)}) collective-permute-start(bf16[4,8,2,16,128]{4,3,2,1,0:T(8,128)(2,1)} %shard_map.42), channel_id=1, source_target_pairs={{0,8},{1,9},{2,10},{3,11},{4,12},{5,13},{6,14},{7,15},{8,0},{9,1},... | collective-permute-start | bytes 786440 | tf_op jit(solution)/shard_map/ppermute | solution.py:113
  378.5 26.8 %collective-permute-start.7 = (bf16[4,8,2,16,128]{4,3,2,1,0:T(8,128)(2,1)}, bf16[4,8,2,16,128]{4,3,2,1,0:T(8,128)(2,1)S(1)}, u32[]{:S(2)}, u32[]{:S(2)}) collective-permute-start(bf16[4,8,2,16,128]{4,3,2,1,0:T(8,128)(2,1)} %shard_map.43), channel_id=1, source_target_pairs={{0,12},{1,13},{2,14},{3,15},{4,8},{5,9},{6,10},{7,11},{8,4},{9,5},... | collective-permute-start | bytes 786440 | tf_op jit(solution)/shard_map/ppermute | solution.py:113
  399.7 5.6 %copy-start.6 = (bf16[4,8,2,16,128]{4,3,2,1,0:T(8,128)(2,1)}, bf16[4,8,2,16,128]{4,3,2,1,0:T(8,128)(2,1)S(1)}, u32[]{:S(2)}) copy-start(bf16[4,8,2,16,128]{4,3,2,1,0:T(8,128)(2,1)S(1)} %collective-permute-done.5.refs_3_) | copy-start | bytes 786436
  405.3 0.7 copy-start.7

commit v2 on v1

--- a/solution.py
+++ b/solution.py
@@ -3,6 +3,7 @@
 
 import jax
 import jax.numpy as jnp
+import numpy as np
 from jax import lax
 from jax.experimental import pallas as pl
 from jax.experimental.pallas import tpu as pltpu
@@ -114,23 +115,21 @@
 
 
 def coarse_rows(frame_len, band_half, chunks):
-    half = lax.axis_index("win")
     rows = []
     for h in range(2):
-        base = 0
+        base = frame_len // 8 + h * band_half
         for size in chunks:
-            for part in range(2):
-                channel = (half ^ h) * band_half + base + jnp.arange(size, dtype=jnp.int32)
-                rows.append(channel * 2 + part)
+            channel = np.arange(base, base + size, dtype=np.int32)
+            products = channel[:, None] * np.arange(frame_len, dtype=np.int32)[None, :]
+            angles = (products % frame_len).astype(np.float32) * np.float32(2.0 * math.pi / frame_len)
+            rows += [np.cos(angles), -np.sin(angles)]
             base += size
-    code = jnp.concatenate(rows)
-    channel = frame_len // 8 + code // 2
-    products = channel[:, None] * jnp.arange(frame_len, dtype=jnp.int32)[None, :]
-    angles = (products % frame_len).astype(jnp.float32) * (2.0 * math.pi / frame_len)
-    return jnp.where((code % 2 == 0)[:, None], jnp.cos(angles), -jnp.sin(angles)).astype(jnp.bfloat16)
-
-
-def coarse_kernel(chunks, taps_n, x_ref, before_ref, hist_ref, taps_ref, dft_ref, *refs):
+    return np.concatenate(rows).reshape(2, 2 * band_half, frame_len).astype(jnp.bfloat16)
+
+
+def coarse_kernel(chunks, taps_n, win_ref, x_ref, before_ref, taps_ref, dft_ref, *refs):
+    opening = len(refs) > 3 + 2 * len(chunks)
+    hist_ref, refs = (refs[0], refs[1:]) if opening else (None, refs)
     outs, (xs, even, odd) = refs[:-3], refs[-3:]
     step, last = pl.program_id(0), pl.num_programs(0) - 1
     keep = taps_n - 1
@@ -139,19 +138,17 @@
     group = 8
 
     def load():
-        @pl.when(step == 0)
-        def _():
+        def put(ref, gap):
             for f in range(keep):
                 for j in range(pieces):
-                    at = (f * pieces + j) * WIDE
-                    xs[f, j] = hist_ref[:, at : at + WIDE]
-
-        @pl.when(step > 0)
-        def _():
-            for f in range(keep):
-                for j in range(pieces):
-                    at = ((f + skip) * pieces + j) * WIDE
-                    xs[f, j] = before_ref[:, at : at + WIDE]
+                    at = ((f + gap) * pieces + j) * WIDE
+                    xs[f, j] = ref[:, at : at + WIDE]
+
+        if opening:
+            pl.when(step == 0)(lambda: put(hist_ref, 0))
+            pl.when(step > 0)(lambda: put(before_ref, skip))
+        else:
+            put(before_ref, skip)
 
         def move(f, _):
             for j in range(pieces):
@@ -166,7 +163,7 @@
         xv = [xs[first + t, j] for t in range(group + keep)]
         for g in range(group):
             terms = [taps[m] * xv[g + keep - m] for m in range(taps_n)]
-            for _ in range(1):
+            for _ in range(2):
                 terms = [a + b for a, b in zip(terms[::2], terms[1::2])]
             wide = [t.astype(jnp.float32) for t in terms]
             while len(wide) > 1:
@@ -181,8 +178,10 @@
             parts = [wd[j, pl.ds(2 * p + t, BLOCK, stride=PITCH), :] for j in range(wd.shape[0])]
             rows.append(jnp.concatenate(parts, axis=1).astype(jnp.bfloat16))
         both = jnp.concatenate(rows, axis=0)
+        mine = win_ref[0]
+        matrix = jnp.concatenate([dft_ref[mine], dft_ref[1 - mine]], axis=0)
         res = lax.dot_general(
-            dft_ref[...], both, (((1,), (1,)), ((), ())), preferred_element_type=jnp.float32
+            matrix, both, (((1,), (1,)), ((), ())), preferred_element_type=jnp.float32
         ).astype(jnp.bfloat16)
         for t in range(2):
             base = 0
@@ -229,33 +228,33 @@
         run(None, odd)
 
 
-def coarse(samples, hist, coarse_taps, dft, chunks):
-    sig, samp = samples.shape
+def coarse(win, samples, hist, coarse_taps, dft, chunks, start, blocks):
+    sig, _ = samples.shape
     taps_n, frame_len = coarse_taps.shape
     pieces = frame_len // WIDE
-    frames = samp // frame_len
+    frames = blocks * BLOCK
     before = taps_n
     taps = jnp.broadcast_to(
         coarse_taps.reshape(taps_n, pieces, WIDE).transpose(1, 0, 2)[:, :, None],
         (pieces, taps_n, ROWS, WIDE),
     )
     ratio = BLOCK // before
-    blocks = frames // BLOCK
     shapes = [jax.ShapeDtypeStruct((sig, 2 * c, frames), jnp.bfloat16) for c in chunks * 2]
 
     def at(i):
-        return jnp.minimum(i, blocks - 1)
+        return start + jnp.minimum(i, blocks - 1)
 
     return pl.pallas_call(
         functools.partial(coarse_kernel, chunks, taps_n),
         grid=(blocks + 1,),
         in_specs=[
+            pl.BlockSpec(memory_space=pltpu.SMEM),
             pl.BlockSpec((sig, BLOCK * frame_len), lambda i: (0, at(i))),
             pl.BlockSpec((sig, before * frame_len), lambda i: (0, jnp.maximum(at(i) * ratio - 1, 0))),
-            pl.BlockSpec(hist.shape, lambda i: (0, 0)),
             pl.BlockSpec(taps.shape, lambda i: (0, 0, 0, 0)),
-            pl.BlockSpec(dft.shape, lambda i: (0, 0)),
-        ],
+            pl.BlockSpec(dft.shape, lambda i: (0, 0, 0)),
+        ]
+        + [pl.BlockSpec(h.shape, lambda i: (0, 0)) for h in hist],
         out_specs=[
             pl.BlockSpec((sig, 2 * c, BLOCK), lambda i: (0, 0, jnp.maximum(i - 1, 0)))
             for c in chunks * 2
@@ -265,11 +264,11 @@
         + [pltpu.VMEM((frame_len // LANES, BLOCK * PITCH, LANES), jnp.float32)] * 2,
         compiler_params=pltpu.CompilerParams(vmem_limit_bytes=VMEM),
         cost_estimate=pl.CostEstimate(
-            flops=2 * sig * frames * frame_len * (dft.shape[0] + 128 * taps_n),
-            bytes_accessed=2 * sig * samp * 2,
+            flops=2 * sig * frames * frame_len * (dft.shape[0] * dft.shape[1] + 128 * taps_n),
+            bytes_accessed=4 * sig * frames * frame_len,
             transcendentals=0,
         ),
-    )(samples, samples, hist, taps, dft)
+    )(win, samples, samples, taps, dft, *hist)
 
 
 def fill_tables(tables, town_ref, toth_ref, cos_ref, sin_ref, u):
@@ -281,30 +280,30 @@
             tables[u, side * frames : (side + 1) * frames, part * LANES : (part + 1) * LANES] = rows
 
 
-def fine_kernel(steps, first, own_ref, oth_ref, *refs):
+def fine_kernel(steps, first, count, *refs):
+    parts, refs = refs[:count], refs[count:]
     if first:
         makers, outs, table_ref, zs = refs[:4], refs[4:-2], refs[-2], refs[-1]
     else:
         table_ref, outs, zs = refs[0], refs[1:-1], refs[-1]
-    sig, two_c, frames = own_ref.shape
+    sig, two_c, frames = parts[0].shape
     size = two_c // 2
     pitch = two_c + 1
     step = pl.program_id(0)
     units = table_ref.shape[0] * table_ref.shape[1]
     span = sig * (two_c + 8)
-    tables = table_ref.reshape(units, 2 * frames, 2 * LANES)
+    tables = table_ref.reshape(units, count * frames, 2 * LANES)
     for u in range(units):
         if first:
             fill_tables(tables, *makers, u)
-        acc = jnp.dot(
-            own_ref[...].reshape(sig * two_c, frames),
-            tables[u, :frames],
-            preferred_element_type=jnp.float32,
-        ) + jnp.dot(
-            oth_ref[...].reshape(sig * two_c, frames),
-            tables[u, frames:],
-            preferred_element_type=jnp.float32,
-        )
+        acc = None
+        for n, part in enumerate(parts):
+            term = jnp.dot(
+                part[...].reshape(sig * two_c, frames),
+                tables[u, n * frames : (n + 1) * frames],
+                preferred_element_type=jnp.float32,
+            )
+            acc = term if acc is None else acc + term
         acc = acc.reshape(sig, 2, size, 2 * LANES)
         p, q = acc[..., :LANES], acc[..., LANES:]
         real, imag = p[:, 0] + q[:, 1], p[:, 1] - q[:, 0]
@@ -322,12 +321,13 @@
                         out[u, c, part] = zs[at, :].astype(jnp.bfloat16)
 
 
-def fine(own, oth, tables, turned, makers=None):
-    sig, two_c, frames = own.shape
+def fine(parts, tables, turned, makers=None):
+    sig, two_c, span = parts[0].shape
+    frames = span * len(parts)
     first = makers is not None
     if first:
         dests = makers[2].shape[0]
-        tables = jax.ShapeDtypeStruct((dests // 4, 4, 2 * frames, 2 * LANES), jnp.bfloat16)
+        tables = jax.ShapeDtypeStruct((dests // 4, 4, frames, 2 * LANES), jnp.bfloat16)
     high, low = tables.shape[:2]
     unit = (two_c // 2, 2, sig, LANES)
     if turned:
@@ -341,18 +341,18 @@
     def place(n):
         return lambda t: (jnp.clip(t - n * steps, 0, steps - 1), 0, 0, 0, 0)
 
-    whole = pl.BlockSpec(own.shape, lambda t: (0, 0, 0))
+    whole = [pl.BlockSpec(p.shape, lambda t: (0, 0, 0)) for p in parts]
     out_specs = [pl.BlockSpec((units,) + unit, place(n)) for n in range(count)]
     out_shape = [jax.ShapeDtypeStruct((steps * units,) + unit, jnp.bfloat16) for _ in range(count)]
     if first:
         kept = pl.BlockSpec(makers[0].shape, lambda t: (0, 0, 0))
         turn = pl.BlockSpec((low,) + makers[2].shape[1:], lambda t: (t, 0, 0))
-        in_specs, operands = [whole, whole, kept, kept, turn, turn], (own, oth, *makers)
+        in_specs, operands = whole + [kept, kept, turn, turn], (*parts, *makers)
         out_specs, out_shape = out_specs + [spec], out_shape + [tables]
     else:
-        in_specs, operands = [whole, whole, spec], (own, oth, tables)
+        in_specs, operands = whole + [spec], (*parts, tables)
     return pl.pallas_call(
-        functools.partial(fine_kernel, steps, first),
+        functools.partial(fine_kernel, steps, first, len(parts)),
         grid=(grid,),
         in_specs=in_specs,
         out_specs=out_specs,
@@ -360,8 +360,8 @@
         scratch_shapes=[pltpu.VMEM((units * sig * (two_c + 8), LANES), jnp.float32)],
         compiler_params=pltpu.CompilerParams(vmem_limit_bytes=VMEM),
         cost_estimate=pl.CostEstimate(
-            flops=2 * sig * two_c * 2 * frames * high * low * 2 * LANES,
-            bytes_accessed=6 * sig * two_c * frames + 8 * high * low * frames * LANES,
+            flops=2 * sig * two_c * frames * high * low * 2 * LANES,
+            bytes_accessed=3 * sig * two_c * frames + 4 * high * low * frames * LANES,
             transcendentals=0,
         ),
     )(*operands)
@@ -459,7 +459,7 @@
     return [eighth, 2 * eighth, 2 * eighth, 2 * eighth, eighth]
 
 
-DIRECT = 2
+DIRECT = 3
 
 
 def per_device(samples, coarse_taps, fine_taps):
@@ -478,10 +478,16 @@
     low = 4
     high = dests // low
 
+    dft = coarse_rows(frame_len, channels, chunks)
+    side = win[None].astype(jnp.int32)
+    blocks = frames // BLOCK
+    half = blocks // 2
+    later = coarse(side, samples, (), coarse_taps, dft, chunks, half, blocks - half)
     hist = from_behind(samples[:, samp - (taps_n - 1) * frame_len :], "win", 1)
-    dft = coarse_rows(frame_len, channels, chunks)
-    parts = coarse(samples, hist, coarse_taps, dft, chunks)
-    own, away = parts[: len(chunks)], parts[len(chunks) :]
+    early = coarse(side, samples, (hist,), coarse_taps, dft, chunks, 0, half)
+    count = len(chunks)
+    own = [(early[k], later[k]) for k in range(count)]
+    away = [(early[count + k], later[count + k]) for k in range(count)]
 
     lane = jnp.arange(LANES, dtype=jnp.int32)
     frame_of = lane % total
@@ -502,14 +508,14 @@
 
     shape = (channels, per_dest, 2, sig * dests, sig * dests)
     highs = range(high)
-    oths = [swap(away[k], "win", 1) for k in range(len(chunks))]
+    oths = [[swap(part, "win", 1) for part in away[k]] for k in range(count)]
 
     pieces = []
     for k in range(len(chunks)):
         if k == 0:
-            *sent, tables = fine(own[k], oths[k], None, False, makers)
+            *sent, tables = fine((*own[k], *oths[k]), None, False, makers)
         else:
-            sent = fine(own[k], oths[k], tables, k >= DIRECT)
+            sent = fine((*own[k], *oths[k]), tables, k >= DIRECT)
         if k < DIRECT:
             held = [sent[0]] + [swap(sent[n], "sta", low * n) for n in highs if n]
             block = pack([(h, (2 + c,)) for c in range(2) for h in held])
@@ -557,7 +563,7 @@
         and sig == ROWS
         and taps_n == ROWS
         and frame_len % WIDE == 0
-        and frames % BLOCK == 0
+        and frames % (2 * BLOCK) == 0
         and frames % fine_len == 0
         and fine_len % stas == 0
         and fine_len // stas * (2 * frames // fine_len) == LANES

time: 419 us -> 413 us (0.986)
  waiting for transfers between devices: 132 us -> 146 us
  starting transfers between devices: 70 us -> 59.9 us
  Pallas kernels: 195 us -> 187 us
    ppermute x30 -> x35, waiting for transfers between devices: 132 us -> 146 us  [swap(): lax.ppermute(x, axis, [(i, i ^ by) for i in range(lax.axis_size(axis))])]
    ppermute x30 -> x35, starting transfers between devices: 65.1 us -> 54.3 us  [swap(): lax.ppermute(x, axis, [(i, i ^ by) for i in range(lax.axis_size(axis))])]
    pallas_call x1 -> x2, Pallas kernels: 56.8 us -> 52.4 us  [coarse(): pl.pallas_call(functools.partial(coarse_kernel, chunks, taps_n), grid=(bl...]
    pallas_call x16 -> x14, Pallas kernels: 29.1 us -> 25.9 us  [pack(): pl.pallas_call(pack_kernel, grid=(2,), in_specs=[pl.BlockSpec((1,) * len(...]
  transfers between devices with their start and end apart: 31 -> 36, of which waited for: 9 -> 9; matrix products, arithmetic and copies ran while one was open for 3% -> 2% of each run, Pallas kernels for 32% -> 44%
where the time goes in v2:
time: 413 us; the launch traced here: 406 us
  Pallas kernels  187 us (45%)
  waiting for transfers between devices  146 us (35%)
  starting transfers between devices  59.9 us (15%)
  local copies, waits for them, and re-layouts  6.12 us (1%)
  other arithmetic  5.83 us (1%)
    ppermute x35, waiting for transfers between devices, swap(): lax.ppermute(x, axis, [(i, i ^ by) for i in range(lax.axis_size(axis))])  146 us
    pallas_call x5, Pallas kernels, fine(): pl.pallas_call(functools.partial(fine_kernel, steps, first, len(parts)),...  60.9 us
    ppermute x35, starting transfers between devices, swap(): lax.ppermute(x, axis, [(i, i ^ by) for i in range(lax.axis_size(axis))])  54.3 us
    pallas_call x2, Pallas kernels, coarse(): pl.pallas_call(functools.partial(coarse_kernel, chunks, taps_n), grid=(bl...  52.4 us
    pallas_call x5, Pallas kernels, correlate_chunk(): pl.pallas_call(functools.partial(correlate_kernel, sources, scale, per_q)...  48 us
    pallas_call x14, Pallas kernels, pack(): pl.pallas_call(pack_kernel, grid=(2,), in_specs=[pl.BlockSpec((1,) * len(...  25.9 us
  transfers between devices with their start and end apart: 36, of which 9 were waited for; matrix products, arithmetic and copies ran while one was open for 2% of the time, Pallas kernels for 44%

profile of v2, /device:TPU:0, one launch (start us, length us, event | category | flops | bytes accessed | tf_op | source)
XLA Modules:
  0.0 405.7 jit_solution(8722742012802350641)
XLA Ops:
  0.0 1.0 slice.35
  1.0 5.6 %collective-permute-start = (bf16[16,7680]{1,0:T(8,128)(2,1)S(1)}, bf16[16,7680]{1,0:T(8,128)(2,1)}, u32[]{:S(2)}, u32[]{:S(2)}) collective-permute-start(bf16[16,7680]{1,0:T(8,128)(2,1)S(1)} %slice.35), channel_id=1, source_target_pairs={{0,16},{1,17},{2,18},{3,19},{4,20},{5,21},{6,22},{7,23},{8,24},{9,... | collective-permute-start | bytes 737288 | tf_op jit(solution)/shard_map/ppermute | solution.py:25
  7.3 0.7 broadcast_in_dim.227.taps_ref
  8.0 26.1 %shard_map.47 = (bf16[16,16,512]{2,1,0:T(8,128)(2,1)}, bf16[16,32,512]{2,1,0:T(8,128)(2,1)}, bf16[16,32,512]{2,1,0:T(8,128)(2,1)}, bf16[16,32,512]{2,1,0:T(8,128...) custom-call(s32[1]{0:T(128)} %bitcast.1.win_ref, ...), custom_call_target="tpu_custom_call" | custom-call | flops 19327352832 | bytes 16777216 | tf_op jit(solution)/shard_map/pallas_call | solution.py:247
  34.2 2.0 collective-permute-start.11
  36.5 2.9 fusion.6
  39.4 26.3 %shard_map.46 = (bf16[16,16,512]{2,1,0:T(8,128)(2,1)}, bf16[16,32,512]{2,1,0:T(8,128)(2,1)}, bf16[16,32,512]{2,1,0:T(8,128)(2,1)}, bf16[16,32,512]{2,1,0:T(8,128...) custom-call(s32[1]{0:T(128)} %bitcast.1.win_ref, ...), custom_call_target="tpu_custom_call" | custom-call | flops 19327352832 | bytes 16777216 | tf_op jit(solution)/shard_map/pallas_call | solution.py:247
  65.8 2.0 collective-permute-start.3
  67.8 1.3 select_add_fusion.refs_5_
  69.2 1.4 select_add_fusion.1.refs_4_
  70.6 1.9 collective-permute-start.18
  72.5 2.8 collective-permute-done.3.refs_2_
  75.3 1.9 collective-permute-start.10
  77.3 10.1 %shard_map.48 = (bf16[4,8,2,16,128]{4,3,2,1,0:T(8,128)(2,1)}, bf16[4,8,2,16,128]{4,3,2,1,0:T(8,128)(2,1)}, bf16[4,8,2,16,128]{4,3,2,1,0:T(8,128)(2,1)}, bf16[4,8...) custom-call(bf16[16,16,512]{2,1,0:T(8,128)(2,1)} %get-tuple-element.46.refs_0_, ...), custom_call_target="tpu_custom_call" | custom-call | flops 4294967296 | bytes 18350080 | tf_op jit(solution)/shard_map/pallas_call | solution.py:354
  88.2 13.8 %shard_map.62 = (bf16[4,16,2,16,128]{4,3,2,1,0:T(8,128)(2,1)}, bf16[4,16,2,16,128]{4,3,2,1,0:T(8,128)(2,1)}, bf16[4,16,2,16,128]{4,3,2,1,0:T(8,128)(2,1)}, bf16[4,16,2,16,128]{4,3,2,1,0:T(8,128)(2,1)}) custom-call(bf16[16,32,512]{2,1,0:T(8,128)(2,1)} %get-tuple-element.67.refs_0_, bf16[16,32,512]{2,1,0:T(8,128)(2,1)} %get-tuple-element.68.refs_1_, ...), custom_call_target="tpu_custom_call" | custom-call | flops 8589934592 | bytes 19922944 | tf_op jit(solution)/shard_map/pallas_call | solution.py:354
  102.0 1.6 collective-permute-start.26
  103.6 14.6 %collective-permute-done.17.refs_2_ = bf16[16,32,512]{2,1,0:T(8,128)(2,1)} collective-permute-done((bf16[16,32,512]{2,1,0:T(8,128)(2,1)}, bf16[16,32,512]{2,1,0:T(8,128)(2,1)}, u32[]{:S(2)}, u32[]{:S(2)}) %collective-permute-start.17) | collective-permute-done | bytes 524320 | tf_op jit(solution)/shard_map/ppermute | solution.py:114
  118.2 13.8 %shard_map.59 = (bf16[4,16,2,16,128]{4,3,2,1,0:T(8,128)(2,1)}, bf16[4,16,2,16,128]{4,3,2,1,0:T(8,128)(2,1)}, bf16[4,16,2,16,128]{4,3,2,1,0:T(8,128)(2,1)}, bf16[4,16,2,16,128]{4,3,2,1,0:T(8,128)(2,1)}) custom-call(bf16[16,32,512]{2,1,0:T(8,128)(2,1)} %get-tuple-element.59.refs_0_, bf16[16,32,512]{2,1,0:T(8,128)(2,1)} %get-tuple-element.60.refs_1_, ...), custom_call_target="tpu_custom_call" | custom-call | flops 8589934592 | bytes 19922944 | tf_op jit(solution)/shard_map/pallas_call | solution.py:354
  132.1 1.7 collective-permute-start.19
  133.7 2.6 collective-permute-start.20
  136.5 1.7 collective-permute-start.27
  138.2 2.1 collective-permute-start.28
  140.3 13.5 %shard_map.54 = (bf16[8,16,2,16,128]{4,3,2,1,0:T(8,128)(2,1)}, bf16[8,16,2,16,128]{4,3,2,1,0:T(8,128)(2,1)}) custom-call(bf16[16,32,512]{2,1,0:T(8,128)(2,1)} %get-tuple-element.53.refs_0_, bf16[16,32,512]{2,1,0:T(8,128)(2,1)} %get-tuple-element.54.refs_1_, bf16[16,32,512]{2,1,0:T(8,128)(2,1)} %collective-permute-done.10.refs_2_, ...), custom_call_target="tpu_custom_call" | custom-call | flops 8589934592 | bytes 19922944 | tf_op jit(solution)/shard_map/pallas_call | solution.py:354
  153.8 63.4 %collective-permute-done.27.refs_2_.refs_6_ = bf16[4,16,2,16,128]{4,3,2,1,0:T(8,128)(2,1)} collective-permute-done((bf16[4,16,2,16,128]{4,3,2,1,0:T(8,128)(2,1)}, bf16[4,16,2,16,128]{4,3,2,1,0:T(8,128)(2,1)}, u32[]{:S(2)}, u32[]{:S(2)}) %collective-permute-start.27) | collective-permute-done | bytes 524320 | tf_op jit(solution)/shard_map/ppermute | solution.py:114
  217.2 2.1 shard_map.63
  219.3 1.4 collective-permute-start.29
  220.7 1.7 collective-permute-start.2
  222.8 8.6 %collective-permute-start.31 = (bf16[4,8,2,16,128]{4,3,2,1,0:T(8,128)(2,1)}, bf16[4,8,2,16,128]{4,3,2,1,0:T(8,128)(2,1)S(1)}, u32[]{:S(2)}, u32[]{:S(2)}) collective-permute-start(bf16[4,8,2,16,128]{4,3,2,1,0:T(8,128)(2,1)} %get-tuple-element.76), channel_id=1, source_target_pairs={{0,4},{1,5},{2,6},{3,7},{4,0},{5,1},{6,2},{7,3},{8,12},{9,13},{10,... | collective-permute-start | bytes 786440 | tf_op jit(solution)/shard_map/ppermute | solution.py:114
  231.4 2.1 shard_map.60
  233.5 0.8 collective-permute-start.22
  235.7 6.3 %collective-permute-start.32 = (bf16[4,8,2,16,128]{4,3,2,1,0:T(8,128)(2,1)}, bf16[4,8,2,16,128]{4,3,2,1,0:T(8,128)(2,1)S(1)}, u32[]{:S(2)}, u32[]{:S(2)}) collective-permute-start(bf16[4,8,2,16,128]{4,3,2,1,0:T(8,128)(2,1)} %get-tuple-element.77), channel_id=1, source_target_pairs={{0,8},{1,9},{2,10},{3,11},{4,12},{5,13},{6,14},{7,15},{8,0},{9,1},... | collective-permute-start | bytes 786440 | tf_op jit(solution)/shard_map/ppermute | solution.py:114
  242.1 1.1 collective-permute-start.33
  243.2 9.6 %shard_map.49 = (bf16[8,8,2,16,128]{4,3,2,1,0:T(8,128)(2,1)}, bf16[8,8,2,16,128]{4,3,2,1,0:T(8,128)(2,1)}) custom-call(bf16[16,16,512]{2,1,0:T(8,128)(2,1)} %get-tuple-element.42.refs_0_, bf16[16,16,512]{2,1,0:T(8,128)(2,1)} %get-tuple-element.43.refs_1_, bf16[16,16,512]{2,1,0:T(8,128)(2,1)} %copy-done.8, bf16[16,16,512]{2,1,0:T(8,128)(2,1)} %copy-done.7, ...), custom_call_target="tpu_custom_call" | custom-call | flops 4294967296 | bytes 18350080 | tf_op jit(solution)/shard_map/pallas_call | solution.py:354
  252.8 4.0 collective-permute-done.32.refs_2_.refs_6_
  257.6 1.8 shard_map.65
  259.4 1.0 collective-permute-start.34
  260.3 2.1 shard_map.55
  262.4 1.1 collective-permute-start.13
  263.5 2.1 shard_map.64
  265.6 0.8 copy-done
  266.4 1.7 shard_map.50
  268.1 1.0 collective-permute-start.6
  269.1 10.2 %collective-permute-done.34.refs_4_.refs_5_.refs_6_.refs_7_ = bf16[8,8,2,16,128]{4,3,2,1,0:T(8,128)(2,1)} collective-permute-done((bf16[8,8,2,16,128]{4,3,2,1,0:T(8,128)(2,1)}, bf16[8,8,2,16,128]{4,3,2,1,0:T(8,128)(2,1)}, u32[]{:S(2)}, u32[]{:S(2)}) %collective-permute-start.34) | collective-permute-done | bytes 524320 | tf_op jit(solution)/shard_map/ppermute | solution.py:114
  279.3 1.8 shard_map.66
  281.1 2.2 shard_map.61
  283.8 28.7 %collective-permute-done.6.refs_2_.refs_3_ = bf16[8,8,2,16,128]{4,3,2,1,0:T(8,128)(2,1)S(1)} collective-permute-done((bf16[8,8,2,16,128]{4,3,2,1,0:T(8,128)(2,1)}, bf16[8,8,2,16,128]{4,3,2,1,0:T(8,128)(2,1)S(1)}, u32[]{:S(2)}, u32[]{:S(2)}) %collective-permute-start.6) | collective-permute-done | bytes 524320 | tf_op jit(solution)/shard_map/ppermute | solution.py:114
  312.5 0.8 copy-done.1
  313.3 1.5 shard_map.51
  314.8 5.4 %collective-permute-start.7 = (bf16[4,8,2,16,128]{4,3,2,1,0:T(8,128)(2,1)}, bf16[4,8,2,16,128]{4,3,2,1,0:T(8,128)(2,1)S(1)}, u32[]{:S(2)}, u32[]{:S(2)}) collective-permute-start(bf16[4,8,2,16,128]{4,3,2,1,0:T(8,128)(2,1)} %shard_map.51), channel_id=1, source_target_pairs={{0,4},{1,5},{2,6},{3,7},{4,0},{5,1},{6,2},{7,3},{8,12},{9,13},{10,... | collective-permute-start | bytes 786440 | tf_op jit(solution)/shard_map/ppermute | solution.py:114
  320.2 1.5 shard_map.53
  321.7 1.6 shard_map.52
  323.3 7.2 %shard_map.67.refs_6_ = bf16[64,4,2,256,256]{4,3,2,1,0:T(8,128)(2,1)} custom-call(s32[1]{0:T(128)} %bitcast.me_ref, bf16[4,8,2,16,128]{4,3,2,1,0:T(8,128)(2,1)} %get-tuple-element.75.refs_0_.refs_4_, bf16[4,8,2,16,128]{4,3,2,1,0:T(8,128)(2,1)} %copy-done.3, bf16[4,8,2,16,128]{4,3,2,1,0:T(8,128)(2,1)} %copy-done.4, ...), custom_call_target="tpu_custom_call" | custom-call | flops 2147483648 | bytes 8388608 | tf_op jit(solution)/shard_map/pallas_call | solution.py:440
  330.4 1.8 shard_map.56
  332.3 1.8 shard_map.57
  334.1 3.0 collective-permute-start.15
  337.1 1.8 shard_map.58
  338.9 1.4 collective-permute-start.16
  340.2 11.3 %shard_map.68.refs_6_ = bf16[64,4,2,256,256]{4,3,2,1,0:T(8,128)(2,1)} custom-call(s32[1]{0:T(128)} %bitcast.me_ref, bf16[4,16,2,16,128]{4,3,2,1,0:T(8,128)(2,1)} %get-tuple-element.71.refs_0_.refs_4_, bf16[4,16,2,16,128]{4,3,2,1,0:T(8,128)(2,1)} %copy-done.2, ...), custom_call_target="tpu_custom_call", output_to_operand_aliasing={{}: (7, {})} | custom-call | flops 4294967296 | bytes 16777216 | tf_op jit(solution)/shard_map/pallas_call | solution.py:440
  351.7 11.2 %shard_map.69.refs_6_ = bf16[64,4,2,256,256]{4,3,2,1,0:T(8,128)(2,1)} custom-call(s32[1]{0:T(128)} %bitcast.me_ref, bf16[4,16,2,16,128]{4,3,2,1,0:T(8,128)(2,1)} %get-tuple-element.63.refs_0_.refs_4_, bf16[4,16,2,16,128]{4,3,2,1,0:T(8,128)(2,1)} %collective-permute-done.19.refs_1_.refs_5_, ...), custom_call_target="tpu_custom_call", output_to_operand_aliasing={{}: (7, {})} | custom-call | flops 4294967296 | bytes 16777216 | tf_op jit(solution)/shard_map/pallas_call | solution.py:440
  362.9 2.5 collective-permute-start.9
  365.4 18.2 %collective-permute-done.15.refs_4_ = bf16[4,16,2,16,128]{4,3,2,1,0:T(8,128)(2,1)} collective-permute-done((bf16[4,16,2,16,128]{4,3,2,1,0:T(8,128)(2,1)}, bf16[4,16,2,16,128]{4,3,2,1,0:T(8,128)(2,1)}, u32[]{:S(2)}, u32[]{:S(2)}) %collective-permute-start.15) | collective-permute-done | bytes 524320 | tf_op jit(solution)/shard_map/ppermute | solution.py:114
  383.6 11.2 %shard_map.70.refs_6_ = bf16[64,4,2,256,256]{4,3,2,1,0:T(8,128)(2,1)} custom-call(s32[1]{0:T(128)} %bitcast.me_ref, bf16[8,16,2,16,128]{4,3,2,1,0:T(8,128)(2,1)} %get-tuple-element.57.refs_0_.refs_2_.refs_4_.refs_6_, bf16[8,16,2,16,128]{4,3,2,1,0:T(8,128)(2,1)} %collective-permute-done.12.refs_1_.refs_3_.refs_5_.refs_7_, ...), custom_call_target="tpu_custom_call", output_to_operand_aliasing={{}: (7, {})} | custom-call | flops 4294967296 | bytes 16777216 | tf_op jit(solution)/shard_map/pallas_call | solution.py:440
  394.8 3.7 collective-permute-done.8.refs_4_
  398.6 7.1 %shard_map.71 = bf16[64,4,2,256,256]{4,3,2,1,0:T(8,128)(2,1)} custom-call(s32[1]{0:T(128)} %bitcast.me_ref, bf16[8,8,2,16,128]{4,3,2,1,0:T(8,128)(2,1)} %get-tuple-element.51.refs_0_.refs_2_.refs_4_.refs_6_, bf16[8,8,2,16,128]{4,3,2,1,0:T(8,128)(2,1)} %copy-done, bf16[8,8,2,16,128]{4,3,2,1,0:T(8,128)(2,1)} %copy-done.1, ...), custom_call_target="tpu_custom_call", output_to_operand_aliasing={{}: (7, {})} | custom-call | flops 2147483648 | bytes 8388608 | tf_op jit(solution)/shard_map/pallas_call | solution.py:440
  (71 shorter events, 5.4 us)
Async XLA Ops:
  0.0 36.3 %copy-start.9 = (bf16[8,64]{1,0:T(8,128)(2,1)S(1)}, bf16[8,64]{1,0:T(8,128)(2,1)}, u32[]{:S(2)}) copy-start(bf16[8,64]{1,0:T(8,128)(2,1)} %param.6) | copy-start | bytes 3076
  1.0 38.5 %collective-permute-start = (bf16[16,7680]{1,0:T(8,128)(2,1)S(1)}, bf16[16,7680]{1,0:T(8,128)(2,1)}, u32[]{:S(2)}, u32[]{:S(2)}) collective-permute-start(bf16[16,7680]{1,0:T(8,128)(2,1)S(1)} %slice.35), channel_id=1, source_target_pairs={{0,16},{1,17},{2,18},{3,19},{4,20},{5,21},{6,22},{7,23},{8,24},{9,... | collective-permute-start | bytes 737288 | tf_op jit(solution)/shard_map/ppermute | solution.py:25
  34.1 36.5 %collective-permute-start.4 = (bf16[16,16,512]{2,1,0:T(8,128)(2,1)}, bf16[16,16,512]{2,1,0:T(8,128)(2,1)}, u32[]{:S(2)}, u32[]{:S(2)}) collective-permute-start(bf16[16,16,512]{2,1,0:T(8,128)(2,1)} %get-tuple-element.49), channel_id=1, source_target_pairs={{0,16},{16,0},{1,17},{17,1},{2,18},{18,2},{3,19},{19,3},{4,20},{20... | collective-permute-start | bytes 786440 | tf_op jit(solution)/shard_map/ppermute | solution.py:114
  34.2 102.1 %collective-permute-start.11 = (bf16[16,32,512]{2,1,0:T(8,128)(2,1)}, bf16[16,32,512]{2,1,0:T(8,128)(2,1)}, u32[]{:S(2)}, u32[]{:S(2)}) collective-permute-start(bf16[16,32,512]{2,1,0:T(8,128)(2,1)} %get-tuple-element.56), channel_id=1, source_target_pairs={{0,16},{16,0},{1,17},{17,1},{2,18},{18,2},{3,19},{19,3},{4,20},{20... | collective-permute-start | bytes 1572872 | tf_op jit(solution)/shard_map/ppermute | solution.py:114
  36.2 51.2 %collective-permute-start.25 = (bf16[16,32,512]{2,1,0:T(8,128)(2,1)}, bf16[16,32,512]{2,1,0:T(8,128)(2,1)S(1)}, u32[]{:S(2)}, u32[]{:S(2)}) collective-permute-start(bf16[16,32,512]{2,1,0:T(8,128)(2,1)} %get-tuple-element.70), channel_id=1, source_target_pairs={{0,16},{16,0},{1,17},{17,1},{2,18},{18,2},{3,19},{19,3},{4,20},{20... | collective-permute-start | bytes 1572872 | tf_op jit(solution)/shard_map/ppermute | solution.py:114
  65.8 9.6 %collective-permute-start.3 = (bf16[16,16,512]{2,1,0:T(8,128)(2,1)}, bf16[16,16,512]{2,1,0:T(8,128)(2,1)}, u32[]{:S(2)}, u32[]{:S(2)}) collective-permute-start(bf16[16,16,512]{2,1,0:T(8,128)(2,1)} %get-tuple-element.48), channel_id=1, source_target_pairs={{0,16},{16,0},{1,17},{17,1},{2,18},{18,2},{3,19},{19,3},{4,20},{20... | collective-permute-start | bytes 786440 | tf_op jit(solution)/shard_map/ppermute | solution.py:114
  69.1 18.4 %collective-permute-start.24 = (bf16[16,32,512]{2,1,0:T(8,128)(2,1)}, bf16[16,32,512]{2,1,0:T(8,128)(2,1)}, u32[]{:S(2)}, u32[]{:S(2)}) collective-permute-start(bf16[16,32,512]{2,1,0:T(8,128)(2,1)} %get-tuple-element.69), channel_id=1, source_target_pairs={{0,16},{16,0},{1,17},{17,1},{2,18},{18,2},{3,19},{19,3},{4,20},{20... | collective-permute-start | bytes 1572872 | tf_op jit(solution)/shard_map/ppermute | solution.py:114
  70.6 33.0 %collective-permute-start.18 = (bf16[16,32,512]{2,1,0:T(8,128)(2,1)}, bf16[16,32,512]{2,1,0:T(8,128)(2,1)}, u32[]{:S(2)}, u32[]{:S(2)}) collective-permute-start(bf16[16,32,512]{2,1,0:T(8,128)(2,1)} %get-tuple-element.62), channel_id=1, source_target_pairs={{0,16},{16,0},{1,17},{17,1},{2,18},{18,2},{3,19},{19,3},{4,20},{20... | collective-permute-start | bytes 1572872 | tf_op jit(solution)/shard_map/ppermute | solution.py:114
  75.3 61.1 %collective-permute-start.10 = (bf16[16,32,512]{2,1,0:T(8,128)(2,1)}, bf16[16,32,512]{2,1,0:T(8,128)(2,1)}, u32[]{:S(2)}, u32[]{:S(2)}) collective-permute-start(bf16[16,32,512]{2,1,0:T(8,128)(2,1)} %get-tuple-element.55), channel_id=1, source_target_pairs={{0,16},{16,0},{1,17},{17,1},{2,18},{18,2},{3,19},{19,3},{4,20},{20... | collective-permute-start | bytes 1572872 | tf_op jit(solution)/shard_map/ppermute | solution.py:114
  87.4 0.8 copy-start.10
  87.4 30.9 %collective-permute-start.17 = (bf16[16,32,512]{2,1,0:T(8,128)(2,1)}, bf16[16,32,512]{2,1,0:T(8,128)(2,1)}, u32[]{:S(2)}, u32[]{:S(2)}) collective-permute-start(bf16[16,32,512]{2,1,0:T(8,128)(2,1)} %get-tuple-element.61), channel_id=1, source_target_pairs={{0,16},{16,0},{1,17},{17,1},{2,18},{18,2},{3,19},{19,3},{4,20},{20... | collective-permute-start | bytes 1572872 | tf_op jit(solution)/shard_map/ppermute | solution.py:114
  102.0 36.1 %collective-permute-start.26 = (bf16[4,16,2,16,128]{4,3,2,1,0:T(8,128)(2,1)}, bf16[4,16,2,16,128]{4,3,2,1,0:T(8,128)(2,1)S(1)}, u32[]{:S(2)}, u32[]{:S(2)}) collective-permute-start(bf16[4,16,2,16,128]{4,3,2,1,0:T(8,128)(2,1)} %get-tuple-element.72), channel_id=1, source_target_pairs={{0,4},{1,5},{2,6},{3,7},{4,0},{5,1},{6,2},{7,3},{8,12},{9,13},{10,... | collective-permute-start | bytes 1572872 | tf_op jit(solution)/shard_map/ppermute | solution.py:114
  132.1 88.7 %collective-permute-start.19 = (bf16[4,16,2,16,128]{4,3,2,1,0:T(8,128)(2,1)}, bf16[4,16,2,16,128]{4,3,2,1,0:T(8,128)(2,1)}, u32[]{:S(2)}, u32[]{:S(2)}) collective-permute-start(bf16[4,16,2,16,128]{4,3,2,1,0:T(8,128)(2,1)} %get-tuple-element.64), channel_id=1, source_target_pairs={{0,4},{1,5},{2,6},{3,7},{4,0},{5,1},{6,2},{7,3},{8,12},{9,13},{10,... | collective-permute-start | bytes 1572872 | tf_op jit(solution)/shard_map/ppermute | solution.py:114
  133.7 88.7 %collective-permute-start.20 = (bf16[4,16,2,16,128]{4,3,2,1,0:T(8,128)(2,1)}, bf16[4,16,2,16,128]{4,3,2,1,0:T(8,128)(2,1)}, u32[]{:S(2)}, u32[]{:S(2)}) collective-permute-start(bf16[4,16,2,16,128]{4,3,2,1,0:T(8,128)(2,1)} %get-tuple-element.65), channel_id=1, source_target_pairs={{0,8},{1,9},{2,10},{3,11},{4,12},{5,13},{6,14},{7,15},{8,0},{9,1},... | collective-permute-start | bytes 1572872 | tf_op jit(solution)/shard_map/ppermute | solution.py:114
  136.3 86.4 %collective-permute-start.21 = (bf16[4,16,2,16,128]{4,3,2,1,0:T(8,128)(2,1)}, bf16[4,16,2,16,128]{4,3,2,1,0:T(8,128)(2,1)}, u32[]{:S(2)}, u32[]{:S(2)}) collective-permute-start(bf16[4,16,2,16,128]{4,3,2,1,0:T(8,128)(2,1)} %get-tuple-element.66), channel_id=1, source_target_pairs={{0,12},{1,13},{2,14},{3,15},{4,8},{5,9},{6,10},{7,11},{8,4},{9,5},... | collective-permute-start | bytes 1572872 | tf_op jit(solution)/shard_map/ppermute | solution.py:114
  136.5 80.7 %collective-permute-start.27 = (bf16[4,16,2,16,128]{4,3,2,1,0:T(8,128)(2,1)}, bf16[4,16,2,16,128]{4,3,2,1,0:T(8,128)(2,1)}, u32[]{:S(2)}, u32[]{:S(2)}) collective-permute-start(bf16[4,16,2,16,128]{4,3,2,1,0:T(8,128)(2,1)} %get-tuple-element.73), channel_id=1, source_target_pairs={{0,8},{1,9},{2,10},{3,11},{4,12},{5,13},{6,14},{7,15},{8,0},{9,1},... | collective-permute-start | bytes 1572872 | tf_op jit(solution)/shard_map/ppermute | solution.py:114
  138.2 79.0 %copy-start.2 = (bf16[4,16,2,16,128]{4,3,2,1,0:T(8,128)(2,1)}, bf16[4,16,2,16,128]{4,3,2,1,0:T(8,128)(2,1)S(1)}, u32[]{:S(2)}) copy-start(bf16[4,16,2,16,128]{4,3,2,1,0:T(8,128)(2,1)S(1)} %collective-permute-done.26.refs_1_.refs_5_) | copy-start | bytes 1572868
  138.2 79.0 %collective-permute-start.28 = (bf16[4,16,2,16,128]{4,3,2,1,0:T(8,128)(2,1)}, bf16[4,16,2,16,128]{4,3,2,1,0:T(8,128)(2,1)}, u32[]{:S(2)}, u32[]{:S(2)}) collective-permute-start(bf16[4,16,2,16,128]{4,3,2,1,0:T(8,128)(2,1)} %get-tuple-element.74), channel_id=1, source_target_pairs={{0,12},{1,13},{2,14},{3,15},{4,8},{5,9},{6,10},{7,11},{8,4},{9,5},... | collective-permute-start | bytes 1572872 | tf_op jit(solution)/shard_map/ppermute | solution.py:114
  217.2 43.2 %collective-permute-start.12 = (bf16[8,16,2,16,128]{4,3,2,1,0:T(8,128)(2,1)}, bf16[8,16,2,16,128]{4,3,2,1,0:T(8,128)(2,1)}, u32[]{:S(2)}, u32[]{:S(2)}) collective-permute-start(bf16[8,16,2,16,128]{4,3,2,1,0:T(8,128)(2,1)} %get-tuple-element.58), channel_id=1, source_target_pairs={{0,1},{1,0},{2,3},{3,2},{4,5},{5,4},{6,7},{7,6},{8,9},{9,8},{10,11... | collective-permute-start | bytes 3145736 | tf_op jit(solution)/shard_map/ppermute | solution.py:114
  219.3 44.2 %collective-permute-start.29 = (bf16[8,16,2,16,128]{4,3,2,1,0:T(8,128)(2,1)}, bf16[8,16,2,16,128]{4,3,2,1,0:T(8,128)(2,1)}, u32[]{:S(2)}, u32[]{:S(2)}) collective-permute-start(bf16[8,16,2,16,128]{4,3,2,1,0:T(8,128)(2,1)} %shard_map.63), channel_id=1, source_target_pairs={{0,2},{1,3},{2,0},{3,1},{4,6},{5,7},{6,4},{7,5},{8,10},{9,11},{10,... | collective-permute-start | bytes 3145736 | tf_op jit(solution)/shard_map/ppermute | solution.py:114
  220.7 12.8 %collective-permute-start.2 = (bf16[16,16,512]{2,1,0:T(8,128)(2,1)}, bf16[16,16,512]{2,1,0:T(8,128)(2,1)S(1)}, u32[]{:S(2)}, u32[]{:S(2)}) collective-permute-start(bf16[16,16,512]{2,1,0:T(8,128)(2,1)} %get-tuple-element.45), channel_id=1, source_target_pairs={{0,16},{16,0},{1,17},{17,1},{2,18},{18,2},{3,19},{19,3},{4,20},{20... | collective-permute-start | bytes 786440 | tf_op jit(solution)/shard_map/ppermute | solution.py:114
  222.4 12.6 %collective-permute-start.1 = (bf16[16,16,512]{2,1,0:T(8,128)(2,1)}, bf16[16,16,512]{2,1,0:T(8,128)(2,1)S(1)}, u32[]{:S(2)}, u32[]{:S(2)}) collective-permute-start(bf16[16,16,512]{2,1,0:T(8,128)(2,1)} %get-tuple-element.44), channel_id=1, source_target_pairs={{0,16},{16,0},{1,17},{17,1},{2,18},{18,2},{3,19},{19,3},{4,20},{20... | collective-permute-start | bytes 786440 | tf_op jit(solution)/shard_map/ppermute | solution.py:114
  222.8 19.3 %collective-permute-start.31 = (bf16[4,8,2,16,128]{4,3,2,1,0:T(8,128)(2,1)}, bf16[4,8,2,16,128]{4,3,2,1,0:T(8,128)(2,1)S(1)}, u32[]{:S(2)}, u32[]{:S(2)}) collective-permute-start(bf16[4,8,2,16,128]{4,3,2,1,0:T(8,128)(2,1)} %get-tuple-element.76), channel_id=1, source_target_pairs={{0,4},{1,5},{2,6},{3,7},{4,0},{5,1},{6,2},{7,3},{8,12},{9,13},{10,... | collective-permute-start | bytes 786440 | tf_op jit(solution)/shard_map/ppermute | solution.py:114
  233.5 9.7 %copy-start.7 = (bf16[16,16,512]{2,1,0:T(8,128)(2,1)}, bf16[16,16,512]{2,1,0:T(8,128)(2,1)S(1)}, u32[]{:S(2)}) copy-start(bf16[16,16,512]{2,1,0:T(8,128)(2,1)S(1)} %collective-permute-done.2.refs_3_) | copy-start | bytes 786436
  233.5 47.6 %collective-permute-start.22 = (bf16[8,16,2,16,128]{4,3,2,1,0:T(8,128)(2,1)}, bf16[8,16,2,16,128]{4,3,2,1,0:T(8,128)(2,1)}, u32[]{:S(2)}, u32[]{:S(2)}) collective-permute-start(bf16[8,16,2,16,128]{4,3,2,1,0:T(8,128)(2,1)} %shard_map.60), channel_id=1, source_target_pairs={{0,2},{1,3},{2,0},{3,1},{4,6},{5,7},{6,4},{7,5},{8,10},{9,11},{10,... | collective-permute-start | bytes 3145736 | tf_op jit(solution)/shard_map/ppermute | solution.py:114
  235.0 0.7 copy-start.8
  235.7 21.2 %collective-permute-start.32 = (bf16[4,8,2,16,128]{4,3,2,1,0:T(8,128)(2,1)}, bf16[4,8,2,16,128]{4,3,2,1,0:T(8,128)(2,1)S(1)}, u32[]{:S(2)}, u32[]{:S(2)}) collective-permute-start(bf16[4,8,2,16,128]{4,3,2,1,0:T(8,128)(2,1)} %get-tuple-element.77), channel_id=1, source_target_pairs={{0,8},{1,9},{2,10},{3,11},{4,12},{5,13},{6,14},{7,15},{8,0},{9,1},... | collective-permute-start | bytes 786440 | tf_op jit(solution)/shard_map/ppermute | solution.py:114
  242.1 15.5 %copy-start.3 = (bf16[4,8,2,16,128]{4,3,2,1,0:T(8,128)(2,1)}, bf16[4,8,2,16,128]{4,3,2,1,0:T(8,128)(2,1)S(1)}, u32[]{:S(2)}) copy-start(bf16[4,8,2,16,128]{4,3,2,1,0:T(8,128)(2,1)S(1)} %collective-permute-done.31.refs_1_.refs_5_) | copy-start | bytes 786436
  242.1 15.5 %collective-permute-start.33 = (bf16[4,8,2,16,128]{4,3,2,1,0:T(8,128)(2,1)}, bf16[4,8,2,16,128]{4,3,2,1,0:T(8,128)(2,1)}, u32[]{:S(2)}, u32[]{:S(2)}) collective-permute-start(bf16[4,8,2,16,128]{4,3,2,1,0:T(8,128)(2,1)} %get-tuple-element.78), channel_id=1, source_target_pairs={{0,12},{1,13},{2,14},{3,15},{4,8},{5,9},{6,10},{7,11},{8,4},{9,5},... | collective-permute-start | bytes 786440 | tf_op jit(solution)/shard_map/ppermute | solution.py:114
  256.9 0.7 copy-start.4
  257.6 8.0 %collective-permute-start.5 = (bf16[8,8,2,16,128]{4,3,2,1,0:T(8,128)(2,1)}, bf16[8,8,2,16,128]{4,3,2,1,0:T(8,128)(2,1)S(1)}, u32[]{:S(2)}, u32[]{:S(2)}) collective-permute-start(bf16[8,8,2,16,128]{4,3,2,1,0:T(8,128)(2,1)} %get-tuple-element.52), channel_id=1, source_target_pairs={{0,1},{1,0},{2,3},{3,2},{4,5},{5,4},{6,7},{7,6},{8,9},{9,8},{10,11... | collective-permute-start | bytes 1572872 | tf_op jit(solution)/shard_map/ppermute | solution.py:114
  259.4 20.0 %collective-permute-start.34 = (bf16[8,8,2,16,128]{4,3,2,1,0:T(8,128)(2,1)}, bf16[8,8,2,16,128]{4,3,2,1,0:T(8,128)(2,1)}, u32[]{:S(2)}, u32[]{:S(2)}) collective-permute-start(bf16[8,8,2,16,128]{4,3,2,1,0:T(8,128)(2,1)} %shard_map.65), channel_id=1, source_target_pairs={{0,2},{1,3},{2,0},{3,1},{4,6},{5,7},{6,4},{7,5},{8,10},{9,11},{10,... | collective-permute-start | bytes 1572872 | tf_op jit(solution)/shard_map/ppermute | solution.py:114
  262.4 68.0 %collective-permute-start.13 = (bf16[8,16,2,16,128]{4,3,2,1,0:T(8,128)(2,1)}, bf16[8,16,2,16,128]{4,3,2,1,0:T(8,128)(2,1)}, u32[]{:S(2)}, u32[]{:S(2)}) collective-permute-start(bf16[8,16,2,16,128]{4,3,2,1,0:T(8,128)(2,1)} %shard_map.55), channel_id=1, source_target_pairs={{0,2},{1,3},{2,0},{3,1},{4,6},{5,7},{6,4},{7,5},{8,10},{9,11},{10,... | collective-permute-start | bytes 3145736 | tf_op jit(solution)/shard_map/ppermute | solution.py:114
  265.6 73.3 %collective-permute-start.30 = (bf16[8,16,2,16,128]{4,3,2,1,0:T(8,128)(2,1)}, bf16[8,16,2,16,128]{4,3,2,1,0:T(8,128)(2,1)}, u32[]{:S(2)}, u32[]{:S(2)}) collective-permute-start(bf16[8,16,2,16,128]{4,3,2,1,0:T(8,128)(2,1)} %shard_map.64), channel_id=1, source_target_pairs={{0,1},{1,0},{2,3},{3,2},{4,5},{5,4},{6,7},{7,6},{8,9},{9,8},{10,11... | collective-permute-start | bytes 3145736 | tf_op jit(solution)/shard_map/ppermute | solution.py:114
  265.6 0.8 copy-start
  268.1 44.3 %collective-permute-start.6 = (bf16[8,8,2,16,128]{4,3,2,1,0:T(8,128)(2,1)}, bf16[8,8,2,16,128]{4,3,2,1,0:T(8,128)(2,1)S(1)}, u32[]{:S(2)}, u32[]{:S(2)}) collective-permute-start(bf16[8,8,2,16,128]{4,3,2,1,0:T(8,128)(2,1)} %shard_map.50), channel_id=1, source_target_pairs={{0,2},{1,3},{2,0},{3,1},{4,6},{5,7},{6,4},{7,5},{8,10},{9,11},{10,... | collective-permute-start | bytes 1572872 | tf_op jit(solution)/shard_map/ppermute | solution.py:114
  281.1 42.2 %collective-permute-start.35 = (bf16[8,8,2,16,128]{4,3,2,1,0:T(8,128)(2,1)}, bf16[8,8,2,16,128]{4,3,2,1,0:T(8,128)(2,1)}, u32[]{:S(2)}, u32[]{:S(2)}) collective-permute-start(bf16[8,8,2,16,128]{4,3,2,1,0:T(8,128)(2,1)} %shard_map.66), channel_id=1, source_target_pairs={{0,1},{1,0},{2,3},{3,2},{4,5},{5,4},{6,7},{7,6},{8,9},{9,8},{10,11... | collective-permute-start | bytes 1572872 | tf_op jit(solution)/shard_map/ppermute | solution.py:114
  283.3 68.2 %collective-permute-start.23 = (bf16[8,16,2,16,128]{4,3,2,1,0:T(8,128)(2,1)}, bf16[8,16,2,16,128]{4,3,2,1,0:T(8,128)(2,1)}, u32[]{:S(2)}, u32[]{:S(2)}) collective-permute-start(bf16[8,16,2,16,128]{4,3,2,1,0:T(8,128)(2,1)} %shard_map.61), channel_id=1, source_target_pairs={{0,1},{1,0},{2,3},{3,2},{4,5},{5,4},{6,7},{7,6},{8,9},{9,8},{10,11... | collective-permute-start | bytes 3145736 | tf_op jit(solution)/shard_map/ppermute | solution.py:114
  312.5 0.8 copy-start.1
  314.8 80.0 %collective-permute-start.7 = (bf16[4,8,2,16,128]{4,3,2,1,0:T(8,128)(2,1)}, bf16[4,8,2,16,128]{4,3,2,1,0:T(8,128)(2,1)S(1)}, u32[]{:S(2)}, u32[]{:S(2)}) collective-permute-start(bf16[4,8,2,16,128]{4,3,2,1,0:T(8,128)(2,1)} %shard_map.51), channel_id=1, source_target_pairs={{0,4},{1,5},{2,6},{3,7},{4,0},{5,1},{6,2},{7,3},{8,12},{9,13},{10,... | collective-permute-start | bytes 786440 | tf_op jit(solution)/shard_map/ppermute | solution.py:114
  332.3 30.7 %collective-permute-start.14 = (bf16[4,16,2,16,128]{4,3,2,1,0:T(8,128)(2,1)}, bf16[4,16,2,16,128]{4,3,2,1,0:T(8,128)(2,1)S(1)}, u32[]{:S(2)}, u32[]{:S(2)}) collective-permute-start(bf16[4,16,2,16,128]{4,3,2,1,0:T(8,128)(2,1)} %shard_map.56), channel_id=1, source_target_pairs={{0,4},{1,5},{2,6},{3,7},{4,0},{5,1},{6,2},{7,3},{8,12},{9,13},{10,... | collective-permute-start | bytes 1572872 | tf_op jit(solution)/shard_map/ppermute | solution.py:114
  334.1 49.5 %collective-permute-start.15 = (bf16[4,16,2,16,128]{4,3,2,1,0:T(8,128)(2,1)}, bf16[4,16,2,16,128]{4,3,2,1,0:T(8,128)(2,1)}, u32[]{:S(2)}, u32[]{:S(2)}) collective-permute-start(bf16[4,16,2,16,128]{4,3,2,1,0:T(8,128)(2,1)} %shard_map.57), channel_id=1, source_target_pairs={{0,8},{1,9},{2,10},{3,11},{4,12},{5,13},{6,14},{7,15},{8,0},{9,1},... | collective-permute-start | bytes 1572872 | tf_op jit(solution)/shard_map/ppermute | solution.py:114
  338.9 44.7 %collective-permute-start.16 = (bf16[4,16,2,16,128]{4,3,2,1,0:T(8,128)(2,1)}, bf16[4,16,2,16,128]{4,3,2,1,0:T(8,128)(2,1)}, u32[]{:S(2)}, u32[]{:S(2)}) collective-permute-start(bf16[4,16,2,16,128]{4,3,2,1,0:T(8,128)(2,1)} %shard_map.58), channel_id=1, source_target_pairs={{0,12},{1,13},{2,14},{3,15},{4,8},{5,9},{6,10},{7,11},{8,4},{9,5},... | collective-permute-start | bytes 1572872 | tf_op jit(solution)/shard_map/ppermute | solution.py:114
  351.5 47.1 %collective-permute-start.8 = (bf16[4,8,2,16,128]{4,3,2,1,0:T(8,128)(2,1)}, bf16[4,8,2,16,128]{4,3,2,1,0:T(8,128)(2,1)}, u32[]{:S(2)}, u32[]{:S(2)}) collective-permute-start(bf16[4,8,2,16,128]{4,3,2,1,0:T(8,128)(2,1)} %shard_map.52), channel_id=1, source_target_pairs={{0,8},{1,9},{2,10},{3,11},{4,12},{5,13},{6,14},{7,15},{8,0},{9,1},... | collective-permute-start | bytes 786440 | tf_op jit(solution)/shard_map/ppermute | solution.py:114
  362.9 20.7 %copy-start.5 = (bf16[4,16,2,16,128]{4,3,2,1,0:T(8,128)(2,1)}, bf16[4,16,2,16,128]{4,3,2,1,0:T(8,128)(2,1)S(1)}, u32[]{:S(2)}) copy-start(bf16[4,16,2,16,128]{4,3,2,1,0:T(8,128)(2,1)S(1)} %collective-permute-done.14.refs_3_) | copy-start | bytes 1572868
  362.9 35.7 %collective-permute-start.9 = (bf16[4,8,2,16,128]{4,3,2,1,0:T(8,128)(2,1)}, bf16[4,8,2,16,128]{4,3,2,1,0:T(8,128)(2,1)}, u32[]{:S(2)}, u32[]{:S(2)}) collective-permute-start(bf16[4,8,2,16,128]{4,3,2,1,0:T(8,128)(2,1)} %shard_map.53), channel_id=1, source_target_pairs={{0,12},{1,13},{2,14},{3,15},{4,8},{5,9},{6,10},{7,11},{8,4},{9,5},... | collective-permute-start | bytes 786440 | tf_op jit(solution)/shard_map/ppermute | solution.py:114
  394.8 3.8 copy-start.6

commit v3 on v2

--- a/solution.py
+++ b/solution.py
@@ -271,11 +271,11 @@
     )(win, samples, samples, taps, dft, *hist)
 
 
-def fill_tables(tables, town_ref, toth_ref, cos_ref, sin_ref, u):
+def fill_tables(tables, town_ref, toth_ref, cos_ref, sin_ref, u, dest):
     fine_local, fine_len, _ = town_ref.shape
     frames = fine_local * fine_len
     for side, t_ref in enumerate((town_ref, toth_ref)):
-        for part, turn in enumerate((cos_ref[u], sin_ref[u])):
+        for part, turn in enumerate((cos_ref[dest], sin_ref[dest])):
             rows = (t_ref[...] * turn).astype(jnp.bfloat16).reshape(frames, LANES)
             tables[u, side * frames : (side + 1) * frames, part * LANES : (part + 1) * LANES] = rows
 
@@ -283,24 +283,26 @@
 def fine_kernel(steps, first, count, *refs):
     parts, refs = refs[:count], refs[count:]
     if first:
-        makers, outs, table_ref, zs = refs[:4], refs[4:-2], refs[-2], refs[-1]
+        me, makers, outs, table_ref, zs = refs[0][0], refs[1:5], refs[5:-2], refs[-2], refs[-1]
     else:
         table_ref, outs, zs = refs[0], refs[1:-1], refs[-1]
-    sig, two_c, frames = parts[0].shape
+    sig, two_c, _ = parts[0].shape
+    spans = [part.shape[2] for part in parts]
+    frames = sum(spans)
     size = two_c // 2
     pitch = two_c + 1
     step = pl.program_id(0)
     units = table_ref.shape[0] * table_ref.shape[1]
     span = sig * (two_c + 8)
-    tables = table_ref.reshape(units, count * frames, 2 * LANES)
+    tables = table_ref.reshape(units, frames, 2 * LANES)
     for u in range(units):
         if first:
-            fill_tables(tables, *makers, u)
+            fill_tables(tables, *makers, u, me ^ (step * units + u))
         acc = None
         for n, part in enumerate(parts):
             term = jnp.dot(
-                part[...].reshape(sig * two_c, frames),
-                tables[u, n * frames : (n + 1) * frames],
+                part[...].reshape(sig * two_c, spans[n]),
+                tables[u, sum(spans[:n]) : sum(spans[: n + 1])],
                 preferred_element_type=jnp.float32,
             )
             acc = term if acc is None else acc + term
@@ -322,11 +324,11 @@
 
 
 def fine(parts, tables, turned, makers=None):
-    sig, two_c, span = parts[0].shape
-    frames = span * len(parts)
+    sig, two_c, _ = parts[0].shape
+    frames = sum(p.shape[2] for p in parts)
     first = makers is not None
     if first:
-        dests = makers[2].shape[0]
+        dests = makers[3].shape[0]
         tables = jax.ShapeDtypeStruct((dests // 4, 4, frames, 2 * LANES), jnp.bfloat16)
     high, low = tables.shape[:2]
     unit = (two_c // 2, 2, sig, LANES)
@@ -345,9 +347,9 @@
     out_specs = [pl.BlockSpec((units,) + unit, place(n)) for n in range(count)]
     out_shape = [jax.ShapeDtypeStruct((steps * units,) + unit, jnp.bfloat16) for _ in range(count)]
     if first:
-        kept = pl.BlockSpec(makers[0].shape, lambda t: (0, 0, 0))
-        turn = pl.BlockSpec((low,) + makers[2].shape[1:], lambda t: (t, 0, 0))
-        in_specs, operands = whole + [kept, kept, turn, turn], (*parts, *makers)
+        kept = [pl.BlockSpec(m.shape, lambda t: (0, 0, 0)) for m in makers[1:]]
+        in_specs = whole + [pl.BlockSpec(memory_space=pltpu.SMEM)] + kept
+        operands = (*parts, *makers)
         out_specs, out_shape = out_specs + [spec], out_shape + [tables]
     else:
         in_specs, operands = whole + [spec], (*parts, tables)
@@ -481,10 +483,10 @@
     dft = coarse_rows(frame_len, channels, chunks)
     side = win[None].astype(jnp.int32)
     blocks = frames // BLOCK
-    half = blocks // 2
-    later = coarse(side, samples, (), coarse_taps, dft, chunks, half, blocks - half)
+    opening = blocks // 2
+    later = coarse(side, samples, (), coarse_taps, dft, chunks, opening, blocks - opening)
     hist = from_behind(samples[:, samp - (taps_n - 1) * frame_len :], "win", 1)
-    early = coarse(side, samples, (hist,), coarse_taps, dft, chunks, 0, half)
+    early = coarse(side, samples, (hist,), coarse_taps, dft, chunks, 0, opening)
     count = len(chunks)
     own = [(early[k], later[k]) for k in range(count)]
     away = [(early[count + k], later[count + k]) for k in range(count)]
@@ -501,10 +503,12 @@
             table = table + jnp.where((late == m)[:, None, :], weights[m][None, :, None], 0.0)
         return table
 
-    fine_of = (me ^ jnp.arange(dests, dtype=jnp.int32))[:, None] * per_dest + (lane // total)[None, :]
-    turns = fine_of[:, None, :] * jnp.arange(fine_len, dtype=jnp.int32)[None, :, None]
-    angles = (turns % fine_len).astype(jnp.float32) * (2.0 * math.pi / fine_len)
-    makers = (taps_table(win), taps_table(1 - win), jnp.cos(angles), jnp.sin(angles))
+    spot = np.arange(LANES, dtype=np.int32)
+    fine_of = np.arange(dests, dtype=np.int32)[:, None] * per_dest + (spot // total)[None, :]
+    turns = fine_of[:, None, :] * np.arange(fine_len, dtype=np.int32)[None, :, None]
+    angles = (turns % fine_len).astype(np.float32) * np.float32(2.0 * math.pi / fine_len)
+    who = me[None].astype(jnp.int32)
+    makers = (who, taps_table(win), taps_table(1 - win), np.cos(angles), np.sin(angles))
 
     shape = (channels, per_dest, 2, sig * dests, sig * dests)
     highs = range(high)
@@ -542,7 +546,6 @@
                     sources.append([((b,), low * n + b) for b in range(low)])
         pieces.append((arrays, leads, sources))
     result = None
-    who = me[None].astype(jnp.int32)
     for k in range(len(chunks)):
         result = correlate_chunk(
             who, *pieces[k], result, sum(chunks[:k]), shape, total, 1.0 / total
@@ -563,7 +566,7 @@
         and sig == ROWS
         and taps_n == ROWS
         and frame_len % WIDE == 0
-        and frames % (2 * BLOCK) == 0
+        and frames % (4 * BLOCK) == 0
         and frames % fine_len == 0
         and fine_len % stas == 0
         and fine_len // stas * (2 * frames // fine_len) == LANES

time: 413 us -> 410 us (level)
  transfers between devices with their start and end apart: 36 -> 36, of which waited for: 9 -> 9; matrix products, arithmetic and copies ran while one was open for 2% -> 1% of each run, Pallas kernels for 44% -> 45%
where the time goes in v3:
time: 410 us; the launch traced here: 402 us
  Pallas kernels  187 us (46%)
  waiting for transfers between devices  147 us (36%)
  starting transfers between devices  59.3 us (14%)
  local copies, waits for them, and re-layouts  6.04 us (1%)
    ppermute x35, waiting for transfers between devices, swap(): lax.ppermute(x, axis, [(i, i ^ by) for i in range(lax.axis_size(axis))])  147 us
    pallas_call x5, Pallas kernels, fine(): pl.pallas_call(functools.partial(fine_kernel, steps, first, len(parts)),...  61 us
    ppermute x35, starting transfers between devices, swap(): lax.ppermute(x, axis, [(i, i ^ by) for i in range(lax.axis_size(axis))])  53.8 us
    pallas_call x2, Pallas kernels, coarse(): pl.pallas_call(functools.partial(coarse_kernel, chunks, taps_n), grid=(bl...  52.4 us
    pallas_call x5, Pallas kernels, correlate_chunk(): pl.pallas_call(functools.partial(correlate_kernel, sources, scale, per_q)...  48 us
    pallas_call x14, Pallas kernels, pack(): pl.pallas_call(pack_kernel, grid=(2,), in_specs=[pl.BlockSpec((1,) * len(...  25.8 us
  transfers between devices with their start and end apart: 36, of which 9 were waited for; matrix products, arithmetic and copies ran while one was open for 1% of the time, Pallas kernels for 45%

profile of v3, /device:TPU:0, one launch (start us, length us, event | category | flops | bytes accessed | tf_op | source)
XLA Modules:
  0.0 402.4 jit_solution(4567626801863474601)
XLA Ops:
  0.0 1.0 slice.35
  1.0 5.6 %collective-permute-start = (bf16[16,7680]{1,0:T(8,128)(2,1)S(1)}, bf16[16,7680]{1,0:T(8,128)(2,1)}, u32[]{:S(2)}, u32[]{:S(2)}) collective-permute-start(bf16[16,7680]{1,0:T(8,128)(2,1)S(1)} %slice.35), channel_id=1, source_target_pairs={{0,16},{1,17},{2,18},{3,19},{4,20},{5,21},{6,22},{7,23},{8,24},{9,... | collective-permute-start | bytes 737288 | tf_op jit(solution)/shard_map/ppermute | solution.py:25
  6.6 0.7 copy.14
  7.3 0.7 broadcast_in_dim.223.taps_ref
  8.0 26.1 %shard_map.65 = (bf16[16,16,512]{2,1,0:T(8,128)(2,1)}, bf16[16,32,512]{2,1,0:T(8,128)(2,1)}, bf16[16,32,512]{2,1,0:T(8,128)(2,1)}, bf16[16,32,512]{2,1,0:T(8,128...) custom-call(s32[1]{0:T(128)} %bitcast.1.win_ref, ...), custom_call_target="tpu_custom_call" | custom-call | flops 19327352832 | bytes 16777216 | tf_op jit(solution)/shard_map/pallas_call | solution.py:247
  34.2 2.0 collective-permute-start.11
  36.4 26.3 %shard_map.64 = (bf16[16,16,512]{2,1,0:T(8,128)(2,1)}, bf16[16,32,512]{2,1,0:T(8,128)(2,1)}, bf16[16,32,512]{2,1,0:T(8,128)(2,1)}, bf16[16,32,512]{2,1,0:T(8,128...) custom-call(s32[1]{0:T(128)} %bitcast.1.win_ref, ...), custom_call_target="tpu_custom_call" | custom-call | flops 19327352832 | bytes 16777216 | tf_op jit(solution)/shard_map/pallas_call | solution.py:247
  62.7 2.0 collective-permute-start.3
  64.7 1.4 select_add_fusion.refs_6_
  66.2 1.3 select_add_fusion.1.refs_5_
  67.5 2.0 collective-permute-start.18
  69.5 2.8 collective-permute-done.3.refs_2_
  72.3 2.0 collective-permute-start.10
  74.2 10.2 %shard_map.66 = (bf16[4,8,2,16,128]{4,3,2,1,0:T(8,128)(2,1)}, bf16[4,8,2,16,128]{4,3,2,1,0:T(8,128)(2,1)}, bf16[4,8,2,16,128]{4,3,2,1,0:T(8,128)(2,1)}, bf16[4,8...) custom-call(bf16[16,16,512]{2,1,0:T(8,128)(2,1)} %get-tuple-element.46.refs_0_, ...), custom_call_target="tpu_custom_call" | custom-call | flops 4294967296 | bytes 18350080 | tf_op jit(solution)/shard_map/pallas_call | solution.py:356
  85.3 13.8 %shard_map.80 = (bf16[4,16,2,16,128]{4,3,2,1,0:T(8,128)(2,1)}, bf16[4,16,2,16,128]{4,3,2,1,0:T(8,128)(2,1)}, bf16[4,16,2,16,128]{4,3,2,1,0:T(8,128)(2,1)}, bf16[4,16,2,16,128]{4,3,2,1,0:T(8,128)(2,1)}) custom-call(bf16[16,32,512]{2,1,0:T(8,128)(2,1)} %get-tuple-element.67.refs_0_, bf16[16,32,512]{2,1,0:T(8,128)(2,1)} %get-tuple-element.68.refs_1_, ...), custom_call_target="tpu_custom_call" | custom-call | flops 8589934592 | bytes 19922944 | tf_op jit(solution)/shard_map/pallas_call | solution.py:356
  99.1 1.6 collective-permute-start.26
  100.7 14.6 %collective-permute-done.17.refs_2_ = bf16[16,32,512]{2,1,0:T(8,128)(2,1)} collective-permute-done((bf16[16,32,512]{2,1,0:T(8,128)(2,1)}, bf16[16,32,512]{2,1,0:T(8,128)(2,1)}, u32[]{:S(2)}, u32[]{:S(2)}) %collective-permute-start.17) | collective-permute-done | bytes 524320 | tf_op jit(solution)/shard_map/ppermute | solution.py:114
  115.3 13.8 %shard_map.77 = (bf16[4,16,2,16,128]{4,3,2,1,0:T(8,128)(2,1)}, bf16[4,16,2,16,128]{4,3,2,1,0:T(8,128)(2,1)}, bf16[4,16,2,16,128]{4,3,2,1,0:T(8,128)(2,1)}, bf16[4,16,2,16,128]{4,3,2,1,0:T(8,128)(2,1)}) custom-call(bf16[16,32,512]{2,1,0:T(8,128)(2,1)} %get-tuple-element.59.refs_0_, bf16[16,32,512]{2,1,0:T(8,128)(2,1)} %get-tuple-element.60.refs_1_, ...), custom_call_target="tpu_custom_call" | custom-call | flops 8589934592 | bytes 19922944 | tf_op jit(solution)/shard_map/pallas_call | solution.py:356
  129.1 1.6 collective-permute-start.19
  130.7 2.6 collective-permute-start.20
  133.5 1.6 collective-permute-start.27
  135.1 2.1 collective-permute-start.28
  137.2 13.5 %shard_map.72 = (bf16[8,16,2,16,128]{4,3,2,1,0:T(8,128)(2,1)}, bf16[8,16,2,16,128]{4,3,2,1,0:T(8,128)(2,1)}) custom-call(bf16[16,32,512]{2,1,0:T(8,128)(2,1)} %get-tuple-element.53.refs_0_, bf16[16,32,512]{2,1,0:T(8,128)(2,1)} %get-tuple-element.54.refs_1_, bf16[16,32,512]{2,1,0:T(8,128)(2,1)} %collective-permute-done.10.refs_2_, ...), custom_call_target="tpu_custom_call" | custom-call | flops 8589934592 | bytes 19922944 | tf_op jit(solution)/shard_map/pallas_call | solution.py:356
  150.7 63.4 %collective-permute-done.27.refs_2_.refs_6_ = bf16[4,16,2,16,128]{4,3,2,1,0:T(8,128)(2,1)} collective-permute-done((bf16[4,16,2,16,128]{4,3,2,1,0:T(8,128)(2,1)}, bf16[4,16,2,16,128]{4,3,2,1,0:T(8,128)(2,1)}, u32[]{:S(2)}, u32[]{:S(2)}) %collective-permute-start.27) | collective-permute-done | bytes 524320 | tf_op jit(solution)/shard_map/ppermute | solution.py:114
  214.1 2.1 shard_map.81
  216.2 1.5 collective-permute-start.29
  217.7 1.6 collective-permute-start.2
  219.7 8.7 %collective-permute-start.31 = (bf16[4,8,2,16,128]{4,3,2,1,0:T(8,128)(2,1)}, bf16[4,8,2,16,128]{4,3,2,1,0:T(8,128)(2,1)S(1)}, u32[]{:S(2)}, u32[]{:S(2)}) collective-permute-start(bf16[4,8,2,16,128]{4,3,2,1,0:T(8,128)(2,1)} %get-tuple-element.76), channel_id=1, source_target_pairs={{0,4},{1,5},{2,6},{3,7},{4,0},{5,1},{6,2},{7,3},{8,12},{9,13},{10,... | collective-permute-start | bytes 786440 | tf_op jit(solution)/shard_map/ppermute | solution.py:114
  228.5 2.1 shard_map.78
  231.2 0.8 collective-permute-done.1.refs_2_
  232.0 0.7 copy-done.8
  232.7 6.3 %collective-permute-start.32 = (bf16[4,8,2,16,128]{4,3,2,1,0:T(8,128)(2,1)}, bf16[4,8,2,16,128]{4,3,2,1,0:T(8,128)(2,1)S(1)}, u32[]{:S(2)}, u32[]{:S(2)}) collective-permute-start(bf16[4,8,2,16,128]{4,3,2,1,0:T(8,128)(2,1)} %get-tuple-element.77), channel_id=1, source_target_pairs={{0,8},{1,9},{2,10},{3,11},{4,12},{5,13},{6,14},{7,15},{8,0},{9,1},... | collective-permute-start | bytes 786440 | tf_op jit(solution)/shard_map/ppermute | solution.py:114
  239.0 1.3 collective-permute-start.33
  240.3 9.6 %shard_map.67 = (bf16[8,8,2,16,128]{4,3,2,1,0:T(8,128)(2,1)}, bf16[8,8,2,16,128]{4,3,2,1,0:T(8,128)(2,1)}) custom-call(bf16[16,16,512]{2,1,0:T(8,128)(2,1)} %get-tuple-element.42.refs_0_, bf16[16,16,512]{2,1,0:T(8,128)(2,1)} %get-tuple-element.43.refs_1_, bf16[16,16,512]{2,1,0:T(8,128)(2,1)} %copy-done.8, bf16[16,16,512]{2,1,0:T(8,128)(2,1)} %copy-done.7, ...), custom_call_target="tpu_custom_call" | custom-call | flops 4294967296 | bytes 18350080 | tf_op jit(solution)/shard_map/pallas_call | solution.py:356
  250.0 4.1 %collective-permute-done.32.refs_2_.refs_6_ = bf16[4,8,2,16,128]{4,3,2,1,0:T(8,128)(2,1)S(1)} collective-permute-done((bf16[4,8,2,16,128]{4,3,2,1,0:T(8,128)(2,1)}, bf16[4,8,2,16,128]{4,3,2,1,0:T(8,128)(2,1)S(1)}, u32[]{:S(2)}, u32[]{:S(2)}) %collective-permute-start.32) | collective-permute-done | bytes 262176 | tf_op jit(solution)/shard_map/ppermute | solution.py:114
  254.1 0.7 copy-done.4
  254.8 1.8 shard_map.83
  257.1 2.1 shard_map.73
  259.2 1.5 collective-permute-start.13
  260.7 2.1 shard_map.82
  262.8 0.8 copy-done
  263.6 1.7 shard_map.68
  265.8 10.4 %collective-permute-done.34.refs_4_.refs_5_.refs_6_.refs_7_ = bf16[8,8,2,16,128]{4,3,2,1,0:T(8,128)(2,1)} collective-permute-done((bf16[8,8,2,16,128]{4,3,2,1,0:T(8,128)(2,1)}, bf16[8,8,2,16,128]{4,3,2,1,0:T(8,128)(2,1)}, u32[]{:S(2)}, u32[]{:S(2)}) %collective-permute-start.34) | collective-permute-done | bytes 524320 | tf_op jit(solution)/shard_map/ppermute | solution.py:114
  276.3 1.7 shard_map.84
  278.0 2.2 shard_map.79
  280.6 28.7 %collective-permute-done.6.refs_2_.refs_3_ = bf16[8,8,2,16,128]{4,3,2,1,0:T(8,128)(2,1)S(1)} collective-permute-done((bf16[8,8,2,16,128]{4,3,2,1,0:T(8,128)(2,1)}, bf16[8,8,2,16,128]{4,3,2,1,0:T(8,128)(2,1)S(1)}, u32[]{:S(2)}, u32[]{:S(2)}) %collective-permute-start.6) | collective-permute-done | bytes 524320 | tf_op jit(solution)/shard_map/ppermute | solution.py:114
  309.4 0.8 copy-done.1
  310.2 1.5 shard_map.69
  311.7 5.3 %collective-permute-start.7 = (bf16[4,8,2,16,128]{4,3,2,1,0:T(8,128)(2,1)}, bf16[4,8,2,16,128]{4,3,2,1,0:T(8,128)(2,1)S(1)}, u32[]{:S(2)}, u32[]{:S(2)}) collective-permute-start(bf16[4,8,2,16,128]{4,3,2,1,0:T(8,128)(2,1)} %shard_map.69), channel_id=1, source_target_pairs={{0,4},{1,5},{2,6},{3,7},{4,0},{5,1},{6,2},{7,3},{8,12},{9,13},{10,... | collective-permute-start | bytes 786440 | tf_op jit(solution)/shard_map/ppermute | solution.py:114
  317.0 1.5 shard_map.71
  318.5 1.5 shard_map.70
  320.1 7.2 %shard_map.85.refs_6_ = bf16[64,4,2,256,256]{4,3,2,1,0:T(8,128)(2,1)} custom-call(s32[1]{0:T(128)} %bitcast.refs_4_.me_ref, bf16[4,8,2,16,128]{4,3,2,1,0:T(8,128)(2,1)} %get-tuple-element.75.refs_0_.refs_4_, bf16[4,8,2,16,128]{4,3,2,1,0:T(8,128)(2,1)} %copy-done.3, bf16[4,8,2,16,128]{4,3,2,1,0:T(8,128)(2,1)} %copy-done.4, ...), custom_call_target="tpu_custom_call" | custom-call | flops 2147483648 | bytes 8388608 | tf_op jit(solution)/shard_map/pallas_call | solution.py:442
  327.2 1.8 shard_map.74
  329.1 1.8 shard_map.75
  330.9 3.0 collective-permute-start.15
  333.8 1.8 shard_map.76
  335.6 1.4 collective-permute-start.16
  337.0 11.3 %shard_map.86.refs_6_ = bf16[64,4,2,256,256]{4,3,2,1,0:T(8,128)(2,1)} custom-call(s32[1]{0:T(128)} %bitcast.refs_4_.me_ref, bf16[4,16,2,16,128]{4,3,2,1,0:T(8,128)(2,1)} %get-tuple-element.71.refs_0_.refs_4_, bf16[4,16,2,16,128]{4,3,2,1,0:T(8,128)(2,1)} %copy-done.2, ...), custom_call_target="tpu_custom_call", output_to_operand_aliasing={{}: (7, {})} | custom-call | flops 4294967296 | bytes 16777216 | tf_op jit(solution)/shard_map/pallas_call | solution.py:442
  348.4 11.2 %shard_map.87.refs_6_ = bf16[64,4,2,256,256]{4,3,2,1,0:T(8,128)(2,1)} custom-call(s32[1]{0:T(128)} %bitcast.refs_4_.me_ref, bf16[4,16,2,16,128]{4,3,2,1,0:T(8,128)(2,1)} %get-tuple-element.63.refs_0_.refs_4_, bf16[4,16,2,16,128]{4,3,2,1,0:T(8,128)(2,1)} %collective-permute-done.19.refs_1_.refs_5_, ...), custom_call_target="tpu_custom_call", output_to_operand_aliasing={{}: (7, {})} | custom-call | flops 4294967296 | bytes 16777216 | tf_op jit(solution)/shard_map/pallas_call | solution.py:442
  359.7 2.4 collective-permute-start.9
  362.2 18.2 %collective-permute-done.15.refs_4_ = bf16[4,16,2,16,128]{4,3,2,1,0:T(8,128)(2,1)} collective-permute-done((bf16[4,16,2,16,128]{4,3,2,1,0:T(8,128)(2,1)}, bf16[4,16,2,16,128]{4,3,2,1,0:T(8,128)(2,1)}, u32[]{:S(2)}, u32[]{:S(2)}) %collective-permute-start.15) | collective-permute-done | bytes 524320 | tf_op jit(solution)/shard_map/ppermute | solution.py:114
  380.3 11.2 %shard_map.88.refs_6_ = bf16[64,4,2,256,256]{4,3,2,1,0:T(8,128)(2,1)} custom-call(s32[1]{0:T(128)} %bitcast.refs_4_.me_ref, bf16[8,16,2,16,128]{4,3,2,1,0:T(8,128)(2,1)} %get-tuple-element.57.refs_0_.refs_2_.refs_4_.refs_6_, bf16[8,16,2,16,128]{4,3,2,1,0:T(8,128)(2,1)} %collective-permute-done.12.refs_1_.refs_3_.refs_5_.refs_7_, ...), custom_call_target="tpu_custom_call", output_to_operand_aliasing={{}: (7, {})} | custom-call | flops 4294967296 | bytes 16777216 | tf_op jit(solution)/shard_map/pallas_call | solution.py:442
  391.6 3.7 collective-permute-done.8.refs_4_
  395.3 7.1 %shard_map.89 = bf16[64,4,2,256,256]{4,3,2,1,0:T(8,128)(2,1)} custom-call(s32[1]{0:T(128)} %bitcast.refs_4_.me_ref, bf16[8,8,2,16,128]{4,3,2,1,0:T(8,128)(2,1)} %get-tuple-element.51.refs_0_.refs_2_.refs_4_.refs_6_, bf16[8,8,2,16,128]{4,3,2,1,0:T(8,128)(2,1)} %copy-done, bf16[8,8,2,16,128]{4,3,2,1,0:T(8,128)(2,1)} %copy-done.1, ...), custom_call_target="tpu_custom_call", output_to_operand_aliasing={{}: (7, {})} | custom-call | flops 2147483648 | bytes 8388608 | tf_op jit(solution)/shard_map/pallas_call | solution.py:442
  (67 shorter events, 4.1 us)
Async XLA Ops:
  0.0 36.3 %copy-start.9 = (bf16[8,64]{1,0:T(8,128)(2,1)S(1)}, bf16[8,64]{1,0:T(8,128)(2,1)}, u32[]{:S(2)}) copy-start(bf16[8,64]{1,0:T(8,128)(2,1)} %param.8) | copy-start | bytes 3076
  1.0 35.5 %collective-permute-start = (bf16[16,7680]{1,0:T(8,128)(2,1)S(1)}, bf16[16,7680]{1,0:T(8,128)(2,1)}, u32[]{:S(2)}, u32[]{:S(2)}) collective-permute-start(bf16[16,7680]{1,0:T(8,128)(2,1)S(1)} %slice.35), channel_id=1, source_target_pairs={{0,16},{1,17},{2,18},{3,19},{4,20},{5,21},{6,22},{7,23},{8,24},{9,... | collective-permute-start | bytes 737288 | tf_op jit(solution)/shard_map/ppermute | solution.py:25
  34.1 33.4 %collective-permute-start.4 = (bf16[16,16,512]{2,1,0:T(8,128)(2,1)}, bf16[16,16,512]{2,1,0:T(8,128)(2,1)}, u32[]{:S(2)}, u32[]{:S(2)}) collective-permute-start(bf16[16,16,512]{2,1,0:T(8,128)(2,1)} %get-tuple-element.49), channel_id=1, source_target_pairs={{0,16},{16,0},{1,17},{17,1},{2,18},{18,2},{3,19},{19,3},{4,20},{20... | collective-permute-start | bytes 786440 | tf_op jit(solution)/shard_map/ppermute | solution.py:114
  34.2 99.1 %collective-permute-start.11 = (bf16[16,32,512]{2,1,0:T(8,128)(2,1)}, bf16[16,32,512]{2,1,0:T(8,128)(2,1)}, u32[]{:S(2)}, u32[]{:S(2)}) collective-permute-start(bf16[16,32,512]{2,1,0:T(8,128)(2,1)} %get-tuple-element.56), channel_id=1, source_target_pairs={{0,16},{16,0},{1,17},{17,1},{2,18},{18,2},{3,19},{19,3},{4,20},{20... | collective-permute-start | bytes 1572872 | tf_op jit(solution)/shard_map/ppermute | solution.py:114
  36.2 48.3 %collective-permute-start.25 = (bf16[16,32,512]{2,1,0:T(8,128)(2,1)}, bf16[16,32,512]{2,1,0:T(8,128)(2,1)S(1)}, u32[]{:S(2)}, u32[]{:S(2)}) collective-permute-start(bf16[16,32,512]{2,1,0:T(8,128)(2,1)} %get-tuple-element.70), channel_id=1, source_target_pairs={{0,16},{16,0},{1,17},{17,1},{2,18},{18,2},{3,19},{19,3},{4,20},{20... | collective-permute-start | bytes 1572872 | tf_op jit(solution)/shard_map/ppermute | solution.py:114
  62.7 9.6 %collective-permute-start.3 = (bf16[16,16,512]{2,1,0:T(8,128)(2,1)}, bf16[16,16,512]{2,1,0:T(8,128)(2,1)}, u32[]{:S(2)}, u32[]{:S(2)}) collective-permute-start(bf16[16,16,512]{2,1,0:T(8,128)(2,1)} %get-tuple-element.48), channel_id=1, source_target_pairs={{0,16},{16,0},{1,17},{17,1},{2,18},{18,2},{3,19},{19,3},{4,20},{20... | collective-permute-start | bytes 786440 | tf_op jit(solution)/shard_map/ppermute | solution.py:114
  66.1 18.5 %collective-permute-start.24 = (bf16[16,32,512]{2,1,0:T(8,128)(2,1)}, bf16[16,32,512]{2,1,0:T(8,128)(2,1)}, u32[]{:S(2)}, u32[]{:S(2)}) collective-permute-start(bf16[16,32,512]{2,1,0:T(8,128)(2,1)} %get-tuple-element.69), channel_id=1, source_target_pairs={{0,16},{16,0},{1,17},{17,1},{2,18},{18,2},{3,19},{19,3},{4,20},{20... | collective-permute-start | bytes 1572872 | tf_op jit(solution)/shard_map/ppermute | solution.py:114
  67.5 33.1 %collective-permute-start.18 = (bf16[16,32,512]{2,1,0:T(8,128)(2,1)}, bf16[16,32,512]{2,1,0:T(8,128)(2,1)}, u32[]{:S(2)}, u32[]{:S(2)}) collective-permute-start(bf16[16,32,512]{2,1,0:T(8,128)(2,1)} %get-tuple-element.62), channel_id=1, source_target_pairs={{0,16},{16,0},{1,17},{17,1},{2,18},{18,2},{3,19},{19,3},{4,20},{20... | collective-permute-start | bytes 1572872 | tf_op jit(solution)/shard_map/ppermute | solution.py:114
  72.3 61.2 %collective-permute-start.10 = (bf16[16,32,512]{2,1,0:T(8,128)(2,1)}, bf16[16,32,512]{2,1,0:T(8,128)(2,1)}, u32[]{:S(2)}, u32[]{:S(2)}) collective-permute-start(bf16[16,32,512]{2,1,0:T(8,128)(2,1)} %get-tuple-element.55), channel_id=1, source_target_pairs={{0,16},{16,0},{1,17},{17,1},{2,18},{18,2},{3,19},{19,3},{4,20},{20... | collective-permute-start | bytes 1572872 | tf_op jit(solution)/shard_map/ppermute | solution.py:114
  84.5 0.8 copy-start.10
  84.5 30.8 %collective-permute-start.17 = (bf16[16,32,512]{2,1,0:T(8,128)(2,1)}, bf16[16,32,512]{2,1,0:T(8,128)(2,1)}, u32[]{:S(2)}, u32[]{:S(2)}) collective-permute-start(bf16[16,32,512]{2,1,0:T(8,128)(2,1)} %get-tuple-element.61), channel_id=1, source_target_pairs={{0,16},{16,0},{1,17},{17,1},{2,18},{18,2},{3,19},{19,3},{4,20},{20... | collective-permute-start | bytes 1572872 | tf_op jit(solution)/shard_map/ppermute | solution.py:114
  99.1 36.1 %collective-permute-start.26 = (bf16[4,16,2,16,128]{4,3,2,1,0:T(8,128)(2,1)}, bf16[4,16,2,16,128]{4,3,2,1,0:T(8,128)(2,1)S(1)}, u32[]{:S(2)}, u32[]{:S(2)}) collective-permute-start(bf16[4,16,2,16,128]{4,3,2,1,0:T(8,128)(2,1)} %get-tuple-element.72), channel_id=1, source_target_pairs={{0,4},{1,5},{2,6},{3,7},{4,0},{5,1},{6,2},{7,3},{8,12},{9,13},{10,... | collective-permute-start | bytes 1572872 | tf_op jit(solution)/shard_map/ppermute | solution.py:114
  129.1 88.6 %collective-permute-start.19 = (bf16[4,16,2,16,128]{4,3,2,1,0:T(8,128)(2,1)}, bf16[4,16,2,16,128]{4,3,2,1,0:T(8,128)(2,1)}, u32[]{:S(2)}, u32[]{:S(2)}) collective-permute-start(bf16[4,16,2,16,128]{4,3,2,1,0:T(8,128)(2,1)} %get-tuple-element.64), channel_id=1, source_target_pairs={{0,4},{1,5},{2,6},{3,7},{4,0},{5,1},{6,2},{7,3},{8,12},{9,13},{10,... | collective-permute-start | bytes 1572872 | tf_op jit(solution)/shard_map/ppermute | solution.py:114
  130.7 88.7 %collective-permute-start.20 = (bf16[4,16,2,16,128]{4,3,2,1,0:T(8,128)(2,1)}, bf16[4,16,2,16,128]{4,3,2,1,0:T(8,128)(2,1)}, u32[]{:S(2)}, u32[]{:S(2)}) collective-permute-start(bf16[4,16,2,16,128]{4,3,2,1,0:T(8,128)(2,1)} %get-tuple-element.65), channel_id=1, source_target_pairs={{0,8},{1,9},{2,10},{3,11},{4,12},{5,13},{6,14},{7,15},{8,0},{9,1},... | collective-permute-start | bytes 1572872 | tf_op jit(solution)/shard_map/ppermute | solution.py:114
  133.3 86.5 %collective-permute-start.21 = (bf16[4,16,2,16,128]{4,3,2,1,0:T(8,128)(2,1)}, bf16[4,16,2,16,128]{4,3,2,1,0:T(8,128)(2,1)}, u32[]{:S(2)}, u32[]{:S(2)}) collective-permute-start(bf16[4,16,2,16,128]{4,3,2,1,0:T(8,128)(2,1)} %get-tuple-element.66), channel_id=1, source_target_pairs={{0,12},{1,13},{2,14},{3,15},{4,8},{5,9},{6,10},{7,11},{8,4},{9,5},... | collective-permute-start | bytes 1572872 | tf_op jit(solution)/shard_map/ppermute | solution.py:114
  133.5 80.6 %collective-permute-start.27 = (bf16[4,16,2,16,128]{4,3,2,1,0:T(8,128)(2,1)}, bf16[4,16,2,16,128]{4,3,2,1,0:T(8,128)(2,1)}, u32[]{:S(2)}, u32[]{:S(2)}) collective-permute-start(bf16[4,16,2,16,128]{4,3,2,1,0:T(8,128)(2,1)} %get-tuple-element.73), channel_id=1, source_target_pairs={{0,8},{1,9},{2,10},{3,11},{4,12},{5,13},{6,14},{7,15},{8,0},{9,1},... | collective-permute-start | bytes 1572872 | tf_op jit(solution)/shard_map/ppermute | solution.py:114
  135.1 79.0 %copy-start.2 = (bf16[4,16,2,16,128]{4,3,2,1,0:T(8,128)(2,1)}, bf16[4,16,2,16,128]{4,3,2,1,0:T(8,128)(2,1)S(1)}, u32[]{:S(2)}) copy-start(bf16[4,16,2,16,128]{4,3,2,1,0:T(8,128)(2,1)S(1)} %collective-permute-done.26.refs_1_.refs_5_) | copy-start | bytes 1572868
  135.1 79.0 %collective-permute-start.28 = (bf16[4,16,2,16,128]{4,3,2,1,0:T(8,128)(2,1)}, bf16[4,16,2,16,128]{4,3,2,1,0:T(8,128)(2,1)}, u32[]{:S(2)}, u32[]{:S(2)}) collective-permute-start(bf16[4,16,2,16,128]{4,3,2,1,0:T(8,128)(2,1)} %get-tuple-element.74), channel_id=1, source_target_pairs={{0,12},{1,13},{2,14},{3,15},{4,8},{5,9},{6,10},{7,11},{8,4},{9,5},... | collective-permute-start | bytes 1572872 | tf_op jit(solution)/shard_map/ppermute | solution.py:114
  214.1 43.0 %collective-permute-start.12 = (bf16[8,16,2,16,128]{4,3,2,1,0:T(8,128)(2,1)}, bf16[8,16,2,16,128]{4,3,2,1,0:T(8,128)(2,1)}, u32[]{:S(2)}, u32[]{:S(2)}) collective-permute-start(bf16[8,16,2,16,128]{4,3,2,1,0:T(8,128)(2,1)} %get-tuple-element.58), channel_id=1, source_target_pairs={{0,1},{1,0},{2,3},{3,2},{4,5},{5,4},{6,7},{7,6},{8,9},{9,8},{10,11... | collective-permute-start | bytes 3145736 | tf_op jit(solution)/shard_map/ppermute | solution.py:114
  216.2 44.5 %collective-permute-start.29 = (bf16[8,16,2,16,128]{4,3,2,1,0:T(8,128)(2,1)}, bf16[8,16,2,16,128]{4,3,2,1,0:T(8,128)(2,1)}, u32[]{:S(2)}, u32[]{:S(2)}) collective-permute-start(bf16[8,16,2,16,128]{4,3,2,1,0:T(8,128)(2,1)} %shard_map.81), channel_id=1, source_target_pairs={{0,2},{1,3},{2,0},{3,1},{4,6},{5,7},{6,4},{7,5},{8,10},{9,11},{10,... | collective-permute-start | bytes 3145736 | tf_op jit(solution)/shard_map/ppermute | solution.py:114
  217.7 12.9 %collective-permute-start.2 = (bf16[16,16,512]{2,1,0:T(8,128)(2,1)}, bf16[16,16,512]{2,1,0:T(8,128)(2,1)S(1)}, u32[]{:S(2)}, u32[]{:S(2)}) collective-permute-start(bf16[16,16,512]{2,1,0:T(8,128)(2,1)} %get-tuple-element.45), channel_id=1, source_target_pairs={{0,16},{16,0},{1,17},{17,1},{2,18},{18,2},{3,19},{19,3},{4,20},{20... | collective-permute-start | bytes 786440 | tf_op jit(solution)/shard_map/ppermute | solution.py:114
  219.4 12.6 %collective-permute-start.1 = (bf16[16,16,512]{2,1,0:T(8,128)(2,1)}, bf16[16,16,512]{2,1,0:T(8,128)(2,1)S(1)}, u32[]{:S(2)}, u32[]{:S(2)}) collective-permute-start(bf16[16,16,512]{2,1,0:T(8,128)(2,1)} %get-tuple-element.44), channel_id=1, source_target_pairs={{0,16},{16,0},{1,17},{17,1},{2,18},{18,2},{3,19},{19,3},{4,20},{20... | collective-permute-start | bytes 786440 | tf_op jit(solution)/shard_map/ppermute | solution.py:114
  219.7 19.2 %collective-permute-start.31 = (bf16[4,8,2,16,128]{4,3,2,1,0:T(8,128)(2,1)}, bf16[4,8,2,16,128]{4,3,2,1,0:T(8,128)(2,1)S(1)}, u32[]{:S(2)}, u32[]{:S(2)}) collective-permute-start(bf16[4,8,2,16,128]{4,3,2,1,0:T(8,128)(2,1)} %get-tuple-element.76), channel_id=1, source_target_pairs={{0,4},{1,5},{2,6},{3,7},{4,0},{5,1},{6,2},{7,3},{8,12},{9,13},{10,... | collective-permute-start | bytes 786440 | tf_op jit(solution)/shard_map/ppermute | solution.py:114
  230.6 9.7 %copy-start.7 = (bf16[16,16,512]{2,1,0:T(8,128)(2,1)}, bf16[16,16,512]{2,1,0:T(8,128)(2,1)S(1)}, u32[]{:S(2)}) copy-start(bf16[16,16,512]{2,1,0:T(8,128)(2,1)S(1)} %collective-permute-done.2.refs_3_) | copy-start | bytes 786436
  230.6 47.4 %collective-permute-start.22 = (bf16[8,16,2,16,128]{4,3,2,1,0:T(8,128)(2,1)}, bf16[8,16,2,16,128]{4,3,2,1,0:T(8,128)(2,1)}, u32[]{:S(2)}, u32[]{:S(2)}) collective-permute-start(bf16[8,16,2,16,128]{4,3,2,1,0:T(8,128)(2,1)} %shard_map.78), channel_id=1, source_target_pairs={{0,2},{1,3},{2,0},{3,1},{4,6},{5,7},{6,4},{7,5},{8,10},{9,11},{10,... | collective-permute-start | bytes 3145736 | tf_op jit(solution)/shard_map/ppermute | solution.py:114
  232.0 0.7 copy-start.8
  232.7 21.4 %collective-permute-start.32 = (bf16[4,8,2,16,128]{4,3,2,1,0:T(8,128)(2,1)}, bf16[4,8,2,16,128]{4,3,2,1,0:T(8,128)(2,1)S(1)}, u32[]{:S(2)}, u32[]{:S(2)}) collective-permute-start(bf16[4,8,2,16,128]{4,3,2,1,0:T(8,128)(2,1)} %get-tuple-element.77), channel_id=1, source_target_pairs={{0,8},{1,9},{2,10},{3,11},{4,12},{5,13},{6,14},{7,15},{8,0},{9,1},... | collective-permute-start | bytes 786440 | tf_op jit(solution)/shard_map/ppermute | solution.py:114
  239.0 15.8 %copy-start.3 = (bf16[4,8,2,16,128]{4,3,2,1,0:T(8,128)(2,1)}, bf16[4,8,2,16,128]{4,3,2,1,0:T(8,128)(2,1)S(1)}, u32[]{:S(2)}) copy-start(bf16[4,8,2,16,128]{4,3,2,1,0:T(8,128)(2,1)S(1)} %collective-permute-done.31.refs_1_.refs_5_) | copy-start | bytes 786436
  239.0 15.8 %collective-permute-start.33 = (bf16[4,8,2,16,128]{4,3,2,1,0:T(8,128)(2,1)}, bf16[4,8,2,16,128]{4,3,2,1,0:T(8,128)(2,1)}, u32[]{:S(2)}, u32[]{:S(2)}) collective-permute-start(bf16[4,8,2,16,128]{4,3,2,1,0:T(8,128)(2,1)} %get-tuple-element.78), channel_id=1, source_target_pairs={{0,12},{1,13},{2,14},{3,15},{4,8},{5,9},{6,10},{7,11},{8,4},{9,5},... | collective-permute-start | bytes 786440 | tf_op jit(solution)/shard_map/ppermute | solution.py:114
  254.1 0.7 copy-start.4
  254.8 8.0 %collective-permute-start.5 = (bf16[8,8,2,16,128]{4,3,2,1,0:T(8,128)(2,1)}, bf16[8,8,2,16,128]{4,3,2,1,0:T(8,128)(2,1)S(1)}, u32[]{:S(2)}, u32[]{:S(2)}) collective-permute-start(bf16[8,8,2,16,128]{4,3,2,1,0:T(8,128)(2,1)} %get-tuple-element.52), channel_id=1, source_target_pairs={{0,1},{1,0},{2,3},{3,2},{4,5},{5,4},{6,7},{7,6},{8,9},{9,8},{10,11... | collective-permute-start | bytes 1572872 | tf_op jit(solution)/shard_map/ppermute | solution.py:114
  256.5 19.7 %collective-permute-start.34 = (bf16[8,8,2,16,128]{4,3,2,1,0:T(8,128)(2,1)}, bf16[8,8,2,16,128]{4,3,2,1,0:T(8,128)(2,1)}, u32[]{:S(2)}, u32[]{:S(2)}) collective-permute-start(bf16[8,8,2,16,128]{4,3,2,1,0:T(8,128)(2,1)} %shard_map.83), channel_id=1, source_target_pairs={{0,2},{1,3},{2,0},{3,1},{4,6},{5,7},{6,4},{7,5},{8,10},{9,11},{10,... | collective-permute-start | bytes 1572872 | tf_op jit(solution)/shard_map/ppermute | solution.py:114
  259.2 68.1 %collective-permute-start.13 = (bf16[8,16,2,16,128]{4,3,2,1,0:T(8,128)(2,1)}, bf16[8,16,2,16,128]{4,3,2,1,0:T(8,128)(2,1)}, u32[]{:S(2)}, u32[]{:S(2)}) collective-permute-start(bf16[8,16,2,16,128]{4,3,2,1,0:T(8,128)(2,1)} %shard_map.73), channel_id=1, source_target_pairs={{0,2},{1,3},{2,0},{3,1},{4,6},{5,7},{6,4},{7,5},{8,10},{9,11},{10,... | collective-permute-start | bytes 3145736 | tf_op jit(solution)/shard_map/ppermute | solution.py:114
  262.8 72.8 %collective-permute-start.30 = (bf16[8,16,2,16,128]{4,3,2,1,0:T(8,128)(2,1)}, bf16[8,16,2,16,128]{4,3,2,1,0:T(8,128)(2,1)}, u32[]{:S(2)}, u32[]{:S(2)}) collective-permute-start(bf16[8,16,2,16,128]{4,3,2,1,0:T(8,128)(2,1)} %shard_map.82), channel_id=1, source_target_pairs={{0,1},{1,0},{2,3},{3,2},{4,5},{5,4},{6,7},{7,6},{8,9},{9,8},{10,11... | collective-permute-start | bytes 3145736 | tf_op jit(solution)/shard_map/ppermute | solution.py:114
  262.8 0.8 copy-start
  265.3 44.1 %collective-permute-start.6 = (bf16[8,8,2,16,128]{4,3,2,1,0:T(8,128)(2,1)}, bf16[8,8,2,16,128]{4,3,2,1,0:T(8,128)(2,1)S(1)}, u32[]{:S(2)}, u32[]{:S(2)}) collective-permute-start(bf16[8,8,2,16,128]{4,3,2,1,0:T(8,128)(2,1)} %shard_map.68), channel_id=1, source_target_pairs={{0,2},{1,3},{2,0},{3,1},{4,6},{5,7},{6,4},{7,5},{8,10},{9,11},{10,... | collective-permute-start | bytes 1572872 | tf_op jit(solution)/shard_map/ppermute | solution.py:114
  278.0 42.1 %collective-permute-start.35 = (bf16[8,8,2,16,128]{4,3,2,1,0:T(8,128)(2,1)}, bf16[8,8,2,16,128]{4,3,2,1,0:T(8,128)(2,1)}, u32[]{:S(2)}, u32[]{:S(2)}) collective-permute-start(bf16[8,8,2,16,128]{4,3,2,1,0:T(8,128)(2,1)} %shard_map.84), channel_id=1, source_target_pairs={{0,1},{1,0},{2,3},{3,2},{4,5},{5,4},{6,7},{7,6},{8,9},{9,8},{10,11... | collective-permute-start | bytes 1572872 | tf_op jit(solution)/shard_map/ppermute | solution.py:114
  280.2 68.1 %collective-permute-start.23 = (bf16[8,16,2,16,128]{4,3,2,1,0:T(8,128)(2,1)}, bf16[8,16,2,16,128]{4,3,2,1,0:T(8,128)(2,1)}, u32[]{:S(2)}, u32[]{:S(2)}) collective-permute-start(bf16[8,16,2,16,128]{4,3,2,1,0:T(8,128)(2,1)} %shard_map.79), channel_id=1, source_target_pairs={{0,1},{1,0},{2,3},{3,2},{4,5},{5,4},{6,7},{7,6},{8,9},{9,8},{10,11... | collective-permute-start | bytes 3145736 | tf_op jit(solution)/shard_map/ppermute | solution.py:114
  309.4 0.8 copy-start.1
  311.7 79.9 %collective-permute-start.7 = (bf16[4,8,2,16,128]{4,3,2,1,0:T(8,128)(2,1)}, bf16[4,8,2,16,128]{4,3,2,1,0:T(8,128)(2,1)S(1)}, u32[]{:S(2)}, u32[]{:S(2)}) collective-permute-start(bf16[4,8,2,16,128]{4,3,2,1,0:T(8,128)(2,1)} %shard_map.69), channel_id=1, source_target_pairs={{0,4},{1,5},{2,6},{3,7},{4,0},{5,1},{6,2},{7,3},{8,12},{9,13},{10,... | collective-permute-start | bytes 786440 | tf_op jit(solution)/shard_map/ppermute | solution.py:114
  329.1 30.6 %collective-permute-start.14 = (bf16[4,16,2,16,128]{4,3,2,1,0:T(8,128)(2,1)}, bf16[4,16,2,16,128]{4,3,2,1,0:T(8,128)(2,1)S(1)}, u32[]{:S(2)}, u32[]{:S(2)}) collective-permute-start(bf16[4,16,2,16,128]{4,3,2,1,0:T(8,128)(2,1)} %shard_map.74), channel_id=1, source_target_pairs={{0,4},{1,5},{2,6},{3,7},{4,0},{5,1},{6,2},{7,3},{8,12},{9,13},{10,... | collective-permute-start | bytes 1572872 | tf_op jit(solution)/shard_map/ppermute | solution.py:114
  330.9 49.4 %collective-permute-start.15 = (bf16[4,16,2,16,128]{4,3,2,1,0:T(8,128)(2,1)}, bf16[4,16,2,16,128]{4,3,2,1,0:T(8,128)(2,1)}, u32[]{:S(2)}, u32[]{:S(2)}) collective-permute-start(bf16[4,16,2,16,128]{4,3,2,1,0:T(8,128)(2,1)} %shard_map.75), channel_id=1, source_target_pairs={{0,8},{1,9},{2,10},{3,11},{4,12},{5,13},{6,14},{7,15},{8,0},{9,1},... | collective-permute-start | bytes 1572872 | tf_op jit(solution)/shard_map/ppermute | solution.py:114
  335.6 44.7 %collective-permute-start.16 = (bf16[4,16,2,16,128]{4,3,2,1,0:T(8,128)(2,1)}, bf16[4,16,2,16,128]{4,3,2,1,0:T(8,128)(2,1)}, u32[]{:S(2)}, u32[]{:S(2)}) collective-permute-start(bf16[4,16,2,16,128]{4,3,2,1,0:T(8,128)(2,1)} %shard_map.76), channel_id=1, source_target_pairs={{0,12},{1,13},{2,14},{3,15},{4,8},{5,9},{6,10},{7,11},{8,4},{9,5},... | collective-permute-start | bytes 1572872 | tf_op jit(solution)/shard_map/ppermute | solution.py:114
  348.3 47.0 %collective-permute-start.8 = (bf16[4,8,2,16,128]{4,3,2,1,0:T(8,128)(2,1)}, bf16[4,8,2,16,128]{4,3,2,1,0:T(8,128)(2,1)}, u32[]{:S(2)}, u32[]{:S(2)}) collective-permute-start(bf16[4,8,2,16,128]{4,3,2,1,0:T(8,128)(2,1)} %shard_map.70), channel_id=1, source_target_pairs={{0,8},{1,9},{2,10},{3,11},{4,12},{5,13},{6,14},{7,15},{8,0},{9,1},... | collective-permute-start | bytes 786440 | tf_op jit(solution)/shard_map/ppermute | solution.py:114
  359.7 20.6 %copy-start.5 = (bf16[4,16,2,16,128]{4,3,2,1,0:T(8,128)(2,1)}, bf16[4,16,2,16,128]{4,3,2,1,0:T(8,128)(2,1)S(1)}, u32[]{:S(2)}) copy-start(bf16[4,16,2,16,128]{4,3,2,1,0:T(8,128)(2,1)S(1)} %collective-permute-done.14.refs_3_) | copy-start | bytes 1572868
  359.7 35.6 %collective-permute-start.9 = (bf16[4,8,2,16,128]{4,3,2,1,0:T(8,128)(2,1)}, bf16[4,8,2,16,128]{4,3,2,1,0:T(8,128)(2,1)}, u32[]{:S(2)}, u32[]{:S(2)}) collective-permute-start(bf16[4,8,2,16,128]{4,3,2,1,0:T(8,128)(2,1)} %shard_map.71), channel_id=1, source_target_pairs={{0,12},{1,13},{2,14},{3,15},{4,8},{5,9},{6,10},{7,11},{8,4},{9,5},... | collective-permute-start | bytes 786440 | tf_op jit(solution)/shard_map/ppermute | solution.py:114
  391.6 3.8 copy-start.6
